TPU v7x, 32 devices: a whole 2x2x4 slice. The times are simulated.
32 devices in a mesh: seq: 4 (over y, x), ctx: 8 (over z, core).
Axes of the slice: x: 2, y: 2, z: 4, core: 2. Of those that a mesh axis runs over, the one named last changes fastest.
Arguments:
- hidden_in: bfloat16 [16, 1024, 768], P('seq', 'ctx'), may hold values from -6 to 6
- cotangent: bfloat16 [16, 1024, 768], P('seq', 'ctx'), may hold values from -6 to 6
- segments: int32 [16, 1024], P('seq', 'ctx'), may hold values from 0 to 3, never falling along the last dimension, each value on 1 to 512 neighbouring positions
- qkv_weight: bfloat16 [768, 2304], P('seq'), may hold values from -0.21875 to 0.21875
- query_bias: bfloat16 [768], P('seq'), may hold values from -3 to 3
- value_bias: bfloat16 [768], P('seq'), may hold values from -0.29882812 to 0.29882812
- out_weight: bfloat16 [768, 768], P('seq'), may hold values from -1.75 to 1.75
- out_bias: bfloat16 [768], P('seq'), may hold values from -2 to 2
- first_gain: bfloat16 [768], P('seq'), may hold values from 0.5 to 1.5
- first_shift: bfloat16 [768], P('seq'), may hold values from -2 to 2
- inner_weight: bfloat16 [768, 3072], P('seq'), may hold values from -0.21875 to 0.21875
- inner_bias: bfloat16 [3072], P('seq'), may hold values from -3 to 3
- outer_weight: bfloat16 [3072, 768], P('seq'), may hold values from -0.21875 to 0.21875
- outer_bias: bfloat16 [768], P('seq'), may hold values from -2 to 2
- second_gain: bfloat16 [768], P('seq'), may hold values from 0.5 to 1.5
- second_shift: bfloat16 [768], P('seq'), may hold values from -2 to 2
Outputs:
- output: bfloat16 [16, 1024, 768], P('seq', 'ctx')
- grad_input: float32 [16, 1024, 768], P('seq', 'ctx')
- grad_qkv_weight: float32 [768, 2304], P('seq')
- grad_query_bias: float32 [768], P('seq')
- grad_value_bias: float32 [768], P('seq')
- grad_out_weight: float32 [768, 768], P('seq')
- grad_out_bias: float32 [768], P('seq')
- grad_first_gain: float32 [768], P('seq')
- grad_first_shift: float32 [768], P('seq')
- grad_inner_weight: float32 [768, 3072], P('seq')
- grad_inner_bias: float32 [3072], P('seq')
- grad_outer_weight: float32 [3072, 768], P('seq')
- grad_outer_bias: float32 [768], P('seq')
- grad_second_gain: float32 [768], P('seq')
- grad_second_shift: float32 [768], P('seq')
Inputs may be any that keep to these rules, and one draw needn't show every extreme that they name: `segments`: in each sequence the document numbers never fall along the positions; a document holds 1 to 512 positions, and some document holds exactly 512; attention joins only positions of one document of one sequence.
All inputs are finite; a program needn't handle non-finite values.
Results may differ from a plain program's by a relative error of at most 0.035.
Values may be sent and summed in bfloat16 or wider, within the bound.
A program may use at most 320 MiB of HBM per device.

v0:
```python
from functools import partial

import jax
import jax.numpy as jnp
from jax import lax
from jax.sharding import PartitionSpec as P

HEADS = 12
HEAD_DIM = 64


norm_epsilon = 1e-12


def norm_forward(matrix, gain, shift):
    average = jnp.mean(matrix, axis=-1, keepdims=True)
    centred = matrix - average
    factor = lax.rsqrt(jnp.mean(centred * centred, axis=-1, keepdims=True) + norm_epsilon)
    normed = centred * factor
    return (normed * gain + shift, normed, factor)


def norm_backward(upstream, normed, factor, gain):
    scaled = upstream * gain
    return factor * (
        scaled
        - jnp.mean(scaled, axis=-1, keepdims=True)
        - normed * jnp.mean(scaled * normed, axis=-1, keepdims=True)
    )


def split_heads(matrix):
    groups, positions, widths = matrix.shape
    return jnp.moveaxis(matrix.reshape(groups, positions, HEADS, widths // HEADS), 2, 0)


def join_heads(matrix):
    return jnp.moveaxis(matrix, 0, 2).reshape(
        matrix.shape[1], matrix.shape[2], matrix.shape[0] * matrix.shape[3]
    )


def grads_block(query_one, upstream_one, lse_one, delta_one, key_one, value_one, allowed, scaling):
    scores = (
        jnp.einsum("sqd,skd->sqk", query_one, key_one, preferred_element_type=jnp.float32) * scaling
    )
    probability = jnp.exp(jnp.where(allowed, scores - lse_one[..., None], -1e30))
    grad_probs = jnp.einsum(
        "sqd,skd->sqk", upstream_one, value_one, preferred_element_type=jnp.float32
    )
    grad_scores = (probability * (grad_probs - delta_one[..., None])).astype(jnp.bfloat16)
    grad_query = (
        jnp.einsum("sqk,skd->sqd", grad_scores, key_one, preferred_element_type=jnp.float32)
        * scaling
    )
    grad_key = (
        jnp.einsum("sqk,sqd->skd", grad_scores, query_one, preferred_element_type=jnp.float32)
        * scaling
    )
    grad_value = jnp.einsum(
        "sqk,sqd->skd",
        probability.astype(jnp.bfloat16),
        upstream_one,
        preferred_element_type=jnp.float32,
    )
    return (grad_query, grad_key, grad_value)


def on_device(
    hidden_in,
    cotangent,
    segments,
    qkv_weight,
    query_bias,
    value_bias,
    out_weight,
    out_bias,
    first_gain,
    first_shift,
    inner_weight,
    inner_bias,
    outer_weight,
    outer_bias,
    second_gain,
    second_shift,
):
    groups, positions, model_width = hidden_in.shape
    row_count = groups * positions
    scaling = HEAD_DIM ** (-0.5)
    gathered = (
        lax.all_gather(qkv_weight, "seq", axis=0, tiled=True),
        lax.all_gather(query_bias, "seq", axis=0, tiled=True),
        lax.all_gather(value_bias, "seq", axis=0, tiled=True),
        lax.all_gather(out_weight, "seq", axis=0, tiled=True),
        lax.all_gather(out_bias, "seq", axis=0, tiled=True),
        lax.all_gather(first_gain, "seq", axis=0, tiled=True),
        lax.all_gather(first_shift, "seq", axis=0, tiled=True),
        lax.all_gather(inner_weight, "seq", axis=0, tiled=True),
        lax.all_gather(inner_bias, "seq", axis=0, tiled=True),
        lax.all_gather(outer_weight, "seq", axis=0, tiled=True),
        lax.all_gather(outer_bias, "seq", axis=0, tiled=True),
        lax.all_gather(second_gain, "seq", axis=0, tiled=True),
        lax.all_gather(second_shift, "seq", axis=0, tiled=True),
    )
    (
        qkv_full,
        qbias_full,
        vbias_full,
        out_full,
        obias_full,
        fgain_full,
        fshift_full,
        inner_full,
        ibias_full,
        outer_full,
        ubias_full,
        sgain_full,
        sshift_full,
    ) = gathered
    token_rows = hidden_in.reshape(row_count, model_width)
    projected = jnp.dot(token_rows, qkv_full, preferred_element_type=jnp.float32)
    queries_low = (
        (projected[:, :model_width] + qbias_full)
        .astype(jnp.bfloat16)
        .reshape(groups, positions, model_width)
    )
    keys_low = (
        projected[:, model_width : 2 * model_width]
        .astype(jnp.bfloat16)
        .reshape(groups, positions, model_width)
    )
    values_low = (
        (projected[:, 2 * model_width :] + vbias_full)
        .astype(jnp.bfloat16)
        .reshape(groups, positions, model_width)
    )
    seg_low = segments.astype(jnp.bfloat16)
    query_heads = split_heads(queries_low)
    start_state = (
        jnp.full((HEADS, groups, positions), -1e30, jnp.float32),
        jnp.zeros((HEADS, groups, positions), jnp.float32),
        jnp.zeros((HEADS, groups, positions, HEAD_DIM), jnp.float32),
    )
    key_part = lax.all_gather(keys_low, "ctx", axis=1, tiled=True)
    value_part = lax.all_gather(values_low, "ctx", axis=1, tiled=True)
    seg_part = lax.all_gather(seg_low, "ctx", axis=1, tiled=True)
    fold_allowed = seg_low[:, :, None] == seg_part[:, None, :]

    def per_head(head_item):
        query_one, key_one, value_one, old_max, old_total, old_acc = head_item
        scores = (
            jnp.einsum("sqd,skd->sqk", query_one, key_one, preferred_element_type=jnp.float32)
            * scaling
        )
        scores = jnp.where(fold_allowed, scores, -1e30)
        new_max = jnp.maximum(old_max, jnp.max(scores, axis=-1))
        retain = jnp.exp(old_max - new_max)
        weights = jnp.where(fold_allowed, jnp.exp(scores - new_max[..., None]), 0.0)
        run_total = old_total * retain + jnp.sum(weights, axis=-1)
        run_acc = old_acc * retain[..., None] + jnp.einsum(
            "sqk,skd->sqd",
            weights.astype(jnp.bfloat16),
            value_one,
            preferred_element_type=jnp.float32,
        )
        return (new_max, run_total, run_acc)

    run_max, run_total, run_acc = lax.map(
        per_head,
        (
            query_heads,
            split_heads(key_part),
            split_heads(value_part),
            start_state[0],
            start_state[1],
            start_state[2],
        ),
    )
    out_heads = run_acc / run_total[..., None]
    row_lse = run_max + jnp.log(run_total)
    context_low = join_heads(out_heads).reshape(row_count, model_width).astype(jnp.bfloat16)
    attended = jnp.dot(context_low, out_full, preferred_element_type=jnp.float32) + obias_full
    residual = token_rows.astype(jnp.float32) + attended
    first, first_normed, first_factor = norm_forward(residual, fgain_full, fshift_full)
    first_low = first.astype(jnp.bfloat16)
    inner = jnp.dot(first_low, inner_full, preferred_element_type=jnp.float32) + ibias_full
    active = jax.nn.gelu(inner, approximate=False).astype(jnp.bfloat16)
    branch = jnp.dot(active, outer_full, preferred_element_type=jnp.float32) + ubias_full
    result, second_normed, second_factor = norm_forward(first + branch, sgain_full, sshift_full)
    output = result.astype(jnp.bfloat16).reshape(groups, positions, model_width)
    qkv_back, out_back, inner_back, outer_back, fgain_back, sgain_back = (
        lax.all_gather(qkv_weight, "seq", axis=0, tiled=True),
        lax.all_gather(out_weight, "seq", axis=0, tiled=True),
        lax.all_gather(inner_weight, "seq", axis=0, tiled=True),
        lax.all_gather(outer_weight, "seq", axis=0, tiled=True),
        lax.all_gather(first_gain, "seq", axis=0, tiled=True),
        lax.all_gather(second_gain, "seq", axis=0, tiled=True),
    )
    grad_out = cotangent.reshape(row_count, model_width).astype(jnp.float32)
    grad_second_gain = jnp.sum(grad_out * second_normed, axis=0)
    grad_second_shift = jnp.sum(grad_out, axis=0)
    grad_second = norm_backward(grad_out, second_normed, second_factor, sgain_back)
    grad_branch = grad_second.astype(jnp.bfloat16)
    grad_outer_weight = jnp.einsum(
        "rf,rd->fd", active, grad_branch, preferred_element_type=jnp.float32
    )
    grad_outer_bias = jnp.sum(grad_branch.astype(jnp.float32), axis=0)
    grad_active = jnp.einsum(
        "rd,fd->rf", grad_branch, outer_back, preferred_element_type=jnp.float32
    )
    _, gelu_pull = jax.vjp(partial(jax.nn.gelu, approximate=False), inner)
    grad_inner = gelu_pull(grad_active)[0].astype(jnp.bfloat16)
    grad_inner_weight = jnp.einsum(
        "rd,rf->df", first_low, grad_inner, preferred_element_type=jnp.float32
    )
    grad_inner_bias = jnp.sum(grad_inner.astype(jnp.float32), axis=0)
    grad_first = grad_second + jnp.einsum(
        "rf,df->rd", grad_inner, inner_back, preferred_element_type=jnp.float32
    )
    grad_first_gain = jnp.sum(grad_first * first_normed, axis=0)
    grad_first_shift = jnp.sum(grad_first, axis=0)
    grad_residual = norm_backward(grad_first, first_normed, first_factor, fgain_back)
    grad_attended = grad_residual.astype(jnp.bfloat16)
    grad_out_weight = jnp.einsum(
        "rd,re->de", context_low, grad_attended, preferred_element_type=jnp.float32
    )
    grad_out_bias = jnp.sum(grad_attended.astype(jnp.float32), axis=0)
    grad_context = jnp.einsum(
        "re,de->rd", grad_attended, out_back, preferred_element_type=jnp.float32
    )
    grad_context = grad_context.astype(jnp.bfloat16).reshape(groups, positions, model_width)
    grad_heads = split_heads(grad_context)
    row_delta = jnp.sum(grad_heads.astype(jnp.float32) * out_heads, axis=-1)
    far_keys, far_values, far_segs = (
        lax.all_gather(keys_low, "ctx", axis=1, tiled=True),
        lax.all_gather(values_low, "ctx", axis=1, tiled=True),
        lax.all_gather(seg_low, "ctx", axis=1, tiled=True),
    )
    allowed = seg_low[:, :, None] == far_segs[:, None, :]

    def head_keys(head_item):
        query_one, upstream_one, lse_one, delta_one, key_one, value_one = head_item
        return grads_block(
            query_one, upstream_one, lse_one, delta_one, key_one, value_one, allowed, scaling
        )

    dq_heads, dk_heads, dv_heads = lax.map(
        head_keys,
        (
            query_heads,
            grad_heads,
            row_lse,
            row_delta,
            split_heads(far_keys),
            split_heads(far_values),
        ),
    )
    key_grad, value_grad = (
        lax.psum_scatter(
            join_heads(dk_heads).astype(jnp.bfloat16), "ctx", scatter_dimension=1, tiled=True
        ).astype(jnp.float32),
        lax.psum_scatter(
            join_heads(dv_heads).astype(jnp.bfloat16), "ctx", scatter_dimension=1, tiled=True
        ).astype(jnp.float32),
    )
    query_grad = join_heads(dq_heads)
    query_low_grad = query_grad.reshape(row_count, model_width).astype(jnp.bfloat16)
    key_low_grad = key_grad.reshape(row_count, model_width).astype(jnp.bfloat16)
    value_low_grad = value_grad.reshape(row_count, model_width).astype(jnp.bfloat16)
    grad_projected = jnp.concatenate([query_low_grad, key_low_grad, value_low_grad], axis=1)
    grad_qkv_weight = jnp.einsum(
        "rd,rf->df", token_rows, grad_projected, preferred_element_type=jnp.float32
    )
    grad_query_bias = jnp.sum(query_low_grad.astype(jnp.float32), axis=0)
    grad_value_bias = jnp.sum(value_low_grad.astype(jnp.float32), axis=0)
    grad_input = grad_residual + jnp.einsum(
        "rf,df->rd", grad_projected, qkv_back, preferred_element_type=jnp.float32
    )
    owned = (
        lax.psum_scatter(
            grad_qkv_weight.astype(jnp.bfloat16), "seq", scatter_dimension=0, tiled=True
        ).astype(jnp.float32),
        lax.psum_scatter(
            grad_query_bias.astype(jnp.bfloat16), "seq", scatter_dimension=0, tiled=True
        ).astype(jnp.float32),
        lax.psum_scatter(
            grad_value_bias.astype(jnp.bfloat16), "seq", scatter_dimension=0, tiled=True
        ).astype(jnp.float32),
        lax.psum_scatter(
            grad_out_weight.astype(jnp.bfloat16), "seq", scatter_dimension=0, tiled=True
        ).astype(jnp.float32),
        lax.psum_scatter(
            grad_out_bias.astype(jnp.bfloat16), "seq", scatter_dimension=0, tiled=True
        ).astype(jnp.float32),
        lax.psum_scatter(
            grad_first_gain.astype(jnp.bfloat16), "seq", scatter_dimension=0, tiled=True
        ).astype(jnp.float32),
        lax.psum_scatter(
            grad_first_shift.astype(jnp.bfloat16), "seq", scatter_dimension=0, tiled=True
        ).astype(jnp.float32),
        lax.psum_scatter(
            grad_inner_weight.astype(jnp.bfloat16), "seq", scatter_dimension=0, tiled=True
        ).astype(jnp.float32),
        lax.psum_scatter(
            grad_inner_bias.astype(jnp.bfloat16), "seq", scatter_dimension=0, tiled=True
        ).astype(jnp.float32),
        lax.psum_scatter(
            grad_outer_weight.astype(jnp.bfloat16), "seq", scatter_dimension=0, tiled=True
        ).astype(jnp.float32),
        lax.psum_scatter(
            grad_outer_bias.astype(jnp.bfloat16), "seq", scatter_dimension=0, tiled=True
        ).astype(jnp.float32),
        lax.psum_scatter(
            grad_second_gain.astype(jnp.bfloat16), "seq", scatter_dimension=0, tiled=True
        ).astype(jnp.float32),
        lax.psum_scatter(
            grad_second_shift.astype(jnp.bfloat16), "seq", scatter_dimension=0, tiled=True
        ).astype(jnp.float32),
    )
    summed = (
        lax.psum(owned[0].astype(jnp.bfloat16), "ctx").astype(jnp.float32),
        lax.psum(owned[1].astype(jnp.bfloat16), "ctx").astype(jnp.float32),
        lax.psum(owned[2].astype(jnp.bfloat16), "ctx").astype(jnp.float32),
        lax.psum(owned[3].astype(jnp.bfloat16), "ctx").astype(jnp.float32),
        lax.psum(owned[4].astype(jnp.bfloat16), "ctx").astype(jnp.float32),
        lax.psum(owned[5].astype(jnp.bfloat16), "ctx").astype(jnp.float32),
        lax.psum(owned[6].astype(jnp.bfloat16), "ctx").astype(jnp.float32),
        lax.psum(owned[7].astype(jnp.bfloat16), "ctx").astype(jnp.float32),
        lax.psum(owned[8].astype(jnp.bfloat16), "ctx").astype(jnp.float32),
        lax.psum(owned[9].astype(jnp.bfloat16), "ctx").astype(jnp.float32),
        lax.psum(owned[10].astype(jnp.bfloat16), "ctx").astype(jnp.float32),
        lax.psum(owned[11].astype(jnp.bfloat16), "ctx").astype(jnp.float32),
        lax.psum(owned[12].astype(jnp.bfloat16), "ctx").astype(jnp.float32),
    )
    return (
        output,
        grad_input.reshape(groups, positions, model_width),
        summed[0],
        summed[1],
        summed[2],
        summed[3],
        summed[4],
        summed[5],
        summed[6],
        summed[7],
        summed[8],
        summed[9],
        summed[10],
        summed[11],
        summed[12],
    )


def solution(mesh):
    placed = (
        P("seq", "ctx", None),
        P("seq", "ctx", None),
        P("seq", "ctx"),
        P("seq", None),
        P("seq"),
        P("seq"),
        P("seq", None),
        P("seq"),
        P("seq"),
        P("seq"),
        P("seq", None),
        P("seq"),
        P("seq", None),
        P("seq"),
        P("seq"),
        P("seq"),
    )
    return jax.shard_map(
        on_device,
        mesh=mesh,
        in_specs=placed,
        out_specs=(
            P("seq", "ctx", None),
            P("seq", "ctx", None),
            P("seq", None),
            P("seq"),
            P("seq"),
            P("seq", None),
            P("seq"),
            P("seq"),
            P("seq"),
            P("seq", None),
            P("seq"),
            P("seq", None),
            P("seq"),
            P("seq"),
            P("seq"),
        ),
        check_vma=False,
    )
```

profile of v0, /device:TPU:0, one launch (start us, length us, event | category | flops | bytes accessed | tf_op | source)
XLA Modules:
  0.0 961.5 jit_solution(5188691105644556815)
XLA Ops:
  15.8 17.8 %all-reduce.20 = (bf16[768]{0:T(1024)(128)(2,1)S(1)}, bf16[768]{0:T(1024)(128)(2,1)S(1)}, bf16[768]{0:T(1024)(128)(2,1)S(1)}, bf16[768]{0:T(1024)(128)(2,1)S(1)}...) all-reduce(bf16[768]{0:T(1024)(128)(2,1)S(1)} %dynamic-update-slice, ...), channel_id=1, replica_groups=mesh['seq'=4,'ctx'=8] {'seq'}, use_global_device_ids=true, to_apply=%add | all-reduce | flops 5376 | bytes 21504
  33.7 26.3 %all-gather.8.cloned.1.call-done = bf16[768,2304]{1,0:T(8,128)(2,1)} async-done(((bf16[192,2304]{1,0:T(8,128)(2,1)}), bf16[768,2304]{1,0:T(8,128)(2,1)}) %all-gather.8.cloned.1.call-update) | async-done | bytes 3538960 | tf_op jit(solution)/shard_map/all_gather | solution.py:91
  72.2 11.9 %all_gather.60 = bf16[4,1024]{1,0:T(4,128)(2,1)S(1)} all-gather(bf16[4,128]{1,0:T(4,128)(2,1)S(1)} %convert_element_type.236), channel_id=1, replica_groups=mesh['seq'=4,'ctx'=8] {'ctx'}, dimensions={1}, use_global_device_ids=true | all-gather | bytes 9216 | tf_op jit(solution)/shard_map/all_gather | solution.py:146
  84.1 8.4 all-gather
  96.8 36.1 %all-gather.12.cloned.1.call-done = bf16[4,1024,768]{1,2,0:T(8,128)(2,1)} async-done(((bf16[4,128,768]{1,2,0:T(8,128)(2,1)}), bf16[4,1024,768]{1,2,0:T(8,128)(2,1)}) %all-gather.12.cloned.1.call-update) | async-done | bytes 6291472 | tf_op jit(solution)/shard_map/all_gather | solution.py:145
  139.6 58.8 %all-gather.10.cloned.1.call-done = bf16[4,1024,768]{1,2,0:T(8,128)(2,1)} async-done(((bf16[4,128,768]{1,2,0:T(8,128)(2,1)}), bf16[4,1024,768]{1,2,0:T(8,128)(2,1)}) %all-gather.10.cloned.1.call-update) | async-done | bytes 6291472 | tf_op jit(solution)/shard_map/all_gather | solution.py:144
  205.1 51.8 %while.30 = (s32[]{:T(128)}, f32[12,4,128]{2,1,0:T(4,128)S(1)}, f32[12,4,128]{2,1,0:T(4,128)S(1)}, f32[12,4,128,64]{2,1,3,0:T(4,128)S(1)}, bf16[12,4,128,64]{2,3...) while((s32[]{:T(128)}, f32[12,4,128]{2,1,0:T(4,128)S(1)}, ...), condition=%wide.region_3.4_spmd.clone, body=%wide.region_0.3_spmd.clone.sunk | while | flops 142641664 | bytes 7852653 | solution.py:168
  261.0 23.9 %all-gather.16.cloned.1.call-done = bf16[768,3072]{1,0:T(8,128)(2,1)} async-done(((bf16[192,3072]{1,0:T(8,128)(2,1)}), bf16[768,3072]{1,0:T(8,128)(2,1)}) %all-gather.16.cloned.1.call-update) | async-done | bytes 4718608 | tf_op jit(solution)/shard_map/all_gather | solution.py:98
  284.9 19.8 %multiply_convert_fusion.1 = (bf16[512,3072]{1,0:T(8,128)(2,1)}, f32[512,3072]{1,0:T(8,128)}, f32[512,3072]{1,0:T(8,128)}) fusion(f32[3072]{0:T(1024)S(1)} %bitcast.237, bf16[768,3072]{1,0:T(8,128)(2,1)} %all-gather.16.cloned.1.call-done, f32[512,768]{1,0:T(8,128)S(1)} %get-tuple-element.358, f32[768]{0:T(1024)S(1)} %convert_element_type.244, ...), kind=kOutput, calls=%fused_computation.66 | convolution fusion | flops 2521694208 | bytes 22042624 | tf_op jit(solution)/shard_map/dot_general | solution.py:186
  304.7 39.0 %all-gather.18.cloned.1.call-done = bf16[3072,768]{1,0:T(8,128)(2,1)} async-done(((bf16[768,768]{1,0:T(8,128)(2,1)}), bf16[3072,768]{1,0:T(8,128)(2,1)}) %all-gather.18.cloned.1.call-update) | async-done | bytes 4718608 | tf_op jit(solution)/shard_map/all_gather | solution.py:100
  353.2 9.2 fusion.85
  375.0 103.1 %while.31 = (s32[]{:T(128)}, bf16[12,4,128,64]{2,3,1,0:T(8,128)(2,1)}, bf16[12,4,1024,64]{2,3,0,1:T(8,128)(2,1)}, bf16[12,4,1024,64]{2,3,0,1:T(8,128)(2,1)}, bf1...) while((s32[]{:T(128)}, ...), condition=%wide.region_14.15_spmd.clone, body=%wide.region_13.14_spmd.clone.sunk | while | flops 340033536 | bytes 13657221 | solution.py:247
  478.1 10.8 %copy.70 = bf16[4,1024,768]{2,0,1:T(4,128)(2,1)} copy(bf16[4,1024,768]{1,2,0:T(8,128)(2,1)} %bitcast.219) | data formatting | bytes 12582912
  495.9 11.0 %copy.72 = bf16[4,1024,768]{2,0,1:T(4,128)(2,1)} copy(bf16[4,1024,768]{1,2,0:T(8,128)(2,1)} %bitcast.220) | data formatting | bytes 12582912
  516.6 49.2 %reduce-scatter.19.cloned.1.call-done = bf16[128,3072]{1,0:T(8,128)(2,1)} async-done(((bf16[1024,3072]{1,0:T(8,128)(2,1)}), bf16[128,3072]{1,0:T(8,128)(2,1)}) %reduce-scatter.19.cloned.1.call-update) | async-done | bytes 786448
  569.1 67.2 %reduce-scatter.21.cloned.1.call-done = bf16[128,3072]{1,0:T(8,128)(2,1)} async-done(((bf16[1024,3072]{1,0:T(8,128)(2,1)}), bf16[128,3072]{1,0:T(8,128)(2,1)}) %reduce-scatter.21.cloned.1.call-update) | async-done | bytes 786448
  659.0 8.0 convolution_convert_fusion.1
  674.6 26.4 %reduce-scatter.23.cloned.1.call-done = bf16[192,2304]{1,0:T(8,128)(2,1)} async-done(((bf16[768,2304]{1,0:T(8,128)(2,1)}), bf16[192,2304]{1,0:T(8,128)(2,1)}) %reduce-scatter.23.cloned.1.call-update) | async-done | bytes 884752
  703.2 29.0 %reduce-scatter.13.cloned.1.call-done = bf16[192,768]{1,0:T(8,128)(2,1)} async-done(((bf16[768,768]{1,0:T(8,128)(2,1)}), bf16[192,768]{1,0:T(8,128)(2,1)}) %reduce-scatter.13.cloned.1.call-update) | async-done | bytes 294928 | tf_op jit(solution)/shard_map/reduce_scatter | solution.py:289
  732.2 60.1 %reduce-scatter.15.cloned.1.call-done = bf16[192,3072]{1,0:T(8,128)(2,1)} async-done(((bf16[768,3072]{1,0:T(8,128)(2,1)}), bf16[192,3072]{1,0:T(8,128)(2,1)}) %reduce-scatter.15.cloned.1.call-update) | async-done | bytes 1179664 | tf_op jit(solution)/shard_map/reduce_scatter | solution.py:301
  792.4 60.0 %reduce-scatter.17.cloned.1.call-done = bf16[768,768]{1,0:T(8,128)(2,1)} async-done(((bf16[3072,768]{1,0:T(8,128)(2,1)}), bf16[768,768]{1,0:T(8,128)(2,1)}) %reduce-scatter.17.cloned.1.call-update) | async-done | bytes 1179664 | tf_op jit(solution)/shard_map/reduce_scatter | solution.py:307
  855.9 15.5 %all-reduce.19 = (bf16[768]{0:T(1024)(128)(2,1)S(1)}, bf16[768]{0:T(1024)(128)(2,1)S(1)}, bf16[768]{0:T(1024)(128)(2,1)S(1)}, bf16[768]{0:T(1024)(128)(2,1)S(1)}...) all-reduce(bf16[768]{0:T(1024)(128)(2,1)S(1)} %dynamic-update-slice, ...), channel_id=1, replica_groups=mesh['seq'=4,'ctx'=8] {'seq'}, use_global_device_ids=true, to_apply=%add.7 | all-reduce | flops 9984 | bytes 39936
  872.0 15.0 %all-reduce.17 = (bf16[192]{0:T(256)(128)(2,1)S(1)}, bf16[192]{0:T(256)(128)(2,1)S(1)}, bf16[192]{0:T(256)(128)(2,1)S(1)}, bf16[192]{0:T(256)(128)(2,1)S(1)}, bf...) all-reduce(bf16[192]{0:T(256)(128)(2,1)S(1)} %dynamic-slice.9, ...), channel_id=1, replica_groups=mesh['seq'=4,'ctx'=8] {'ctx'}, use_global_device_ids=true, to_apply=%region_21.22 | all-reduce | flops 2304 | bytes 9216 | tf_op jit(solution)/shard_map/psum | solution.py:322
  899.3 48.1 %all-reduce.23.cloned.1.call-done = (bf16[192,2304]{0,1:T(8,128)(2,1)}, bf16[192,768]{1,0:T(8,128)(2,1)}, bf16[192,3072]{1,0:T(8,128)(2,1)}, bf16[768,768]{1,0:T(8,128)(2,1)}) async-done(((bf16[192,2304]{0,1:T(8,128)(2,1)}, bf16[192,768]{1,0:T(8,128)(2,1)}, bf16[192,3072]{1,0:T(8,128)(2,1)}, bf16[768,768]{1,0:T(8,128)(2,1)}), (bf16[192,2304]{0,1:T(8,128)(2,1)}, bf16[192,768]{1,0:T(8,128)(2,1)}, ...) | async-done | bytes 3538960 | tf_op jit(solution)/shard_map/psum | solution.py:321
  (333 shorter events, 292.6 us)
Async XLA Ops:
  7.2 52.8 %all-gather.8.cloned.1.call-start = ((), (), s32[]{:S(2)}) async-start(), calls=%async_computation.6 | async-start | bytes 4423680 | tf_op jit(solution)/shard_map/all_gather | solution.py:91
  7.9 125.0 %all-gather.12.cloned.1.call-start = ((), (), s32[]{:S(2)}) async-start(), calls=%async_computation.8 | async-start | bytes 7077888 | tf_op jit(solution)/shard_map/all_gather | solution.py:145
  67.5 130.9 %all-gather.10.cloned.1.call-start = ((), (), s32[]{:S(2)}) async-start(), calls=%async_computation.7 | async-start | bytes 7077888 | tf_op jit(solution)/shard_map/all_gather | solution.py:144
  69.1 15.0 %copy-start.13 = (bf16[768]{0:T(1024)(128)(2,1)S(1)}, bf16[768]{0:T(1024)(128)(2,1)}, u32[]{:S(2)}) copy-start(bf16[768]{0:T(1024)(128)(2,1)} %param.31) | copy-start | bytes 4612
  69.1 23.5 %copy-start = (bf16[4,128,768]{2,1,0:T(8,128)(2,1)S(1)}, bf16[4,128,768]{2,1,0:T(8,128)(2,1)}, u32[]{:S(2)}) copy-start(bf16[4,128,768]{2,1,0:T(8,128)(2,1)} %param.21) | copy-start | bytes 2359300
  70.3 187.0 %all-gather.14.cloned.1.call-start = ((), (), s32[]{:S(2)}) async-start(), calls=%async_computation.9 | async-start | bytes 1474560 | tf_op jit(solution)/shard_map/all_gather | solution.py:94
  70.9 214.0 %all-gather.16.cloned.1.call-start = ((), (), s32[]{:S(2)}) async-start(), calls=%async_computation.10 | async-start | bytes 5898240 | tf_op jit(solution)/shard_map/all_gather | solution.py:98
  71.5 272.2 %all-gather.18.cloned.1.call-start = ((), (), s32[]{:S(2)}) async-start(), calls=%async_computation.11 | async-start | bytes 5898240 | tf_op jit(solution)/shard_map/all_gather | solution.py:100
  72.0 493.7 %reduce-scatter.19.cloned.1.call-start = ((), (), s32[]{:S(2)}) async-start(), calls=%async_computation.15 | async-start | bytes 7077888
  257.2 3.4 copy-start.7
  260.7 44.0 %copy-start.3 = (f32[512,768]{1,0:T(8,128)}, f32[512,768]{1,0:T(8,128)S(1)}, u32[]{:S(2)}) copy-start(f32[512,768]{1,0:T(8,128)S(1)} %get-tuple-element.358) | copy-start | bytes 4718596
  351.1 11.3 %slice-start = ((s8[4718592]{0:T(1024)(128)(4,1)}), s8[4194304]{0:T(1024)(128)(4,1)S(1)}, s32[]{:S(2)}) async-start(s8[4718592]{0:T(1024)(128)(4,1)} %bitcast.239), calls=%async_computation.19 | async-start | bytes 8388608
  351.7 10.7 %copy-start.8 = (f32[512,768]{1,0:T(8,128)}, f32[512,768]{1,0:T(8,128)S(1)}, u32[]{:S(2)}) copy-start(f32[512,768]{1,0:T(8,128)S(1)} %get-tuple-element.340) | copy-start | bytes 4718596
  353.2 9.2 copy-start.4
  353.2 9.2 slice-start.1
  495.8 140.5 %reduce-scatter.21.cloned.1.call-start = ((), (), s32[]{:S(2)}) async-start(), calls=%async_computation.16 | async-start | bytes 7077888
  513.8 187.1 %reduce-scatter.23.cloned.1.call-start = ((), (), s32[]{:S(2)}) async-start(), calls=%async_computation.17 | async-start | bytes 4423680
  639.6 4.3 copy-start.16
  655.2 77.1 %reduce-scatter.13.cloned.1.call-start = ((), (), s32[]{:S(2)}) async-start(), calls=%async_computation.12 | async-start | bytes 1474560 | tf_op jit(solution)/shard_map/reduce_scatter | solution.py:289
  658.7 133.6 %reduce-scatter.15.cloned.1.call-start = ((), (), s32[]{:S(2)}) async-start(), calls=%async_computation.13 | async-start | bytes 5898240 | tf_op jit(solution)/shard_map/reduce_scatter | solution.py:301
  667.0 185.3 %reduce-scatter.17.cloned.1.call-start = ((), (), s32[]{:S(2)}) async-start(), calls=%async_computation.14 | async-start | bytes 5898240 | tf_op jit(solution)/shard_map/reduce_scatter | solution.py:307
  674.5 272.9 %all-reduce.23.cloned.1.call-start = ((), (), s32[]{:S(2)}) async-start(), calls=%async_computation.18 | async-start | bytes 7667712 | tf_op jit(solution)/shard_map/psum | solution.py:321
  703.2 150.6 %copy-start.17 = (bf16[192]{0:T(256)(128)(2,1)S(1)}, bf16[192]{0:T(256)(128)(2,1)}, u32[]{:S(2)}) copy-start(bf16[192]{0:T(256)(128)(2,1)} %param.35) | copy-start | bytes 1156
  855.9 37.5 %copy-start.2 = (f32[512,768]{1,0:T(8,128)S(1)}, f32[512,768]{1,0:T(8,128)}, u32[]{:S(2)}) copy-start(f32[512,768]{1,0:T(8,128)} %copy-done.1) | copy-start | bytes 4718596
  (9 other events, 18.2 us)
Sparse Core Ops, SparseCore 0:
  9.9 50.0 all-gather.7
  67.7 65.1 all-gather.11
  135.0 63.2 all-gather.9
  200.1 25.9 all-gather.13
  227.7 57.1 all-gather.15
  286.6 57.0 all-gather.17
  495.9 69.7 reduce-scatter.18
  568.1 68.1 reduce-scatter.20
  655.3 45.5 reduce-scatter.22
  703.7 28.5 reduce-scatter.12
  735.2 57.0 reduce-scatter.14
  795.2 57.0 reduce-scatter.16
  855.5 91.8 all-reduce.22
where the time goes:
time: 970 us; the launch traced here: 961 us
  waiting for transfers between devices  526 us (54%)
  matrix products  222 us (23%)
  local copies, waits for them, and re-layouts  98.2 us (10%)
  blocking collectives  68.7 us (7%)
  other arithmetic  27.7 us (3%)
  between operations  16.8 us (2%)
    unnamed x16, waiting for transfers between devices  145 us
    unnamed x81, local copies, waits for them, and re-layouts  80.3 us
    reduce_scatter x1, waiting for transfers between devices, on_device(): lax.psum_scatter(grad_inner_weight.astype(jnp.bfloat16), 'seq', scatter_d...  60.1 us
    reduce_scatter x1, waiting for transfers between devices, on_device(): lax.psum_scatter(grad_outer_weight.astype(jnp.bfloat16), 'seq', scatter_d...  60 us
    all_gather x1, waiting for transfers between devices, on_device(): key_part = lax.all_gather(keys_low, 'ctx', axis=1, tiled=True)  58.8 us
    psum x1, waiting for transfers between devices, on_device(): lax.psum(owned[0].astype(jnp.bfloat16), 'ctx').astype(jnp.float32)  48.1 us
    all_gather x1, waiting for transfers between devices, on_device(): lax.all_gather(outer_weight, 'seq', axis=0, tiled=True)  39 us
    all_gather x1, waiting for transfers between devices, on_device(): value_part = lax.all_gather(values_low, 'ctx', axis=1, tiled=True)  36.1 us
  transfers between devices with their start and end apart: 13, of which 12 were waited for; matrix products, arithmetic and copies ran while one was open for 17% of the time, Pallas kernels for 0%

commit v1 on v0

v1 whole, which is shorter than its diff:
```python
import functools

import jax
import jax.numpy as jnp
from jax import lax
from jax.experimental import pallas as pl
from jax.experimental.pallas import tpu as pltpu
from jax.sharding import PartitionSpec as P

HEAD_DIM = 64
EPS = 1e-12
NEG = -1e30
RB = 64
ROOT_HALF = 0.7071067811865476
PDF_SCALE = 0.3989422804014327
f32 = jnp.float32
bf16 = jnp.bfloat16
MESH = pl.DeviceIdType.MESH
ANY = pl.BlockSpec(memory_space=pl.ANY)
VMEM = pl.BlockSpec(memory_space=pltpu.VMEM)

QB, VB, OB, FG, FS, UB, SG, SS, IB = 0, 1, 2, 3, 4, 5, 6, 7, 8


def tile(i, width):
    return pl.ds(pl.multiple_of(i * width, width), width)


def span(start, width, unit=128):
    return pl.ds(pl.multiple_of(start, unit), width)


def dotf(a, b):
    return jnp.dot(a, b, preferred_element_type=f32)


def dotg(a, b, ca, cb):
    return lax.dot_general(a, b, (((ca,), (cb,)), ((), ())), preferred_element_type=f32)


def remote(src, dst, send_sem, recv_sem, **where):
    return pltpu.make_async_remote_copy(
        src_ref=src,
        dst_ref=dst,
        send_sem=send_sem,
        recv_sem=recv_sem,
        device_id=where,
        device_id_type=MESH,
    )


def enter(S, C):
    s, c = lax.axis_index("seq"), lax.axis_index("ctx")
    barrier = pltpu.get_barrier_semaphore()
    for d in range(1, S):
        pl.semaphore_signal(
            barrier, inc=1, device_id={"seq": lax.rem(s + d, S)}, device_id_type=MESH
        )

    def greet(d, carry):
        pl.semaphore_signal(
            barrier, inc=1, device_id={"ctx": lax.rem(c + d, C)}, device_id_type=MESH
        )
        return carry

    lax.fori_loop(1, C, greet, 0)
    pl.semaphore_wait(barrier, S - 1 + C - 1)


def bit_orders(S):
    bits = [1 << k for k in range(S.bit_length() - 1)]
    return (bits, bits[1:] + bits[:1])


def subsets(bits):
    out = [0]
    for b in bits:
        out = out + [o | b for o in out]
    return out


class Gather:
    def __init__(self, S, shard, full, send, recv, local):
        self.S, self.shard, self.full = S, shard, full
        self.send, self.recv, self.local = send, recv, local
        self.R, self.N = shard.shape
        self.s, self.c = lax.axis_index("seq"), lax.axis_index("ctx")
        self.core = lax.rem(self.c, 2)
        self.cols = span(self.core * (self.N // 2), self.N // 2)
        self.orders = bit_orders(S)
        self.half = self.R // 2

    def block(self, owner, p):
        return self.full.at[span(owner * self.R + p * self.half, self.half, 16), self.cols]

    def own(self, p):
        return self.shard.at[pl.ds(p * self.half, self.half), self.cols]

    def copy_own(self):
        return pltpu.make_async_copy(
            self.shard.at[:, self.cols],
            self.full.at[span(self.s * self.R, self.R, 16), self.cols],
            self.local,
        )

    def copies(self, t):
        out = []
        for p in range(2):
            order = self.orders[p]
            peer = jnp.bitwise_xor(self.s, order[t])
            for i, mask in enumerate(subsets(order[:t])):
                owner = jnp.bitwise_xor(self.s, mask)
                src = self.own(p) if mask == 0 else self.block(owner, p)
                k = (1 << t) - 1 + i
                out.append(
                    remote(src, self.block(owner, p), self.send.at[p, k], self.recv.at[p, k], seq=peer)
                )
        return out

    def swap(self):
        k = self.S - 1
        half = self.full.at[:, self.cols]
        other = jnp.bitwise_xor(self.c, 1)
        return remote(half, half, self.send.at[0, k], self.recv.at[0, k], ctx=other)

    def start(self, t):
        if t == 0:
            self.copy_own().start()
        for copy in self.copies(t):
            copy.start()

    def finish(self, t):
        for copy in self.copies(t):
            copy.wait_recv()

    def start_swap(self):
        self.copy_own().wait()
        self.swap().start()

    def finish_swap(self):
        self.swap().wait_recv()

    def drain(self):
        for t in range(len(self.orders[0])):
            for copy in self.copies(t):
                copy.wait_send()
        self.swap().wait_send()


class Regroup:
    def __init__(self, src, dst, send, recv, local, C, G):
        self.src, self.dst, self.send, self.recv, self.local = src, dst, send, recv, local
        self.G, self.M = G, C // G
        self.c = lax.axis_index("ctx")

    def dst_at(self, j):
        if len(self.dst.shape) == 2:
            rows = self.src.shape[1]
            return self.dst.at[tile(j, rows), :]
        return self.dst.at[j]

    def each(self, on_remote, on_local):
        place = lax.rem(self.c, self.G)
        for g in range(self.G):
            target = g * self.M + lax.div(self.c, self.G)
            far = remote(
                self.src.at[g], self.dst_at(place), self.send.at[g], self.recv.at[place], ctx=target
            )
            near = pltpu.make_async_copy(self.src.at[g], self.dst_at(place), self.local)

            @pl.when(target != self.c)
            def _():
                on_remote(far)

            @pl.when(target == self.c)
            def _():
                on_local(near)

    def start(self):
        self.each(lambda far: far.start(), lambda near: near.start())

    def drain(self):
        self.each(lambda far: far.wait_send(), lambda near: None)

    def finish(self):
        m = lax.rem(self.c, self.M)
        for j in range(self.G):
            source = m * self.G + j

            @pl.when(source != self.c)
            def _():
                remote(
                    self.src.at[0], self.dst_at(j), self.send.at[0], self.recv.at[j], ctx=source
                ).wait_recv()

            @pl.when(source == self.c)
            def _():
                pltpu.make_async_copy(self.src.at[0], self.dst_at(j), self.local).wait()


class Ungroup:
    def __init__(self, src, dst, send, recv, local, C, G):
        self.src, self.dst, self.send, self.recv, self.local = src, dst, send, recv, local
        self.G, self.M, self.P = G, C // G, dst.shape[1]
        self.c = lax.axis_index("ctx")

    def each(self, on_remote, on_local):
        g, m = lax.div(self.c, self.M), lax.rem(self.c, self.M)
        for j in range(self.G):
            target = m * self.G + j
            rows = self.src.at[pl.ds(j * self.P, self.P), :]
            far = remote(rows, self.dst.at[g], self.send.at[j], self.recv.at[g], ctx=target)
            near = pltpu.make_async_copy(rows, self.dst.at[g], self.local)

            @pl.when(target != self.c)
            def _():
                on_remote(far)

            @pl.when(target == self.c)
            def _():
                on_local(near)

    def start(self):
        self.each(lambda far: far.start(), lambda near: near.start())

    def drain(self):
        self.each(lambda far: far.wait_send(), lambda near: None)

    def finish(self):
        rows = self.src.at[pl.ds(0, self.P), :]
        for g in range(self.G):
            source = g * self.M + lax.div(self.c, self.G)

            @pl.when(source != self.c)
            def _():
                remote(
                    rows, self.dst.at[g], self.send.at[0], self.recv.at[g], ctx=source
                ).wait_recv()

            @pl.when(source == self.c)
            def _():
                pltpu.make_async_copy(rows, self.dst.at[g], self.local).wait()


def mask_bias(seg_keys, seg_queries, bias, G, PP):
    rows = [seg_queries[i].astype(f32) for i in range(G)]
    for a in range(G):
        column = jnp.broadcast_to(seg_keys[a].astype(f32), (PP, PP)).T
        for b in range(G):
            bias[a * PP : (a + 1) * PP, b * PP : (b + 1) * PP] = jnp.where(
                column == rows[b], jnp.zeros((PP, PP), f32), jnp.full((PP, PP), NEG, f32)
            ).astype(bias.dtype)


def norm_rows(x):
    centred = x - jnp.mean(x, axis=-1, keepdims=True)
    factor = lax.rsqrt(jnp.mean(centred * centred, axis=-1, keepdims=True) + EPS)
    return centred * factor, factor


def norm_back(g, gain, normed, factor):
    h = g * gain
    return factor * (
        h
        - jnp.mean(h, axis=-1, keepdims=True)
        - normed * jnp.mean(h * normed, axis=-1, keepdims=True)
    )


def loop(n, body):
    def step(i, carry):
        body(i)
        return carry

    lax.fori_loop(0, n, step, 0)


def colsum(x):
    return jnp.sum(x, axis=0, keepdims=True)


def forward_kernel(
    dims,
    hid, cot, seg, wq_s, wo_s, wi_s, wu_s, small,
    xs_o, wq_o, wo_o, wi_o, wu_o, k_o, v_o, q_o, qt_o, seg_o, lse_o, ctxt_o, ctx_o,
    n1_o, f1_o, flow_o, act_o, dgel_o, gsec_o, gb_o, out_o, smg_o, sm_o,
    xs, ct, wq, wo, wi, wu, small_all, segc, segk, q, qt, kown, vown, kc, vc, bias, m_s, l_s, ctxt, ctx,
    first, n1, f1, flow, h, act, dgel, n2, gsec, gb, outv,
    ag_send, ag_recv, ag_local, rg_send, rg_recv, rg_local, sm_send, sm_recv,
    kv_send, kv_recv, kv_local, kc_sem, out_sem,
):
    S, C, G, PP = dims
    M, L, D = C // G, G * PP, hid.shape[2]
    FF = wi.shape[1]
    NP = D // 128
    T = 256
    s, c = lax.axis_index("seq"), lax.axis_index("ctx")
    m = lax.rem(c, M)

    gathers = [
        Gather(S, shard, full, ag_send.at[w], ag_recv.at[w], ag_local.at[w])
        for w, (shard, full) in enumerate(((wq_s, wq), (wo_s, wo), (wi_s, wi), (wu_s, wu)))
    ]
    full_out = [wq_o, wo_o, wi_o, wu_o]
    steps = S.bit_length() - 1
    events = [(w, t) for w in range(4) for t in range(steps)]
    pending = []

    def put(src, dst):
        copy = pltpu.make_async_copy(src, dst, out_sem.at[len(pending)])
        copy.start()
        pending.append(copy)

    def tick(w, t):
        gathers[w].finish(t)
        k = events.index((w, t))
        if t + 1 < steps:
            gathers[w].start(t + 1)
        else:
            gathers[w].start_swap()
        for ahead in (k + 1, k + 2):
            if ahead < len(events) and events[ahead][1] == 0 and (ahead == k + 2 or steps == 1):
                gathers[events[ahead][0]].start(0)

    def ready(w):
        gathers[w].finish_swap()
        put(gathers[w].full, full_out[w])

    enter(S, C)
    hid_move = Regroup(hid, xs, rg_send.at[0], rg_recv.at[0], rg_local.at[0], C, G)
    cot_move = Regroup(cot, ct, rg_send.at[1], rg_recv.at[1], rg_local.at[1], C, G)
    seg_move = Regroup(seg, segc, rg_send.at[2], rg_recv.at[2], rg_local.at[2], C, G)
    seg_move.start()
    hid_move.start()
    gathers[0].start(0)
    small_copies = [
        remote(small, small_all.at[d - 1], sm_send.at[d - 1], sm_recv.at[d - 1], seq=jnp.bitwise_xor(s, d))
        for d in range(1, S)
    ]
    for copy in small_copies:
        copy.start()
    for t in range(steps):
        tick(0, t)
    seg_move.finish()

    group = lax.div(c, M) * M
    seg_own = pltpu.make_async_copy(segc, seg_o.at[m], kv_local.at[2])
    seg_own.start()

    def peer(d):
        return group + lax.rem(m + d, M)

    def kv_copies(d):
        return [
            remote(src, dst.at[m], kv_send.at[i, d], kv_recv.at[i, m], ctx=peer(d))
            for i, (src, dst) in enumerate(((kown, k_o), (vown, v_o), (segc, seg_o)))
        ]

    def kv_arrivals(d):
        j = lax.rem(m + d, M)
        return [
            remote(src, dst.at[j], kv_send.at[i, d], kv_recv.at[i, j], ctx=peer(d))
            for i, (src, dst) in enumerate(((kown, k_o), (vown, v_o), (segc, seg_o)))
        ]

    for d in range(1, M):
        kv_copies(d)[2].start()

    total = small[...].astype(f32)
    for copy in small_copies:
        copy.wait_recv()
    for d in range(1, S):
        total = total + small_all[d - 1].astype(f32)
    sm_o[...] = total
    hid_move.finish()
    cot_move.start()
    put(xs, xs_o)
    mask_bias(segc, segc, bias, G, PP)
    ready(0)

    def project(i):
        cols = tile(i, T)
        qv = dotf(xs[...], wq[:, cols]) + sm_o[QB : QB + 1, cols]
        kv = dotf(xs[...], wq[:, span(D + i * T, T)])
        vv = dotf(xs[...], wq[:, span(2 * D + i * T, T)]) + sm_o[VB : VB + 1, cols]
        qs = (qv.astype(bf16).astype(f32) * HEAD_DIM**-0.5).astype(bf16)
        kv, vv = kv.astype(bf16), vv.astype(bf16)
        for u in range(T // 128):
            lanes = slice(u * 128, (u + 1) * 128)
            hp = i * (T // 128) + u
            q[hp] = qs[:, lanes]
            qt[hp] = qs[:, lanes].T
            kown[hp] = kv[:, lanes]
            vown[hp] = vv[:, lanes]

    loop(D // T, project)
    for d in range(1, M):
        for copy in kv_copies(d)[:2]:
            copy.start()
    own_kv = [
        pltpu.make_async_copy(kown, k_o.at[m], kv_local.at[0]),
        pltpu.make_async_copy(vown, v_o.at[m], kv_local.at[1]),
    ]
    for copy in own_kv:
        copy.start()
    put(q, q_o)
    put(qt, qt_o)
    for t in range(steps):
        tick(1, t)

    row_of = lax.broadcasted_iota(jnp.int32, (128, L), 0)

    def attend(keys, values, fresh, extra):
        def pair(hp):
            extra(hp)
            qv, kv, vt, b = qt[hp], keys[hp], values[hp].T, bias[...]
            for e in range(2):
                head = slice(e * HEAD_DIM, (e + 1) * HEAD_DIM)
                mine = (row_of < HEAD_DIM) if e == 0 else (row_of >= HEAD_DIM)
                scores = dotf(kv, jnp.where(mine, qv, jnp.zeros_like(qv))) + b
                top = jnp.max(scores, axis=0, keepdims=True)
                if fresh:
                    weights = jnp.exp(scores - top)
                    m_s[hp, e : e + 1, :] = top
                    l_s[hp, e : e + 1, :] = colsum(weights)
                    ctxt[hp, head, :] = dotf(vt[head], weights.astype(bf16))
                else:
                    old = m_s[hp, e : e + 1, :]
                    top = jnp.maximum(old, top)
                    keep = jnp.exp(old - top)
                    weights = jnp.exp(scores - top)
                    m_s[hp, e : e + 1, :] = top
                    l_s[hp, e : e + 1, :] = l_s[hp, e : e + 1, :] * keep + colsum(weights)
                    ctxt[hp, head, :] = ctxt[hp, head, :] * keep + dotf(vt[head], weights.astype(bf16))

        loop(NP, pair)

    def in_own(hp):
        @pl.when(hp == NP - 2)
        def _():
            tick(2, 0)

    attend(kown, vown, True, in_own)

    def far_chunk(d, carry):
        j = lax.rem(m + d, M)
        for copy in kv_arrivals(d):
            copy.wait_recv()
        loads = [
            pltpu.make_async_copy(k_o.at[j], kc, kc_sem.at[0]),
            pltpu.make_async_copy(v_o.at[j], vc, kc_sem.at[1]),
            pltpu.make_async_copy(seg_o.at[j], segk, kc_sem.at[2]),
        ]
        for copy in loads:
            copy.start()
        for copy in loads:
            copy.wait()
        mask_bias(segk, segc, bias, G, PP)
        attend(kc, vc, False, lambda hp: None)
        return carry

    lax.fori_loop(1, M, far_chunk, 0)

    def close(hp):
        for e in range(2):
            head = slice(e * HEAD_DIM, (e + 1) * HEAD_DIM)
            ctxt[hp, head, :] = ctxt[hp, head, :] / l_s[hp, e : e + 1, :]
            l_s[hp, e : e + 1, :] = m_s[hp, e : e + 1, :] + jnp.log(l_s[hp, e : e + 1, :])
        ctx[:, tile(hp, 128)] = ctxt[hp].T.astype(bf16)

    loop(NP, close)

    put(ctxt, ctxt_o)
    put(ctx, ctx_o)
    put(l_s, lse_o)
    ready(1)

    def project_out(i):
        cols = tile(i, T)
        first[:, cols] = dotf(ctx[...], wo[:, cols]) + sm_o[OB : OB + 1, cols]

    loop(D // T, project_out)

    def first_norm(r):
        rows = tile(r, RB)
        normed, factor = norm_rows(first[rows, :] + xs[rows, :].astype(f32))
        y = normed * sm_o[FG : FG + 1, :] + sm_o[FS : FS + 1, :]
        n1[rows, :] = normed
        f1[rows, :] = factor
        first[rows, :] = y
        flow[rows, :] = y.astype(bf16)

    loop(L // RB, first_norm)
    put(n1, n1_o)
    put(f1, f1_o)
    put(flow, flow_o)
    for t in range(1, steps):
        tick(2, t)
    tick(3, 0)
    ready(2)

    def feed_in(i):
        cols = tile(i, D)
        h[...] = dotf(flow[...], wi[:, cols]) + sm_o[pl.ds(IB + i, 1), :]

        def gelu(k):
            rows, lanes = tile(lax.div(k, D // T), RB), lax.rem(k, D // T) * T
            x = h[rows, span(lanes, T)]
            share = 0.5 * (1.0 + lax.erf(x * ROOT_HALF))
            act[rows, span(i * D + lanes, T)] = (x * share).astype(bf16)
            dgel[rows, span(i * D + lanes, T)] = (
                share + x * (PDF_SCALE * jnp.exp(-0.5 * x * x))
            ).astype(bf16)

        loop(L // RB * (D // T), gelu)

    loop(FF // D, feed_in)
    put(act, act_o)
    put(dgel, dgel_o)
    for t in range(1, steps):
        tick(3, t)
    ready(3)

    def feed_out(i):
        cols = tile(i, T)
        n2[:, cols] = dotf(act[...], wu[:, cols]) + sm_o[UB : UB + 1, cols]

    loop(D // T, feed_out)
    cot_move.finish()
    smg_o[...] = jnp.zeros(smg_o.shape, f32)

    def second_norm(r):
        rows = tile(r, RB)
        normed, factor = norm_rows(first[rows, :] + n2[rows, :])
        gain = sm_o[SG : SG + 1, :]
        outv[rows, :] = (normed * gain + sm_o[SS : SS + 1, :]).astype(bf16)
        g = ct[rows, :].astype(f32)
        smg_o[SG : SG + 1, :] += colsum(g * normed)
        smg_o[SS : SS + 1, :] += colsum(g)
        back = norm_back(g, gain, normed, factor)
        gsec[rows, :] = back
        low = back.astype(bf16)
        gb[rows, :] = low
        smg_o[UB : UB + 1, :] += colsum(low.astype(f32))

    loop(L // RB, second_norm)
    put(outv, out_o)
    put(gsec, gsec_o)
    put(gb, gb_o)

    for gather in gathers:
        gather.drain()
    for move in (hid_move, cot_move, seg_move):
        move.drain()
    for copy in small_copies:
        copy.wait_send()
    for d in range(1, M):
        for copy in kv_copies(d):
            copy.wait_send()
    for copy in own_kv + [seg_own] + pending:
        copy.wait()


def forward_call(S, C, hid, cot, seg, wq_s, wo_s, wi_s, wu_s, small):
    G, PP, D = hid.shape
    L, M, NP, FF = G * PP, C // G, D // 128, wi_s.shape[1]
    sds = jax.ShapeDtypeStruct
    outs = [
        ((L, D), bf16), ((D, 3 * D), bf16), ((D, D), bf16), ((D, FF), bf16), ((FF, D), bf16),
        ((M, NP, L, 128), bf16), ((M, NP, L, 128), bf16), ((NP, L, 128), bf16), ((NP, 128, L), bf16),
        ((M, G, 1, PP), jnp.int32), ((NP, 2, L), f32), ((NP, 128, L), f32), ((L, D), bf16),
        ((L, D), f32), ((L, 1), f32), ((L, D), bf16), ((L, FF), bf16), ((L, FF), bf16),
        ((L, D), f32), ((L, D), bf16), ((L, D), bf16),
    ]
    scratch = [
        ((L, D), bf16), ((L, D), bf16), ((D, 3 * D), bf16), ((D, D), bf16), ((D, FF), bf16), ((FF, D), bf16),
        ((S - 1, 16, D), bf16), ((G, 1, PP), jnp.int32), ((G, 1, PP), jnp.int32),
        ((NP, L, 128), bf16), ((NP, 128, L), bf16), ((NP, L, 128), bf16), ((NP, L, 128), bf16),
        ((NP, L, 128), bf16), ((NP, L, 128), bf16), ((L, L), f32), ((NP, 2, L), f32), ((NP, 2, L), f32),
        ((NP, 128, L), f32), ((L, D), bf16),
        ((L, D), f32), ((L, D), f32), ((L, 1), f32), ((L, D), bf16), ((L, D), f32), ((L, FF), bf16),
        ((L, FF), bf16), ((L, D), f32), ((L, D), f32), ((L, D), bf16), ((L, D), bf16),
    ]
    dma = pltpu.SemaphoreType.DMA
    sems = [
        dma((4, 2, S)), dma((4, 2, S)), dma((4,)), dma((3, G)), dma((3, G)), dma((3,)),
        dma((S - 1,)), dma((S - 1,)), dma((3, M)), dma((3, M)), dma((3,)), dma((3,)), dma((24,)),
    ]
    return pl.pallas_call(
        functools.partial(forward_kernel, (S, C, G, PP)),
        out_shape=[sds(*o) for o in outs] + [sds((16, D), f32), sds((16, D), f32)],
        in_specs=[ANY] * 7 + [VMEM],
        out_specs=[ANY] * len(outs) + [VMEM, VMEM],
        scratch_shapes=[pltpu.VMEM(*x) for x in scratch] + sems,
        compiler_params=pltpu.CompilerParams(
            collective_id=0, has_side_effects=True, vmem_limit_bytes=62 << 20
        ),
        name="forward",
    )(hid, cot, seg, wq_s, wo_s, wi_s, wu_s, small)


def pack_small(S, vectors, inner_bias, D):
    s = lax.axis_index("seq")
    width = D // S
    owner = lax.broadcasted_iota(jnp.int32, (1, D), 1) // width
    rows = [jnp.where(owner == s, jnp.tile(v, S)[None, :], 0) for v in vectors]
    share = inner_bias.shape[0]
    flat = jnp.tile(inner_bias, S)
    where = lax.broadcasted_iota(jnp.int32, (1, share * S), 1) // share
    full = jnp.where(where == s, flat[None, :], 0).reshape(share * S // D, D)
    used = len(vectors) + share * S // D
    return jnp.concatenate(rows + [full, jnp.zeros((16 - used, D), bf16)], axis=0).astype(bf16)


def add_rows(dst, src):
    rows = dst.shape[0]
    unit = next(u for u in (96, 48, 16) if rows % u == 0)

    def step(r):
        at = tile(r, unit)
        dst[at, :] = (dst[at, :].astype(f32) + src[at, :].astype(f32)).astype(bf16)

    loop(rows // unit, step)


class Reduce:
    def __init__(self, S, C, part, far, rx, zl, zr, sems, places):
        self.S, self.K, self.part, self.far, self.rx, self.zl, self.zr = S, C // 2, part, far, rx, zl, zr
        self.c_send, self.c_recv, self.x_send, self.x_recv, self.z_send, self.z_recv, self.l_send = sems
        self.places = places
        self.R = part.shape[1] // S
        self.half = self.R // 2
        self.s, self.c = lax.axis_index("seq"), lax.axis_index("ctx")
        self.core = lax.rem(self.c, 2)
        self.k = lax.div(self.c, 2)
        self.root = self.K // 2
        self.orders = bit_orders(S)
        self.steps = len(self.orders[0])
        self.levels = max(self.root, self.K - 1 - self.root)
        self.mine = part.at[self.core]

    def block(self, owner, p):
        return self.part.at[self.core, span(owner * self.R + p * self.half, self.half, 16), :]

    def result(self, core):
        return self.part.at[core, span(self.s * self.R, self.R, 16), :]

    def core_copy(self):
        other = 1 - self.core
        return remote(
            self.part.at[other], self.far, self.c_send.at[0], self.c_recv.at[0], ctx=jnp.bitwise_xor(self.c, 1)
        )

    def core_start(self):
        self.core_copy().start()

    def copies(self, t):
        out, base = [], self.S - (1 << (self.steps - t))
        for p in range(2):
            order = self.orders[p]
            peer = jnp.bitwise_xor(self.s, order[t])
            for i, mask in enumerate(subsets(order[t + 1 :])):
                copy = remote(
                    self.block(jnp.bitwise_xor(peer, mask), p),
                    self.rx.at[p, base + i],
                    self.x_send.at[p, base + i],
                    self.x_recv.at[p, base + i],
                    seq=peer,
                )
                out.append((copy, p, base + i, mask))
        return out

    def cross_start(self, t):
        if t == 0:
            self.core_copy().wait_recv()
            add_rows(self.mine, self.far)
        else:
            self.cross_add(t - 1)
        for copy, _, _, _ in self.copies(t):
            copy.start()

    def cross_add(self, t):
        for copy, p, slot, mask in self.copies(t):
            copy.wait_recv()
            add_rows(self.block(jnp.bitwise_xor(self.s, mask), p), self.rx.at[p, slot])

    def up(self, side):
        src = self.result(self.core)
        if side == 0:
            return remote(src, self.zl, self.z_send.at[0], self.z_recv.at[0], ctx=self.c + 2)
        return remote(src, self.zr, self.z_send.at[0], self.z_recv.at[1], ctx=self.c - 2)

    def take(self, side):
        self.up(side).wait_recv()
        add_rows(self.result(self.core), self.zl if side == 0 else self.zr)

    def down(self, side, src):
        target = self.c - 2 if side == 0 else self.c + 2
        dst = self.zr if side == 0 else self.zl
        return remote(src, dst, self.z_send.at[1 + side], self.z_recv.at[2], ctx=target)

    def chain_up(self, level):
        if level == 0:
            self.cross_add(self.steps - 1)
        if level < self.root:

            @pl.when(self.k == level)
            def _():
                if level > 0:
                    self.take(0)
                self.up(0).start()

        if level < self.K - 1 - self.root:

            @pl.when(self.k == self.K - 1 - level)
            def _():
                if level > 0:
                    self.take(1)
                self.up(1).start()

    def chain_root(self):
        @pl.when(self.k == self.root)
        def _():
            if self.root > 0:
                self.take(0)
            if self.root < self.K - 1:
                self.take(1)
            src = self.result(self.core)
            if self.root > 0:
                self.down(0, src).start()
            if self.root < self.K - 1:
                self.down(1, src).start()
            self.deliver(src)

    def chain_down(self, distance):
        if self.root - distance >= 0:

            @pl.when(self.k == self.root - distance)
            def _():
                self.down(0, self.zr).wait_recv()
                if self.root - distance > 0:
                    self.down(0, self.zr).start()
                self.deliver(self.zr)

        if self.root + distance < self.K:

            @pl.when(self.k == self.root + distance)
            def _():
                self.down(1, self.zl).wait_recv()
                if self.root + distance < self.K - 1:
                    self.down(1, self.zl).start()
                self.deliver(self.zl)

    def deliveries(self, src):
        out = []
        for i, (cols, place) in enumerate(self.places):
            dst = place(self.core)
            out.append(
                (
                    pltpu.make_async_copy(src.at[:, cols], dst, self.l_send.at[i]),
                    remote(
                        src.at[:, cols], dst, self.c_send.at[1 + i], self.c_recv.at[1 + i], ctx=jnp.bitwise_xor(self.c, 1)
                    ),
                )
            )
        return out

    def deliver(self, src):
        for near, far in self.deliveries(src):
            near.start()
            far.start()

    def finish(self):
        for near, far in self.deliveries(self.zl):
            near.wait()
            far.wait_recv()

    def stages(self):
        out = [functools.partial(self.cross_start, t) for t in range(self.steps)]
        out += [functools.partial(self.chain_up, v) for v in range(self.levels)]
        out += [self.chain_root]
        out += [functools.partial(self.chain_down, d) for d in range(1, self.levels + 1)]
        return out + [self.finish]

    def drain(self):
        self.core_copy().wait_send()
        for t in range(self.steps):
            for copy, _, _, _ in self.copies(t):
                copy.wait_send()
        last = self.K - 1

        @pl.when(self.k != self.root)
        def _():
            self.up(0).wait_send()

        @pl.when(jnp.logical_and(self.k <= self.root, self.k > 0))
        def _():
            self.down(0, self.zr).wait_send()

        @pl.when(jnp.logical_and(self.k >= self.root, self.k < last))
        def _():
            self.down(1, self.zl).wait_send()

        for _, far in self.deliveries(self.zl):
            far.wait_send()


def backward_kernel(
    dims,
    outv, gsec_i, gb_i, act_i, dgel_i, wu_i, wi_i, wo_i, wq_i, flow_i, n1_i, f1_i, xs_i, ctx_i, ctxt_i,
    q_i, qt_i, k_i, v_i, seg_i, lse_i, smg_i, sm,
    out_o, gin_o, gq_o, go_o, gi_o, gu_o, land_o, small_o,
    pu, pi, po, pq, ps, fu, fi, fo, fq, fs, ru, ri, ro, rq, rs, zlu, zli, zlo, zlq, zls, zru, zri, zro, zrq, zrs,
    gsec, gb, grad_o, grad_ot, delta, smg,
    c_send, c_recv, x_send, x_recv, z_send, z_recv, rg_send, rg_recv, rg_local, in_sem, kv_sem, dkv_send, dkv_recv,
    land_sem, l_send,
):
    S, C, G, PP = dims
    M, L, D = C // G, G * PP, gsec.shape[1]
    FF = act_i.shape[1]
    NP = D // 128
    T = 256
    s, c = lax.axis_index("seq"), lax.axis_index("ctx")
    m, core = lax.rem(c, M), lax.rem(c, 2)
    group = lax.div(c, M) * M

    def piece(n, places, *refs):
        sems = [a.at[n] for a in (c_send, c_recv, x_send, x_recv, z_send, z_recv, l_send)]
        return Reduce(S, C, *refs, sems, places)

    H = D // 2
    sum_u = piece(0, [(pl.ds(0, H), lambda e: gu_o.at[:, span(e * H, H)])], pu, fu, ru, zlu, zru)
    sum_i = [
        piece(
            1 + i, [(pl.ds(0, D), lambda e, i=i: gi_o.at[:, span(e * (FF // 2) + i * D, D)])],
            pi.at[i], fi.at[i], ri.at[i], zli.at[i], zri.at[i],
        )
        for i in range(2)
    ]
    sum_o = piece(3, [(pl.ds(0, H), lambda e: go_o.at[:, span(e * H, H)])], po, fo, ro, zlo, zro)
    sum_q = [
        piece(
            4 + i,
            [
                (pl.ds(a * 128, 128), lambda e, i=i, a=a: gq_o.at[:, span(a * D + (2 * i + e) * 128, 128)])
                for a in range(3)
            ],
            pq.at[i], fq.at[i], rq.at[i], zlq.at[i], zrq.at[i],
        )
        for i in range(3)
    ]
    sum_s = piece(7, [(pl.ds(0, ps.shape[2]), lambda e: small_o.at[e])], ps, fs, rs, zls, zrs)

    def stages_of(item):
        return item.stages()

    steps = S.bit_length() - 1
    ticks = {
        "u": stages_of(sum_u), "i0": stages_of(sum_i[0]), "i1": stages_of(sum_i[1]), "o": stages_of(sum_o),
        "q0": stages_of(sum_q[0]), "q1": stages_of(sum_q[1]), "q2": stages_of(sum_q[2]), "s": stages_of(sum_s),
    }
    at = {name: 0 for name in ticks}

    def tick(name, until):
        while at[name] < min(until, len(ticks[name])):
            ticks[name][at[name]]()
            at[name] += 1

    enter(S, C)
    out_move = Ungroup(outv, out_o, rg_send.at[0], rg_recv.at[0], rg_local.at[0], C, G)
    out_move.start()
    smg[...] = smg_i[...]

    def feed_forward(act, dgel, wu, wi, h, n1, f1, flow):
        loads = [
            pltpu.make_async_copy(src, dst, in_sem.at[i])
            for i, (src, dst) in enumerate(
                ((gb_i, gb), (act_i, act), (wu_i, wu), (dgel_i, dgel), (flow_i, flow), (wi_i, wi), (gsec_i, gsec),
                 (n1_i, n1), (f1_i, f1))
            )
        ]
        for copy in loads:
            copy.start()
        loads[0].wait()
        loads[1].wait()

        def outer_grad(i):
            rows = tile(i, 512)
            block = dotg(act[:, rows], gb[...], 0, 0).astype(bf16)
            for e in range(2):
                pu[e, rows, :] = block[:, e * (D // 2) : (e + 1) * (D // 2)]

        loop(FF // 512, outer_grad)
        sum_u.core_start()
        for copy in loads[2:5]:
            copy.wait()

        def inner_grad(i, half):
            where = half * (FF // 2) + i * D
            cols = span(where, D)
            h[...] = dotg(gb[...], wu[span(where, D), :], 1, 1)

            def through(k, sums):
                rows = tile(k, RB)
                low = (h[rows, :] * dgel[rows, cols].astype(f32)).astype(bf16)
                act[rows, cols] = low
                return sums + colsum(low.astype(f32))

            sums = lax.fori_loop(0, L // RB, through, jnp.zeros((1, D), f32))
            smg[pl.ds(IB + half * (FF // 2 // D) + i, 1), :] = sums

            def grad(k):
                rows = tile(k, T)
                pi[i, half, rows, :] = dotg(flow[:, rows], act[:, cols], 0, 0).astype(bf16)

            loop(D // T, grad)

        inner_grad(0, 1 - core)
        inner_grad(0, core)
        sum_i[0].core_start()
        tick("u", 1)
        inner_grad(1, 1 - core)
        inner_grad(1, core)
        sum_i[1].core_start()
        tick("i0", 1)
        loads[5].wait()
        loads[6].wait()

        def first_grad(i):
            cols = tile(i, T)
            gsec[:, cols] += dotg(act[...], wi[cols, :], 1, 1)

        loop(D // T, first_grad)
        tick("i1", 1)
        loads[7].wait()
        loads[8].wait()

        def first_back(k):
            rows = tile(k, RB)
            g, normed = gsec[rows, :], n1[rows, :]
            smg[FG : FG + 1, :] += colsum(g * normed)
            smg[FS : FS + 1, :] += colsum(g)
            back = norm_back(g, sm[FG : FG + 1, :], normed, f1[rows, :])
            gsec[rows, :] = back
            low = back.astype(bf16)
            gb[rows, :] = low
            smg[OB : OB + 1, :] += colsum(low.astype(f32))

        loop(L // RB, first_back)

    V = pltpu.VMEM
    pl.run_scoped(
        feed_forward, V((L, FF), bf16), V((L, FF), bf16), V((FF, D), bf16), V((D, FF), bf16), V((L, D), f32),
        V((L, D), f32), V((L, 1), f32), V((L, D), bf16),
    )
    tick("u", steps)

    def context_back(wo, ctx, ctxt):
        loads = [
            pltpu.make_async_copy(src, dst, in_sem.at[i])
            for i, (src, dst) in enumerate(((ctx_i, ctx), (wo_i, wo), (ctxt_i, ctxt)))
        ]
        for copy in loads:
            copy.start()
        loads[0].wait()

        def out_grad(k):
            rows = tile(k, T)
            block = dotg(ctx[:, rows], gb[...], 0, 0).astype(bf16)
            for e in range(2):
                po[e, rows, :] = block[:, e * (D // 2) : (e + 1) * (D // 2)]

        loop(D // T, out_grad)
        sum_o.core_start()
        loads[1].wait()
        loads[2].wait()

        def back(k):
            grad = dotg(gb[...], wo[tile(k, T), :], 1, 1).astype(bf16)
            for u in range(T // 128):
                hp = k * (T // 128) + u
                mine = grad[:, u * 128 : (u + 1) * 128]
                turned = mine.T
                grad_o[hp] = mine
                grad_ot[hp] = turned
                both = turned.astype(f32) * ctxt[hp]
                for e in range(2):
                    delta[hp, e : e + 1, :] = colsum(both[e * HEAD_DIM : (e + 1) * HEAD_DIM])

        loop(D // T, back)

    pl.run_scoped(context_back, V((D, D), bf16), V((L, D), bf16), V((NP, 128, L), f32))

    def attention(wq, xs, q, qt, kb, vb, bias, lse, own_k, own_v, stage, land, segs, grads, dqt, turned_q):
        loads = [
            pltpu.make_async_copy(src, dst, in_sem.at[i])
            for i, (src, dst) in enumerate(
                ((seg_i, segs), (q_i, q), (qt_i, qt), (lse_i, lse), (xs_i, xs), (wq_i, wq))
            )
        ]

        def kv_load(hp):
            slot = lax.rem(hp, 2)
            return [
                pltpu.make_async_copy(src.at[:, hp], dst.at[slot], kv_sem.at[i, slot])
                for i, (src, dst) in enumerate(((k_i, kb), (v_i, vb)))
            ]

        for copy in kv_load(0) + loads:
            copy.start()
        for copy in loads[:4]:
            copy.wait()
        for j in range(M):
            mask_bias(segs.at[j], segs.at[m], bias.at[j], G, PP)
        row_of = lax.broadcasted_iota(jnp.int32, (128, L), 0)
        lane_of = lax.broadcasted_iota(jnp.int32, (L, 128), 1)

        def send_back(hp, d):
            slot = lax.rem(hp, 2)
            return remote(
                stage.at[slot, d - 1], land_o.at[hp, d - 1], dkv_send.at[slot, d - 1], dkv_recv.at[hp, d - 1],
                ctx=group + lax.rem(m + d, M),
            )

        def chunk(hp, slot, j):
            key, value, b = kb[slot, j], vb[slot, j], bias[j].astype(f32)
            turned = key.T
            query, query_t, up, up_t = q[hp], qt[hp], grad_o[hp], grad_ot[hp]
            sums = []
            for e in range(2):
                rows = (row_of < HEAD_DIM) if e == 0 else (row_of >= HEAD_DIM)
                lanes = (lane_of < HEAD_DIM) if e == 0 else (lane_of >= HEAD_DIM)
                zero, zero_t = jnp.zeros_like(query), jnp.zeros_like(query_t)
                scores = dotf(key, jnp.where(rows, query_t, zero_t)) + b
                probs = jnp.exp(scores - lse[hp, e : e + 1, :])
                dprobs = dotf(value, jnp.where(rows, up_t, zero_t))
                dscores = (probs * (dprobs - delta[hp, e : e + 1, :])).astype(bf16)
                sums.append(
                    (
                        dotf(dscores, jnp.where(lanes, query, zero)),
                        dotf(probs.astype(bf16), jnp.where(lanes, up, zero)),
                    )
                )
                head = slice(e * HEAD_DIM, (e + 1) * HEAD_DIM)
                dqt[head, :] += dotf(turned[head], dscores)
            return sums[0][0] + sums[1][0], sums[0][1] + sums[1][1]

        def pair(hp):
            slot = lax.rem(hp, 2)
            for copy in kv_load(hp):
                copy.wait()

            @pl.when(hp + 1 < NP)
            def _():
                for copy in kv_load(hp + 1):
                    copy.start()

            dqt[...] = jnp.zeros(dqt.shape, f32)

            def far(d, carry):
                @pl.when(hp >= 2)
                def _():
                    send_back(hp - 2, d).wait_send()

                dk, dv = chunk(hp, slot, lax.rem(m + d, M))
                stage[slot, d - 1, 0] = dk.astype(bf16)
                stage[slot, d - 1, 1] = dv.astype(bf16)
                send_back(hp, d).start()
                return carry

            lax.fori_loop(1, M, far, 0)
            dk, dv = chunk(hp, slot, m)
            own_k[slot] = dk
            own_v[slot] = dv
            turned_q[slot] = (dqt[...] * HEAD_DIM**-0.5).T.astype(bf16)

        def fetch(i):
            for u in range(2):
                for d in range(1, M):
                    send_back(2 * i + u, d).wait_recv()
            if M > 1:
                pltpu.make_async_copy(land_o.at[pl.ds(2 * i, 2)], land, land_sem.at[0]).start()

        def project_back(i):
            if M > 1:
                pltpu.make_async_copy(land_o.at[pl.ds(2 * i, 2)], land, land_sem.at[0]).wait()
            for u in range(2):
                dk, dv = own_k[u], own_v[u]
                for d in range(1, M):
                    dk = dk + land[u, d - 1, 0].astype(f32)
                    dv = dv + land[u, d - 1, 1].astype(f32)
                grads[:, u * 128 : (u + 1) * 128] = turned_q[u]
                grads[:, T + u * 128 : T + (u + 1) * 128] = dk.astype(bf16)
                grads[:, 2 * T + u * 128 : 2 * T + (u + 1) * 128] = dv.astype(bf16)
            cols = tile(i, T)
            smg[QB : QB + 1, cols] = colsum(grads[:, 0:T].astype(f32))
            smg[VB : VB + 1, cols] = colsum(grads[:, 2 * T : 3 * T].astype(f32))

            def weight(k):
                rows = tile(k, T)
                block = dotg(xs[:, rows], grads[...], 0, 0).astype(bf16)
                for a in range(3):
                    for e in range(2):
                        pq[i, e, rows, a * 128 : (a + 1) * 128] = block[:, a * T + e * 128 : a * T + (e + 1) * 128]

            loop(D // T, weight)

        def input_back(i):
            def back(k):
                rows = tile(k, T)
                total = gsec[:, rows]
                for a in range(3):
                    total = total + dotg(grads[:, a * T : (a + 1) * T], wq[rows, span(a * D + i * T, T)], 1, 1)
                gsec[:, rows] = total

            loop(D // T, back)

        def drain_stage():
            for hp in (NP - 2, NP - 1):
                for d in range(1, M):
                    send_back(hp, d).wait_send()

        def pair_group(i):
            loop(2, lambda u: pair(2 * i + u))

        pair_group(0)
        tick("o", 1)
        tick("i0", steps)
        fetch(0)
        tick("i1", steps)
        tick("u", steps + 1)
        loads[4].wait()
        loads[5].wait()
        project_back(0)
        sum_q[0].core_start()
        input_back(0)
        tick("o", steps)
        tick("i0", steps + 1)
        tick("q0", 1)
        pair_group(1)
        tick("u", steps + 2)
        tick("i1", steps + 1)
        tick("o", steps + 1)
        fetch(1)
        tick("i0", steps + 2)
        tick("q0", steps)
        project_back(1)
        sum_q[1].core_start()
        input_back(1)
        tick("i1", steps + 2)
        tick("o", steps + 2)
        tick("u", steps + 3)
        tick("q1", 1)
        pair_group(2)
        for name in ("i0", "i1", "o"):
            tick(name, steps + 3)
        tick("q0", steps + 1)
        tick("u", steps + 4)
        fetch(2)
        tick("q1", steps)
        tick("q0", steps + 2)
        project_back(2)
        sum_q[2].core_start()

        W = ps.shape[2]
        width = D // S
        ps[...] = jnp.zeros(ps.shape, bf16)
        share = FF // S
        for owner in range(S):
            base = owner * ps.shape[1] // S
            ps[0, base : base + 8, 0:width] = smg[0:8, owner * width : (owner + 1) * width].astype(bf16)
            for r in range(share // width):
                start = owner * share + r * width
                a, b = start // D, start % D
                ps[0, base + 16 + r : base + 17 + r, 0:width] = smg[IB + a : IB + a + 1, b : b + width].astype(bf16)
        sum_s.core_start()
        input_back(2)
        tick("q2", 1)
        tick("s", 1)
        for r in range(L // PP):
            rows = pl.ds(r * PP, PP)
            grads[rows, :] = gsec[rows, :].astype(bf16)
        gin_move = Ungroup(grads, gin_o, rg_send.at[1], rg_recv.at[1], rg_local.at[1], C, G)
        gin_move.start()
        order = ("u", "i0", "i1", "o", "q0", "q1", "q2", "s")
        for stage_no in range(2, len(ticks["u"])):
            for name in ("q2", "s", "q1", "q0", "o", "i1", "i0", "u"):
                tick(name, stage_no)
        for name in order:
            tick(name, len(ticks[name]))
        gin_move.finish()
        gin_move.drain()
        drain_stage()

    pl.run_scoped(
        attention, V((D, 3 * D), bf16), V((L, D), bf16), V((NP, L, 128), bf16), V((NP, 128, L), bf16),
        V((2, M, L, 128), bf16), V((2, M, L, 128), bf16), V((M, L, L), f32 if M <= 2 else bf16), V((NP, 2, L), f32),
        V((2, L, 128), f32), V((2, L, 128), f32), V((2, max(M - 1, 1), 2, L, 128), bf16),
        V((2, max(M - 1, 1), 2, L, 128), bf16), V((M, G, 1, PP), jnp.int32), V((L, 3 * T), bf16), V((128, L), f32),
        V((2, L, 128), bf16),
    )
    out_move.finish()
    out_move.drain()
    for item in [sum_u] + sum_i + [sum_o] + sum_q + [sum_s]:
        item.drain()


def backward_call(S, C, G, PP, saved):
    (xs, wq, wo, wi, wu, k, v, q, qt, seg, lse, ctxt, ctx, n1, f1, flow, act, dgel, gsec, gb, outv, smg, sm) = saved
    L, D = xs.shape
    M, NP, FF = C // G, D // 128, wi.shape[1]
    R, RU = D // S, FF // S
    sds = jax.ShapeDtypeStruct
    land = max(M - 1, 1)
    H, SR, SW = D // 2, 32, 256
    outs = [
        ((G, PP, D), bf16), ((G, PP, D), bf16), ((R, 3 * D), bf16), ((R, D), bf16), ((R, FF), bf16), ((RU, D), bf16),
        ((NP, land, 2, L, 128), bf16), ((2, SR, SW), bf16),
    ]
    scratch = [
        (2, FF, H), (2, 2, D, D), (2, D, H), (3, 2, D, H), (2, S * SR, SW),
        (FF, H), (2, D, D), (D, H), (3, D, H), (S * SR, SW),
        (2, S - 1, RU // 2, H), (2, 2, S - 1, R // 2, D), (2, S - 1, R // 2, H), (3, 2, S - 1, R // 2, H),
        (2, S - 1, SR // 2, SW),
        (RU, H), (2, R, D), (R, H), (3, R, H), (SR, SW),
        (RU, H), (2, R, D), (R, H), (3, R, H), (SR, SW),
    ]
    scratch = [(x, bf16) for x in scratch] + [
        ((L, D), f32), ((L, D), bf16), ((NP, L, 128), bf16), ((NP, 128, L), bf16), ((NP, 2, L), f32), ((16, D), f32),
    ]
    dma = pltpu.SemaphoreType.DMA
    sems = [
        dma((8, 4)), dma((8, 4)), dma((8, 2, S - 1)), dma((8, 2, S - 1)), dma((8, 3)), dma((8, 3)),
        dma((2, G)), dma((2, G)), dma((2,)), dma((10,)), dma((2, 2)), dma((2, land)), dma((NP, land)), dma((1,)),
        dma((8, 3)),
    ]
    results = pl.pallas_call(
        functools.partial(backward_kernel, (S, C, G, PP)),
        out_shape=[sds(*o) for o in outs],
        in_specs=[ANY] * 21 + [VMEM, VMEM],
        out_specs=[ANY] * len(outs),
        scratch_shapes=[pltpu.VMEM(*x) for x in scratch] + sems,
        compiler_params=pltpu.CompilerParams(
            collective_id=1, has_side_effects=True, vmem_limit_bytes=62 << 20
        ),
        name="backward",
    )(outv, gsec, gb, act, dgel, wu, wi, wo, wq, flow, n1, f1, xs, ctx, ctxt, q, qt, k, v, seg, lse, smg, sm)
    return results


def solution(mesh):
    S, C = mesh.shape["seq"], mesh.shape["ctx"]

    def on_device(
        hid, cot, seg, wq, qb, vb, wo, ob, fg, fs, wi, ib, wu, ub, sg, ss
    ):
        G, PP, D = hid.shape
        small = pack_small(S, [qb, vb, ob, fg, fs, ub, sg, ss], ib, D)
        saved = forward_call(S, C, hid, cot, seg.reshape(G, 1, PP), wq, wo, wi, wu, small)
        out, gin, gq, go, gi, gu, _, gs = backward_call(S, C, G, PP, saved)
        gs = gs[0].astype(f32)
        width = D // S
        row = lambda r: gs[r, :width]
        grad_ib = gs[16 : 16 + ib.shape[0] // width, :width].reshape(-1)
        return (
            out, gin.astype(f32), gq.astype(f32), row(QB), row(VB), go.astype(f32), row(OB), row(FG), row(FS),
            gi.astype(f32), grad_ib, gu.astype(f32), row(UB), row(SG), row(SS),
        )

    rows, matrix, vector = P("seq", "ctx", None), P("seq", None), P("seq")
    return jax.shard_map(
        on_device,
        mesh=mesh,
        in_specs=(
            rows, rows, P("seq", "ctx"), matrix, vector, vector, matrix, vector, vector, vector, matrix, vector,
            matrix, vector, vector, vector,
        ),
        out_specs=(
            rows, rows, matrix, vector, vector, matrix, vector, vector, vector, matrix, vector, matrix, vector,
            vector, vector,
        ),
        check_vma=False,
    )
```

time: 970 us -> 269 us (0.28)
  waiting for transfers between devices: 526 us -> 0 us
  Pallas kernels: 0 us -> 247 us
  matrix products: 222 us -> 0 us
  local copies, waits for them, and re-layouts: 98.2 us -> 9.9 us
  blocking collectives: 68.7 us -> 0 us
  other arithmetic: 27.7 us -> 10.4 us
  between operations: 16.8 us -> 0.71 us
    pallas_call x0 -> x2, Pallas kernels: none -> 247 us  [the longest x1 159 us: backward_call(): pl.pallas_call(functools.partial(backward_kernel, (S, C, G, PP)), out_sha...]
    dot_general x96 -> x0, matrix products: 222 us -> none  [the longest x12 25.9 us: grads_block(): jnp.einsum('sqk,skd->sqd', grad_scores, key_one, preferred_element_type=j...]
    all_gather x6 -> x0, waiting for transfers between devices: 184 us -> none  [the longest x1 58.8 us: on_device(): key_part = lax.all_gather(keys_low, 'ctx', axis=1, tiled=True)]
    reduce_scatter x3 -> x0, waiting for transfers between devices: 149 us -> none  [the longest x1 60.1 us: on_device(): lax.psum_scatter(grad_inner_weight.astype(jnp.bfloat16), 'seq', scatter_d...]
    unnamed x16 -> x0, waiting for transfers between devices: 145 us -> none
    unnamed x81 -> x9, local copies, waits for them, and re-layouts: 80.3 us -> 1.38 us
    psum x1 -> x0, waiting for transfers between devices: 48.1 us -> none  [on_device(): lax.psum(owned[0].astype(jnp.bfloat16), 'ctx').astype(jnp.float32)]
    unnamed x2 -> x0, blocking collectives: 33.3 us -> none
  transfers between devices with their start and end apart: 13 -> 0, of which waited for: 12 -> 0; matrix products, arithmetic and copies ran while one was open for 17% -> 0% of each run, Pallas kernels for 0% -> 0%
where the time goes in v1:
time: 269 us; the launch traced here: 268 us
  Pallas kernels  247 us (92%)
  other arithmetic  10.4 us (4%)
  local copies, waits for them, and re-layouts  9.9 us (4%)
    pallas_call x1, Pallas kernels, backward_call(): pl.pallas_call(functools.partial(backward_kernel, (S, C, G, PP)), out_sha...  159 us
    pallas_call x1, Pallas kernels, forward_call(): pl.pallas_call(functools.partial(forward_kernel, (S, C, G, PP)), out_shap...  88 us
    another operation x16, local copies, waits for them, and re-layouts, pack_small(): rows = [jnp.where(owner == s, jnp.tile(v, S)[None, :], 0) for v in vectors]  5.98 us

profile of v1, /device:TPU:0, one launch (start us, length us, event | category | flops | bytes accessed | tf_op | source)
XLA Modules:
  0.0 268.0 jit_solution(4885228512498786104)
XLA Ops:
  0.6 0.7 tile.18
  1.3 0.1 broadcast_in_dim_tile.25
  1.4 0.7 tile.19
  2.1 0.1 broadcast_in_dim_tile.26
  2.2 0.7 tile.20
  2.9 0.7 tile.21
  3.7 0.7 tile.22
  4.4 0.7 tile.23
  5.2 0.7 tile.24
  5.9 0.7 tile.25
  6.7 0.7 fusion.2
  7.4 1.3 concatenate.3.small
  8.7 88.0 %forward.1 = (bf16[512,768]{1,0:T(8,128)(2,1)}, bf16[768,2304]{1,0:T(8,128)(2,1)}, bf16[768,768]{1,0:T(8,128)(2,1)}, bf16[768,3072]{1,0:T(8,128)(2,1)}, bf16[307...) custom-call(bf16[4,128,768]{2,1,0:T(8,128)(2,1)} %hid.1, ...), custom_call_target="tpu_custom_call" | custom-call | tf_op jit(solution)/shard_map/forward/pallas_call | solution.py:589
  96.7 159.0 %backward.1 = (bf16[4,128,768]{2,1,0:T(8,128)(2,1)}, bf16[4,128,768]{2,1,0:T(8,128)(2,1)}, bf16[192,2304]{1,0:T(8,128)(2,1)}, bf16[192,768]{1,0:T(8,128)(2,1)}, ...) custom-call(bf16[512,768]{1,0:T(8,128)(2,1)} %get-tuple-element.45.o, ...), custom_call_target="tpu_custom_call" | custom-call | tf_op jit(solution)/shard_map/backward/pallas_call | solution.py:1237
  255.7 0.7 bitcast_convert_fusion
  256.4 0.6 fusion.4
  257.0 0.7 reshape.211
  257.7 1.9 convert_element_type.36
  259.6 2.4 convert_element_type.32
  262.0 1.3 convert_element_type.33
  263.3 0.5 copy-done.1
  263.8 1.7 convert_element_type.37
  265.5 1.6 convert_element_type.38
  267.1 0.9 copy.32
  (19 shorter events, 0.6 us)
Async XLA Ops:
  257.7 4.3 %copy-start.2 = (bf16[192,2304]{1,0:T(8,128)(2,1)S(1)}, bf16[192,2304]{1,0:T(8,128)(2,1)}, u32[]{:S(2)}) copy-start(bf16[192,2304]{1,0:T(8,128)(2,1)} %get-tuple-element.70) | copy-start | bytes 2654212
  262.0 1.8 copy-start.1
  263.8 1.7 copy-start
  265.5 1.6 copy-start.3

commit v2 on v1

--- a/solution.py
+++ b/solution.py
@@ -80,71 +80,100 @@
 
 
 class Gather:
-    def __init__(self, S, shard, full, send, recv, local):
+    def __init__(self, S, shard, full, send, recv, swap_send, swap_recv, local):
         self.S, self.shard, self.full = S, shard, full
         self.send, self.recv, self.local = send, recv, local
+        self.swap_send, self.swap_recv = swap_send, swap_recv
         self.R, self.N = shard.shape
         self.s, self.c = lax.axis_index("seq"), lax.axis_index("ctx")
-        self.core = lax.rem(self.c, 2)
-        self.cols = span(self.core * (self.N // 2), self.N // 2)
+        self.cols = span(lax.rem(self.c, 2) * (self.N // 2), self.N // 2)
         self.orders = bit_orders(S)
+        self.steps = len(self.orders[0])
         self.half = self.R // 2
 
     def block(self, owner, p):
         return self.full.at[span(owner * self.R + p * self.half, self.half, 16), self.cols]
 
-    def own(self, p):
-        return self.shard.at[pl.ds(p * self.half, self.half), self.cols]
-
     def copy_own(self):
         return pltpu.make_async_copy(
-            self.shard.at[:, self.cols],
-            self.full.at[span(self.s * self.R, self.R, 16), self.cols],
-            self.local,
+            self.shard, self.full.at[span(self.s * self.R, self.R, 16), :], self.local
         )
 
-    def copies(self, t):
+    def copies(self, t, direct):
         out = []
         for p in range(2):
             order = self.orders[p]
-            peer = jnp.bitwise_xor(self.s, order[t])
             for i, mask in enumerate(subsets(order[:t])):
-                owner = jnp.bitwise_xor(self.s, mask)
-                src = self.own(p) if mask == 0 else self.block(owner, p)
-                k = (1 << t) - 1 + i
-                out.append(
-                    remote(src, self.block(owner, p), self.send.at[p, k], self.recv.at[p, k], seq=peer)
-                )
+                if (mask == 0) == direct:
+                    owner = jnp.bitwise_xor(self.s, mask)
+                    src = self.block(owner, p)
+                    if mask == 0:
+                        src = self.shard.at[pl.ds(p * self.half, self.half), self.cols]
+                    k = (1 << t) - 1 + i
+                    peer = jnp.bitwise_xor(self.s, order[t])
+                    out.append(remote(src, self.block(owner, p), self.send.at[p, k], self.recv.at[p, k], seq=peer))
         return out
 
-    def swap(self):
-        k = self.S - 1
-        half = self.full.at[:, self.cols]
-        other = jnp.bitwise_xor(self.c, 1)
-        return remote(half, half, self.send.at[0, k], self.recv.at[0, k], ctx=other)
-
-    def start(self, t):
-        if t == 0:
-            self.copy_own().start()
-        for copy in self.copies(t):
+    def swaps(self, t, direct):
+        out = []
+        for p in range(2):
+            order = self.orders[p]
+            for i, mask in enumerate(subsets(order[:t])):
+                if (mask == 0) == direct:
+                    got = self.block(jnp.bitwise_xor(self.s, order[t] ^ mask), p)
+                    k = (1 << t) - 1 + i
+                    out.append(
+                        remote(
+                            got, got, self.swap_send.at[p, k], self.swap_recv.at[p, k], ctx=jnp.bitwise_xor(self.c, 1)
+                        )
+                    )
+        return out
+
+    def start(self):
+        for t in range(self.steps):
+            for copy in self.copies(t, True):
+                copy.start()
+        self.copy_own().start()
+
+    def pass_on(self, t):
+        for copy in self.copies(t, False):
             copy.start()
 
-    def finish(self, t):
-        for copy in self.copies(t):
+    def arrive(self, t, direct):
+        for copy in self.copies(t, direct):
             copy.wait_recv()
-
-    def start_swap(self):
-        self.copy_own().wait()
-        self.swap().start()
-
-    def finish_swap(self):
-        self.swap().wait_recv()
+        for copy in self.swaps(t, direct):
+            copy.start()
+
+    def first(self):
+        self.arrive(0, True)
+        self.pass_on(1)
+
+    def middle(self):
+        for t in range(1, self.steps):
+            self.arrive(t, True)
+            if t + 1 < self.steps:
+                self.arrive(t, False)
+                self.pass_on(t + 1)
+
+    def last(self):
+        self.arrive(self.steps - 1, False)
+
+    def ready(self, early, late):
+        if early:
+            self.copy_own().wait()
+        for t in range(self.steps):
+            for direct in (True, False):
+                final = t == self.steps - 1 and not direct
+                if late if final else early:
+                    for copy in self.swaps(t, direct):
+                        copy.wait_recv()
 
     def drain(self):
-        for t in range(len(self.orders[0])):
-            for copy in self.copies(t):
-                copy.wait_send()
-        self.swap().wait_send()
+        for t in range(self.steps):
+            for direct in (True, False):
+                for copy in self.copies(t, direct) + self.swaps(t, direct):
+                    copy.wait_send()
 
 
 class Regroup:
@@ -286,7 +315,7 @@
     n1_o, f1_o, flow_o, act_o, dgel_o, gsec_o, gb_o, out_o, smg_o, sm_o,
     xs, ct, wq, wo, wi, wu, small_all, segc, segk, q, qt, kown, vown, kc, vc, bias, m_s, l_s, ctxt, ctx,
     first, n1, f1, flow, h, act, dgel, n2, gsec, gb, outv,
-    ag_send, ag_recv, ag_local, rg_send, rg_recv, rg_local, sm_send, sm_recv,
+    ag_send, ag_recv, sw_send, sw_recv, ag_local, rg_send, rg_recv, rg_local, sm_send, sm_recv,
     kv_send, kv_recv, kv_local, kc_sem, out_sem,
 ):
     S, C, G, PP = dims
@@ -298,33 +327,16 @@
     m = lax.rem(c, M)
 
     gathers = [
-        Gather(S, shard, full, ag_send.at[w], ag_recv.at[w], ag_local.at[w])
+        Gather(S, shard, full, *[a.at[w] for a in (ag_send, ag_recv, sw_send, sw_recv, ag_local)])
         for w, (shard, full) in enumerate(((wq_s, wq), (wo_s, wo), (wi_s, wi), (wu_s, wu)))
     ]
-    full_out = [wq_o, wo_o, wi_o, wu_o]
-    steps = S.bit_length() - 1
-    events = [(w, t) for w in range(4) for t in range(steps)]
+    gq, go, gi, gu = gathers
     pending = []
 
     def put(src, dst):
         copy = pltpu.make_async_copy(src, dst, out_sem.at[len(pending)])
         copy.start()
         pending.append(copy)
-
-    def tick(w, t):
-        gathers[w].finish(t)
-        k = events.index((w, t))
-        if t + 1 < steps:
-            gathers[w].start(t + 1)
-        else:
-            gathers[w].start_swap()
-        for ahead in (k + 1, k + 2):
-            if ahead < len(events) and events[ahead][1] == 0 and (ahead == k + 2 or steps == 1):
-                gathers[events[ahead][0]].start(0)
-
-    def ready(w):
-        gathers[w].finish_swap()
-        put(gathers[w].full, full_out[w])
 
     enter(S, C)
     hid_move = Regroup(hid, xs, rg_send.at[0], rg_recv.at[0], rg_local.at[0], C, G)
@@ -332,15 +344,13 @@
     seg_move = Regroup(seg, segc, rg_send.at[2], rg_recv.at[2], rg_local.at[2], C, G)
     seg_move.start()
     hid_move.start()
-    gathers[0].start(0)
+    gq.start()
     small_copies = [
         remote(small, small_all.at[d - 1], sm_send.at[d - 1], sm_recv.at[d - 1], seq=jnp.bitwise_xor(s, d))
         for d in range(1, S)
     ]
     for copy in small_copies:
         copy.start()
-    for t in range(steps):
-        tick(0, t)
     seg_move.finish()
 
     group = lax.div(c, M) * M
@@ -372,11 +382,17 @@
     for d in range(1, S):
         total = total + small_all[d - 1].astype(f32)
     sm_o[...] = total
+    mask_bias(segc, segc, bias, G, PP)
+    gq.first()
+    go.start()
+    gi.start()
+    gq.middle()
+    gq.last()
     hid_move.finish()
     cot_move.start()
     put(xs, xs_o)
-    mask_bias(segc, segc, bias, G, PP)
-    ready(0)
+    gq.ready(True, True)
+    put(wq, wq_o)
 
     def project(i):
         cols = tile(i, T)
@@ -405,8 +421,9 @@
         copy.start()
     put(q, q_o)
     put(qt, qt_o)
-    for t in range(steps):
-        tick(1, t)
+    go.first()
+    gi.first()
+    gu.start()
 
     row_of = lax.broadcasted_iota(jnp.int32, (128, L), 0)
 
@@ -438,7 +455,8 @@
     def in_own(hp):
         @pl.when(hp == NP - 2)
         def _():
-            tick(2, 0)
+            go.middle()
+            go.last()
 
     attend(kown, vown, True, in_own)
 
@@ -473,7 +491,10 @@
     put(ctxt, ctxt_o)
     put(ctx, ctx_o)
     put(l_s, lse_o)
-    ready(1)
+    gi.middle()
+    gi.last()
+    go.ready(True, True)
+    put(wo, wo_o)
 
     def project_out(i):
         cols = tile(i, T)
@@ -494,10 +515,9 @@
     put(n1, n1_o)
     put(f1, f1_o)
     put(flow, flow_o)
-    for t in range(1, steps):
-        tick(2, t)
-    tick(3, 0)
-    ready(2)
+    gu.first()
+    gi.ready(True, True)
+    put(wi, wi_o)
 
     def feed_in(i):
         cols = tile(i, D)
@@ -517,15 +537,27 @@
     loop(FF // D, feed_in)
     put(act, act_o)
     put(dgel, dgel_o)
-    for t in range(1, steps):
-        tick(3, t)
-    ready(3)
-
-    def feed_out(i):
-        cols = tile(i, T)
-        n2[:, cols] = dotf(act[...], wu[:, cols]) + sm_o[UB : UB + 1, cols]
-
-    loop(D // T, feed_out)
+    RU = FF // S
+
+    def feed_out(masks, fresh):
+        owners = [jnp.bitwise_xor(s, k) for k in masks]
+
+        def step(i):
+            cols = tile(i, T)
+            total = sm_o[UB : UB + 1, cols] if fresh else n2[:, cols]
+            for owner in owners:
+                total = total + dotf(act[:, span(owner * RU, RU)], wu[span(owner * RU, RU), cols])
+            n2[:, cols] = total
+
+        loop(D // T, step)
+
+    gu.middle()
+    gu.ready(True, False)
+    feed_out([k for k in range(S) if k & (k - 1) == 0], True)
+    gu.last()
+    gu.ready(False, True)
+    put(wu, wu_o)
+    feed_out([k for k in range(S) if k & (k - 1)], False)
     cot_move.finish()
     smg_o[...] = jnp.zeros(smg_o.shape, f32)
 
@@ -583,7 +615,7 @@
     ]
     dma = pltpu.SemaphoreType.DMA
     sems = [
-        dma((4, 2, S)), dma((4, 2, S)), dma((4,)), dma((3, G)), dma((3, G)), dma((3,)),
+        dma((4, 2, S)), dma((4, 2, S)), dma((4, 2, S)), dma((4, 2, S)), dma((4,)), dma((3, G)), dma((3, G)), dma((3,)),
         dma((S - 1,)), dma((S - 1,)), dma((3, M)), dma((3, M)), dma((3,)), dma((3,)), dma((24,)),
     ]
     return pl.pallas_call(
@@ -623,43 +655,59 @@
     loop(rows // unit, step)
 
 
+class CoreSwap:
+    def __init__(self, part, far, rows, send, recv):
+        self.part, self.far, self.rows, self.send, self.recv = part, far, rows, send, recv
+        self.c = lax.axis_index("ctx")
+        self.core = lax.rem(self.c, 2)
+        self.count = part.shape[1] // rows
+
+    def copy(self, i):
+        rows = tile(i, self.rows)
+        return remote(
+            self.part.at[1 - self.core, rows, :], self.far.at[rows, :], self.send.at[i], self.recv.at[i],
+            ctx=jnp.bitwise_xor(self.c, 1),
+        )
+
+    def start(self, i):
+        self.copy(i).start()
+
+    def add(self):
+        loop(self.count, lambda i: self.copy(i).wait_recv())
+        add_rows(self.part.at[self.core], self.far)
+
+    def drain(self):
+        loop(self.count, lambda i: self.copy(i).wait_send())
+
+
 class Reduce:
-    def __init__(self, S, C, part, far, rx, zl, zr, sems, places):
-        self.S, self.K, self.part, self.far, self.rx, self.zl, self.zr = S, C // 2, part, far, rx, zl, zr
+    def __init__(self, S, C, part, stride, offset, R, cols, rx, zl, zr, sems, places):
+        self.S, self.K, self.part, self.rx, self.zl, self.zr = S, C // 2, part, rx, zl, zr
         self.c_send, self.c_recv, self.x_send, self.x_recv, self.z_send, self.z_recv, self.l_send = sems
-        self.places = places
-        self.R = part.shape[1] // S
-        self.half = self.R // 2
+        self.places, self.stride, self.offset, self.R, self.cols = places, stride, offset, R, cols
+        self.half = R // 2
         self.s, self.c = lax.axis_index("seq"), lax.axis_index("ctx")
         self.core = lax.rem(self.c, 2)
         self.k = lax.div(self.c, 2)
-        self.root = self.K // 2
+        self.left, self.right = self.K // 2 - 1, self.K // 2
         self.orders = bit_orders(S)
         self.steps = len(self.orders[0])
-        self.levels = max(self.root, self.K - 1 - self.root)
-        self.mine = part.at[self.core]
+
+    def rows(self, owner, start, count):
+        return self.part.at[self.core, span(owner * self.stride + self.offset + start, count, 16), self.cols]
 
     def block(self, owner, p):
-        return self.part.at[self.core, span(owner * self.R + p * self.half, self.half, 16), :]
-
-    def result(self, core):
-        return self.part.at[core, span(self.s * self.R, self.R, 16), :]
-
-    def core_copy(self):
-        other = 1 - self.core
-        return remote(
-            self.part.at[other], self.far, self.c_send.at[0], self.c_recv.at[0], ctx=jnp.bitwise_xor(self.c, 1)
-        )
-
-    def core_start(self):
-        self.core_copy().start()
+        return self.rows(owner, p * self.half, self.half)
+
+    def result(self):
+        return self.rows(self.s, 0, self.R)
 
     def copies(self, t):
         out, base = [], self.S - (1 << (self.steps - t))
         for p in range(2):
             order = self.orders[p]
             peer = jnp.bitwise_xor(self.s, order[t])
-            for i, mask in enumerate(subsets(order[t + 1 :])):
+            for i, mask in reversed(list(enumerate(subsets(order[t + 1 :])))):
                 copy = remote(
                     self.block(jnp.bitwise_xor(peer, mask), p),
                     self.rx.at[p, base + i],
@@ -671,85 +719,66 @@
         return out
 
     def cross_start(self, t):
-        if t == 0:
-            self.core_copy().wait_recv()
-            add_rows(self.mine, self.far)
-        else:
-            self.cross_add(t - 1)
+        if t > 0:
+            self.cross_add(t - 1, False)
         for copy, _, _, _ in self.copies(t):
             copy.start()
 
-    def cross_add(self, t):
+    def cross_add(self, t, last):
         for copy, p, slot, mask in self.copies(t):
-            copy.wait_recv()
-            add_rows(self.block(jnp.bitwise_xor(self.s, mask), p), self.rx.at[p, slot])
-
-    def up(self, side):
-        src = self.result(self.core)
-        if side == 0:
-            return remote(src, self.zl, self.z_send.at[0], self.z_recv.at[0], ctx=self.c + 2)
-        return remote(src, self.zr, self.z_send.at[0], self.z_recv.at[1], ctx=self.c - 2)
-
-    def take(self, side):
-        self.up(side).wait_recv()
-        add_rows(self.result(self.core), self.zl if side == 0 else self.zr)
-
-    def down(self, side, src):
-        target = self.c - 2 if side == 0 else self.c + 2
-        dst = self.zr if side == 0 else self.zl
-        return remote(src, dst, self.z_send.at[1 + side], self.z_recv.at[2], ctx=target)
-
-    def chain_up(self, level):
+            if (mask == 0) == last:
+                copy.wait_recv()
+                add_rows(self.block(jnp.bitwise_xor(self.s, mask), p), self.rx.at[p, slot])
+
+    def from_left(self):
+        return remote(self.result(), self.zl, self.z_send.at[0], self.z_recv.at[0], ctx=self.c + 2)
+
+    def from_right(self):
+        return remote(self.result(), self.zr, self.z_send.at[0], self.z_recv.at[1], ctx=self.c - 2)
+
+    def out_left(self):
+        return remote(self.zr, self.zr, self.z_send.at[1], self.z_recv.at[1], ctx=self.c - 2)
+
+    def out_right(self):
+        return remote(self.zl, self.zl, self.z_send.at[1], self.z_recv.at[0], ctx=self.c + 2)
+
+    def inward(self, level):
         if level == 0:
-            self.cross_add(self.steps - 1)
-        if level < self.root:
-
-            @pl.when(self.k == level)
-            def _():
-                if level > 0:
-                    self.take(0)
-                self.up(0).start()
-
-        if level < self.K - 1 - self.root:
-
-            @pl.when(self.k == self.K - 1 - level)
-            def _():
-                if level > 0:
-                    self.take(1)
-                self.up(1).start()
-
-    def chain_root(self):
-        @pl.when(self.k == self.root)
+            for t in range(self.steps):
+                self.cross_add(t, True)
+
+        @pl.when(self.k == level)
         def _():
-            if self.root > 0:
-                self.take(0)
-            if self.root < self.K - 1:
-                self.take(1)
-            src = self.result(self.core)
-            if self.root > 0:
-                self.down(0, src).start()
-            if self.root < self.K - 1:
-                self.down(1, src).start()
-            self.deliver(src)
-
-    def chain_down(self, distance):
-        if self.root - distance >= 0:
-
-            @pl.when(self.k == self.root - distance)
-            def _():
-                self.down(0, self.zr).wait_recv()
-                if self.root - distance > 0:
-                    self.down(0, self.zr).start()
-                self.deliver(self.zr)
-
-        if self.root + distance < self.K:
-
-            @pl.when(self.k == self.root + distance)
-            def _():
-                self.down(1, self.zl).wait_recv()
-                if self.root + distance < self.K - 1:
-                    self.down(1, self.zl).start()
-                self.deliver(self.zl)
+            if level > 0:
+                self.from_left().wait_recv()
+                add_rows(self.result(), self.zl)
+            self.from_left().start()
+
+        @pl.when(self.k == self.K - 1 - level)
+        def _():
+            if level > 0:
+                self.from_right().wait_recv()
+                add_rows(self.result(), self.zr)
+            self.from_right().start()
+
+    def outward(self, distance):
+        @pl.when(self.k == self.left - distance)
+        def _():
+            self.from_right().wait_recv()
+            if distance == 0:
+                add_rows(self.zr, self.result())
+            if distance < self.left:
+                self.out_left().start()
+            self.deliver(self.zr)
+
+        @pl.when(self.k == self.right + distance)
+        def _():
+            self.from_left().wait_recv()
+            if distance == 0:
+                add_rows(self.zl, self.result())
+            if distance < self.left:
+                self.out_right().start()
+            self.deliver(self.zl)
 
     def deliveries(self, src):
         out = []
@@ -759,7 +788,7 @@
                 (
                     pltpu.make_async_copy(src.at[:, cols], dst, self.l_send.at[i]),
                     remote(
-                        src.at[:, cols], dst, self.c_send.at[1 + i], self.c_recv.at[1 + i], ctx=jnp.bitwise_xor(self.c, 1)
+                        src.at[:, cols], dst, self.c_send.at[i], self.c_recv.at[i], ctx=jnp.bitwise_xor(self.c, 1)
                     ),
                 )
             )
@@ -777,32 +806,56 @@
 
     def stages(self):
         out = [functools.partial(self.cross_start, t) for t in range(self.steps)]
-        out += [functools.partial(self.chain_up, v) for v in range(self.levels)]
-        out += [self.chain_root]
-        out += [functools.partial(self.chain_down, d) for d in range(1, self.levels + 1)]
-        return out + [self.finish]
+        out += [functools.partial(self.inward, v) for v in range(self.left + 1)]
+        out += [functools.partial(self.outward, d) for d in range(self.left + 1)]
+        return out
 
     def drain(self):
-        self.core_copy().wait_send()
         for t in range(self.steps):
             for copy, _, _, _ in self.copies(t):
                 copy.wait_send()
-        last = self.K - 1
-
-        @pl.when(self.k != self.root)
+
+        @pl.when(self.k <= self.left)
         def _():
-            self.up(0).wait_send()
-
-        @pl.when(jnp.logical_and(self.k <= self.root, self.k > 0))
+            self.from_left().wait_send()
+
+        @pl.when(self.k >= self.right)
         def _():
-            self.down(0, self.zr).wait_send()
-
-        @pl.when(jnp.logical_and(self.k >= self.root, self.k < last))
+            self.from_right().wait_send()
+
+        @pl.when(jnp.logical_and(self.k <= self.left, self.k > 0))
         def _():
-            self.down(1, self.zl).wait_send()
+            self.out_left().wait_send()
+
+        @pl.when(jnp.logical_and(self.k >= self.right, self.k < self.K - 1))
+        def _():
+            self.out_right().wait_send()
 
         for _, far in self.deliveries(self.zl):
             far.wait_send()
+
+
+SCHEDULE = {
+    "ffn0": (('u0', 1), ('u1', 1), ('u2', 1)),
+    "ffn2": (('u0', 2), ('i0', 1), ('i1', 1)),
+    "ffn3": (('u1', 2), ('i2', 1)),
+    "first": (('u2', 2), ('i3', 1)),
+    "norm": (('u0', 3),),
+    "context": (('i0', 2), ('o', 1)),
+    "pair0": (('u0', 4), ('u1', 3), ('i1', 2), ('i2', 2)),
+    "pair1": (('u2', 3),),
+    "project0": (('u0', 5), ('u1', 4), ('i3', 2)),
+    "input0": (('i0', 3), ('q0', 1), ('o', 2)),
+    "pair2": (('u2', 4), ('u0', 6), ('i1', 3), ('u1', 5), ('i2', 3), ('i0', 4)),
+    "pair3": (('i3', 3), ('q0', 2)),
+    "project1": (('u1', 6), ('u2', 5), ('i1', 4), ('o', 3)),
+    "input1": (('i0', 5), ('i2', 4), ('q0', 3), ('q1', 1)),
+    "pair4": (('u2', 6), ('i1', 5), ('i3', 4), ('o', 4), ('q1', 2)),
+    "pair5": (('i0', 6), ('i2', 5), ('q0', 4), ('q1', 3)),
+    "project2": (('i1', 6), ('i3', 5)),
+    "input2": (('o', 5), ('q2', 1), ('s', 1)),
+    "end": (('i2', 6), ('q1', 4), ('q0', 5), ('i3', 6), ('q2', 2), ('s', 2), ('q2', 3), ('s', 3), ('q2', 4), ('s', 4), ('o', 6), ('q1', 5), ('q0', 6), ('q2', 5), ('s', 5), ('q1', 6), ('q2', 6), ('s', 6)),
+}
 
 
 def backward_kernel(
@@ -810,9 +863,9 @@
     outv, gsec_i, gb_i, act_i, dgel_i, wu_i, wi_i, wo_i, wq_i, flow_i, n1_i, f1_i, xs_i, ctx_i, ctxt_i,
     q_i, qt_i, k_i, v_i, seg_i, lse_i, smg_i, sm,
     out_o, gin_o, gq_o, go_o, gi_o, gu_o, land_o, small_o,
-    pu, pi, po, pq, ps, fu, fi, fo, fq, fs, ru, ri, ro, rq, rs, zlu, zli, zlo, zlq, zls, zru, zri, zro, zrq, zrs,
+    pu, pi, po, pq, ps, fu, fi, fo, fq, fs, rxu, rxi, rxs, zlu, zli, zls, zru, zri, zrs,
     gsec, gb, grad_o, grad_ot, delta, smg,
-    c_send, c_recv, x_send, x_recv, z_send, z_recv, rg_send, rg_recv, rg_local, in_sem, kv_sem, dkv_send, dkv_recv,
+    cs_send, cs_recv, c_send, c_recv, x_send, x_recv, z_send, z_recv, rg_send, rg_recv, rg_local, in_sem, kv_sem, dkv_send, dkv_recv,
     land_sem, l_send,
 ):
     S, C, G, PP = dims
@@ -824,47 +877,65 @@
     m, core = lax.rem(c, M), lax.rem(c, 2)
     group = lax.div(c, M) * M
 
-    def piece(n, places, *refs):
+    H = D // 2
+    R, RU = D // S, FF // S
+    cut = RU // 3
+    items = {}
+
+    def piece(name, places, *refs):
+        n = len(items)
         sems = [a.at[n] for a in (c_send, c_recv, x_send, x_recv, z_send, z_recv, l_send)]
-        return Reduce(S, C, *refs, sems, places)
-
-    H = D // 2
-    sum_u = piece(0, [(pl.ds(0, H), lambda e: gu_o.at[:, span(e * H, H)])], pu, fu, ru, zlu, zru)
-    sum_i = [
+        items[name] = Reduce(S, C, *refs, sems, places)
+
+    for i in range(3):
         piece(
-            1 + i, [(pl.ds(0, D), lambda e, i=i: gi_o.at[:, span(e * (FF // 2) + i * D, D)])],
-            pi.at[i], fi.at[i], ri.at[i], zli.at[i], zri.at[i],
+            f"u{i}", [(pl.ds(0, H), lambda e, i=i: gu_o.at[pl.ds(i * cut, cut), span(e * H, H)])],
+            pu, RU, i * cut, cut, pl.ds(0, H), rxu.at[i], zlu.at[i], zru.at[i],
         )
-        for i in range(2)
-    ]
-    sum_o = piece(3, [(pl.ds(0, H), lambda e: go_o.at[:, span(e * H, H)])], po, fo, ro, zlo, zro)
-    sum_q = [
-        piece(
-            4 + i,
+
+    def narrow_piece(name, places, part, cols):
+        n = len(items) - 3
+        piece(name, places, part, R, 0, R, cols, rxi.at[n], zli.at[n], zri.at[n])
+
+    for i in range(2):
+        for j in range(2):
+            narrow_piece(
+                f"i{2 * i + j}",
+                [(pl.ds(0, H), lambda e, i=i, j=j: gi_o.at[:, span(e * (FF // 2) + i * D + j * H, H)])],
+                pi.at[i], pl.ds(j * H, H),
+            )
+    narrow_piece("o", [(pl.ds(0, H), lambda e: go_o.at[:, span(e * H, H)])], po, pl.ds(0, H))
+    for i in range(3):
+        narrow_piece(
+            f"q{i}",
             [
                 (pl.ds(a * 128, 128), lambda e, i=i, a=a: gq_o.at[:, span(a * D + (2 * i + e) * 128, 128)])
                 for a in range(3)
             ],
-            pq.at[i], fq.at[i], rq.at[i], zlq.at[i], zrq.at[i],
+            pq.at[i], pl.ds(0, H),
         )
-        for i in range(3)
-    ]
-    sum_s = piece(7, [(pl.ds(0, ps.shape[2]), lambda e: small_o.at[e])], ps, fs, rs, zls, zrs)
-
-    def stages_of(item):
-        return item.stages()
-
-    steps = S.bit_length() - 1
-    ticks = {
-        "u": stages_of(sum_u), "i0": stages_of(sum_i[0]), "i1": stages_of(sum_i[1]), "o": stages_of(sum_o),
-        "q0": stages_of(sum_q[0]), "q1": stages_of(sum_q[1]), "q2": stages_of(sum_q[2]), "s": stages_of(sum_s),
-    }
-    at = {name: 0 for name in ticks}
+    SR, SW = ps.shape[1] // S, ps.shape[2]
+    piece(
+        "s", [(pl.ds(0, SW), lambda e: small_o.at[e])], ps, SR, 0, SR, pl.ds(0, SW), rxs, zls, zrs
+    )
+    swap_u = CoreSwap(pu, fu, 512, cs_send.at[0], cs_recv.at[0])
+    swap_i = [CoreSwap(pi.at[i], fi.at[i], T, cs_send.at[1 + i], cs_recv.at[1 + i]) for i in range(2)]
+    swap_o = CoreSwap(po, fo, T, cs_send.at[3], cs_recv.at[3])
+    swap_q = [CoreSwap(pq.at[i], fq.at[i], T, cs_send.at[4 + i], cs_recv.at[4 + i]) for i in range(3)]
+    swap_s = CoreSwap(ps, fs, ps.shape[1], cs_send.at[7], cs_recv.at[7])
+
+    ticks = {name: item.stages() for name, item in items.items()}
+    at = {name: 0 for name in items}
+    last = len(ticks["s"])
 
     def tick(name, until):
-        while at[name] < min(until, len(ticks[name])):
+        while at[name] < min(until, last):
             ticks[name][at[name]]()
             at[name] += 1
+
+    def point(name):
+        for chunk, until in SCHEDULE.get(name, ()):
+            tick(chunk, until)
 
     enter(S, C)
     out_move = Ungroup(outv, out_o, rg_send.at[0], rg_recv.at[0], rg_local.at[0], C, G)
@@ -889,13 +960,13 @@
             block = dotg(act[:, rows], gb[...], 0, 0).astype(bf16)
             for e in range(2):
                 pu[e, rows, :] = block[:, e * (D // 2) : (e + 1) * (D // 2)]
+            swap_u.start(i)
 
         loop(FF // 512, outer_grad)
-        sum_u.core_start()
         for copy in loads[2:5]:
             copy.wait()
 
-        def inner_grad(i, half):
+        def inner_grad(i, half, send):
             where = half * (FF // 2) + i * D
             cols = span(where, D)
             h[...] = dotg(gb[...], wu[span(where, D), :], 1, 1)
@@ -912,17 +983,22 @@
             def grad(k):
                 rows = tile(k, T)
                 pi[i, half, rows, :] = dotg(flow[:, rows], act[:, cols], 0, 0).astype(bf16)
+                if send:
+                    swap_i[i].start(k)
 
             loop(D // T, grad)
 
-        inner_grad(0, 1 - core)
-        inner_grad(0, core)
-        sum_i[0].core_start()
-        tick("u", 1)
-        inner_grad(1, 1 - core)
-        inner_grad(1, core)
-        sum_i[1].core_start()
-        tick("i0", 1)
+        inner_grad(0, 1 - core, True)
+        swap_u.add()
+        point("ffn0")
+        inner_grad(0, core, False)
+        point("ffn1")
+        inner_grad(1, 1 - core, True)
+        swap_i[0].add()
+        point("ffn2")
+        inner_grad(1, core, False)
+        swap_i[1].add()
+        point("ffn3")
         loads[5].wait()
         loads[6].wait()
 
@@ -931,7 +1007,7 @@
             gsec[:, cols] += dotg(act[...], wi[cols, :], 1, 1)
 
         loop(D // T, first_grad)
-        tick("i1", 1)
+        point("first")
         loads[7].wait()
         loads[8].wait()
 
@@ -953,7 +1029,7 @@
         feed_forward, V((L, FF), bf16), V((L, FF), bf16), V((FF, D), bf16), V((D, FF), bf16), V((L, D), f32),
         V((L, D), f32), V((L, 1), f32), V((L, D), bf16),
     )
-    tick("u", steps)
+    point("norm")
 
     def context_back(wo, ctx, ctxt):
         loads = [
@@ -969,9 +1045,9 @@
             block = dotg(ctx[:, rows], gb[...], 0, 0).astype(bf16)
             for e in range(2):
                 po[e, rows, :] = block[:, e * (D // 2) : (e + 1) * (D // 2)]
+            swap_o.start(k)
 
         loop(D // T, out_grad)
-        sum_o.core_start()
         loads[1].wait()
         loads[2].wait()
 
@@ -990,6 +1066,8 @@
         loop(D // T, back)
 
     pl.run_scoped(context_back, V((D, D), bf16), V((L, D), bf16), V((NP, 128, L), f32))
+    swap_o.add()
+    point("context")
 
     def attention(wq, xs, q, qt, kb, vb, bias, lse, own_k, own_v, stage, land, segs, grads, dqt, turned_q):
         loads = [
@@ -1102,6 +1180,7 @@
                 for a in range(3):
                     for e in range(2):
                         pq[i, e, rows, a * 128 : (a + 1) * 128] = block[:, a * T + e * 128 : a * T + (e + 1) * 128]
+                swap_q[i].start(k)
 
             loop(D // T, weight)
 
@@ -1121,48 +1200,36 @@
                     send_back(hp, d).wait_send()
 
         def pair_group(i):
-            loop(2, lambda u: pair(2 * i + u))
+            def body(u):
+                pair(2 * i + u)
+                for k in range(2):
+
+                    @pl.when(u == k)
+                    def _():
+                        point(f"pair{2 * i + k}")
+
+            loop(2, body)
 
         pair_group(0)
-        tick("o", 1)
-        tick("i0", steps)
         fetch(0)
-        tick("i1", steps)
-        tick("u", steps + 1)
         loads[4].wait()
         loads[5].wait()
         project_back(0)
-        sum_q[0].core_start()
+        point("project0")
         input_back(0)
-        tick("o", steps)
-        tick("i0", steps + 1)
-        tick("q0", 1)
+        swap_q[0].add()
+        point("input0")
         pair_group(1)
-        tick("u", steps + 2)
-        tick("i1", steps + 1)
-        tick("o", steps + 1)
         fetch(1)
-        tick("i0", steps + 2)
-        tick("q0", steps)
         project_back(1)
-        sum_q[1].core_start()
+        point("project1")
         input_back(1)
-        tick("i1", steps + 2)
-        tick("o", steps + 2)
-        tick("u", steps + 3)
-        tick("q1", 1)
+        swap_q[1].add()
+        point("input1")
         pair_group(2)
-        for name in ("i0", "i1", "o"):
-            tick(name, steps + 3)
-        tick("q0", steps + 1)
-        tick("u", steps + 4)
         fetch(2)
-        tick("q1", steps)
-        tick("q0", steps + 2)
         project_back(2)
-        sum_q[2].core_start()
-
-        W = ps.shape[2]
+
         width = D // S
         ps[...] = jnp.zeros(ps.shape, bf16)
         share = FF // S
@@ -1173,21 +1240,20 @@
                 start = owner * share + r * width
                 a, b = start // D, start % D
                 ps[0, base + 16 + r : base + 17 + r, 0:width] = smg[IB + a : IB + a + 1, b : b + width].astype(bf16)
-        sum_s.core_start()
+        swap_s.start(0)
+        point("project2")
         input_back(2)
-        tick("q2", 1)
-        tick("s", 1)
         for r in range(L // PP):
             rows = pl.ds(r * PP, PP)
             grads[rows, :] = gsec[rows, :].astype(bf16)
         gin_move = Ungroup(grads, gin_o, rg_send.at[1], rg_recv.at[1], rg_local.at[1], C, G)
         gin_move.start()
-        order = ("u", "i0", "i1", "o", "q0", "q1", "q2", "s")
-        for stage_no in range(2, len(ticks["u"])):
-            for name in ("q2", "s", "q1", "q0", "o", "i1", "i0", "u"):
-                tick(name, stage_no)
-        for name in order:
-            tick(name, len(ticks[name]))
+        swap_q[2].add()
+        swap_s.add()
+        point("input2")
+        point("end")
+        for name in items:
+            tick(name, last)
         gin_move.finish()
         gin_move.drain()
         drain_stage()
@@ -1201,8 +1267,11 @@
     )
     out_move.finish()
     out_move.drain()
-    for item in [sum_u] + sum_i + [sum_o] + sum_q + [sum_s]:
+    for item in items.values():
+        item.finish()
         item.drain()
+    for swap in [swap_u] + swap_i + [swap_o] + swap_q + [swap_s]:
+        swap.drain()
 
 
 def backward_call(S, C, G, PP, saved):
@@ -1217,22 +1286,23 @@
         ((G, PP, D), bf16), ((G, PP, D), bf16), ((R, 3 * D), bf16), ((R, D), bf16), ((R, FF), bf16), ((RU, D), bf16),
         ((NP, land, 2, L, 128), bf16), ((2, SR, SW), bf16),
     ]
+    cut = RU // 3
     scratch = [
         (2, FF, H), (2, 2, D, D), (2, D, H), (3, 2, D, H), (2, S * SR, SW),
         (FF, H), (2, D, D), (D, H), (3, D, H), (S * SR, SW),
-        (2, S - 1, RU // 2, H), (2, 2, S - 1, R // 2, D), (2, S - 1, R // 2, H), (3, 2, S - 1, R // 2, H),
-        (2, S - 1, SR // 2, SW),
-        (RU, H), (2, R, D), (R, H), (3, R, H), (SR, SW),
-        (RU, H), (2, R, D), (R, H), (3, R, H), (SR, SW),
+        (3, 2, S - 1, cut // 2, H), (8, 2, S - 1, R // 2, H), (2, S - 1, SR // 2, SW),
+        (3, cut, H), (8, R, H), (SR, SW),
+        (3, cut, H), (8, R, H), (SR, SW),
     ]
     scratch = [(x, bf16) for x in scratch] + [
         ((L, D), f32), ((L, D), bf16), ((NP, L, 128), bf16), ((NP, 128, L), bf16), ((NP, 2, L), f32), ((16, D), f32),
     ]
     dma = pltpu.SemaphoreType.DMA
     sems = [
-        dma((8, 4)), dma((8, 4)), dma((8, 2, S - 1)), dma((8, 2, S - 1)), dma((8, 3)), dma((8, 3)),
+        dma((8, 8)), dma((8, 8)), dma((12, 3)), dma((12, 3)), dma((12, 2, S - 1)), dma((12, 2, S - 1)), dma((12, 2)),
+        dma((12, 2)),
         dma((2, G)), dma((2, G)), dma((2,)), dma((10,)), dma((2, 2)), dma((2, land)), dma((NP, land)), dma((1,)),
-        dma((8, 3)),
+        dma((12, 3)),
     ]
     results = pl.pallas_call(
         functools.partial(backward_kernel, (S, C, G, PP)),

time: 269 us -> 213 us (0.79)
  Pallas kernels: 247 us -> 191 us
    pallas_call x1, Pallas kernels: 159 us -> 111 us  [backward_call(): pl.pallas_call(functools.partial(backward_kernel, (S, C, G, PP)), out_sha...]
    pallas_call x1, Pallas kernels: 88 us -> 80.3 us  [forward_call(): pl.pallas_call(functools.partial(forward_kernel, (S, C, G, PP)), out_shap...]
where the time goes in v2:
time: 213 us; the launch traced here: 212 us
  Pallas kernels  191 us (90%)
  other arithmetic  10.4 us (5%)
  local copies, waits for them, and re-layouts  9.9 us (5%)
    pallas_call x1, Pallas kernels, backward_call(): pl.pallas_call(functools.partial(backward_kernel, (S, C, G, PP)), out_sha...  111 us
    pallas_call x1, Pallas kernels, forward_call(): pl.pallas_call(functools.partial(forward_kernel, (S, C, G, PP)), out_shap...  80.3 us
    another operation x16, local copies, waits for them, and re-layouts, pack_small(): rows = [jnp.where(owner == s, jnp.tile(v, S)[None, :], 0) for v in vectors]  5.98 us

profile of v2, /device:TPU:0, one launch (start us, length us, event | category | flops | bytes accessed | tf_op | source)
XLA Modules:
  0.0 212.1 jit_solution(5824749198580636420)
XLA Ops:
  0.6 0.7 tile.18
  1.3 0.1 broadcast_in_dim_tile.25
  1.4 0.7 tile.19
  2.1 0.1 broadcast_in_dim_tile.26
  2.2 0.7 tile.20
  2.9 0.7 tile.21
  3.7 0.7 tile.22
  4.4 0.7 tile.23
  5.2 0.7 tile.24
  5.9 0.7 tile.25
  6.7 0.7 fusion.2
  7.4 1.3 concatenate.3.small
  8.7 80.3 %forward.1 = (bf16[512,768]{1,0:T(8,128)(2,1)}, bf16[768,2304]{1,0:T(8,128)(2,1)}, bf16[768,768]{1,0:T(8,128)(2,1)}, bf16[768,3072]{1,0:T(8,128)(2,1)}, bf16[307...) custom-call(bf16[4,128,768]{2,1,0:T(8,128)(2,1)} %hid.1, ...), custom_call_target="tpu_custom_call" | custom-call | tf_op jit(solution)/shard_map/forward/pallas_call | solution.py:621
  89.1 110.8 %backward.1 = (bf16[4,128,768]{2,1,0:T(8,128)(2,1)}, bf16[4,128,768]{2,1,0:T(8,128)(2,1)}, bf16[192,2304]{1,0:T(8,128)(2,1)}, bf16[192,768]{1,0:T(8,128)(2,1)}, ...) custom-call(bf16[512,768]{1,0:T(8,128)(2,1)} %get-tuple-element.45.o, ...), custom_call_target="tpu_custom_call" | custom-call | tf_op jit(solution)/shard_map/backward/pallas_call | solution.py:1307
  199.9 0.7 bitcast_convert_fusion
  200.6 0.6 fusion.4
  201.2 0.7 reshape.211
  201.9 1.9 convert_element_type.36
  203.8 2.4 %convert_element_type.32 = f32[4,128,768]{2,1,0:T(8,128)} convert(bf16[4,128,768]{2,1,0:T(8,128)(2,1)} %get-tuple-element.69) | non-fusion elementwise | flops 393216 | bytes 2359296 | tf_op jit(solution)/shard_map/convert_element_type | solution.py:1336
  206.2 1.3 convert_element_type.33
  207.5 0.5 copy-done.1
  208.0 1.7 convert_element_type.37
  209.7 1.6 convert_element_type.38
  211.2 0.9 copy.32
  (19 shorter events, 0.6 us)
Async XLA Ops:
  201.9 4.3 %copy-start.2 = (bf16[192,2304]{1,0:T(8,128)(2,1)S(1)}, bf16[192,2304]{1,0:T(8,128)(2,1)}, u32[]{:S(2)}) copy-start(bf16[192,2304]{1,0:T(8,128)(2,1)} %get-tuple-element.70) | copy-start | bytes 2654212
  206.2 1.8 copy-start.1
  208.0 1.7 copy-start
  209.7 1.6 copy-start.3

commit v3 on v2

--- a/solution.py
+++ b/solution.py
@@ -233,9 +233,9 @@
         self.G, self.M, self.P = G, C // G, dst.shape[1]
         self.c = lax.axis_index("ctx")
 
-    def each(self, on_remote, on_local):
+    def each(self, on_remote, on_local, only=None):
         g, m = lax.div(self.c, self.M), lax.rem(self.c, self.M)
-        for j in range(self.G):
+        for j in range(self.G) if only is None else (only,):
             target = m * self.G + j
             rows = self.src.at[pl.ds(j * self.P, self.P), :]
             far = remote(rows, self.dst.at[g], self.send.at[j], self.recv.at[g], ctx=target)
@@ -249,8 +249,8 @@
             def _():
                 on_local(near)
 
-    def start(self):
-        self.each(lambda far: far.start(), lambda near: near.start())
+    def start(self, only=None):
+        self.each(lambda far: far.start(), lambda near: near.start(), only)
 
     def drain(self):
         self.each(lambda far: far.wait_send(), lambda near: None)
@@ -310,13 +310,13 @@
 
 def forward_kernel(
     dims,
-    hid, cot, seg, wq_s, wo_s, wi_s, wu_s, small,
-    xs_o, wq_o, wo_o, wi_o, wu_o, k_o, v_o, q_o, qt_o, seg_o, lse_o, ctxt_o, ctx_o,
+    hid, cot, seg, wq_s, wo_s, wi_s, wu_s, qb, vb, ob, fg, fs, ub, sg, ss, ib,
+    xs_o, wq_o, wo_o, wi_o, wu_o, k_o, v_o, q_o, seg_o, p_o, fac_o, ctxt_o, ctx_o,
     n1_o, f1_o, flow_o, act_o, dgel_o, gsec_o, gb_o, out_o, smg_o, sm_o,
-    xs, ct, wq, wo, wi, wu, small_all, segc, segk, q, qt, kown, vown, kc, vc, bias, m_s, l_s, ctxt, ctx,
+    xs, ct, wq, wo, wi, wu, small_all, segc, segk, q, qt, kown, vown, kc, vc, bias, pst, m_s, l_s, ctxt, ctx,
     first, n1, f1, flow, h, act, dgel, n2, gsec, gb, outv,
     ag_send, ag_recv, sw_send, sw_recv, ag_local, rg_send, rg_recv, rg_local, sm_send, sm_recv,
-    kv_send, kv_recv, kv_local, kc_sem, out_sem,
+    kv_send, kv_recv, kv_local, kc_sem, p_sem, out_sem,
 ):
     S, C, G, PP = dims
     M, L, D = C // G, G * PP, hid.shape[2]
@@ -345,8 +345,15 @@
     seg_move.start()
     hid_move.start()
     gq.start()
+    width, share = D // S, FF // S
+    small = small_all.at[s]
+    small[...] = jnp.zeros(small.shape, bf16)
+    for r, vector in enumerate((qb, vb, ob, fg, fs, ub, sg, ss)):
+        small[r : r + 1, 0:width] = vector[...].reshape(1, width)
+    for r in range(share // width):
+        small[IB + r : IB + r + 1, 0:width] = ib[r * width : (r + 1) * width].reshape(1, width)
     small_copies = [
-        remote(small, small_all.at[d - 1], sm_send.at[d - 1], sm_recv.at[d - 1], seq=jnp.bitwise_xor(s, d))
+        remote(small, small, sm_send.at[d - 1], sm_recv.at[s], seq=jnp.bitwise_xor(s, d))
         for d in range(1, S)
     ]
     for copy in small_copies:
@@ -376,12 +383,17 @@
     for d in range(1, M):
         kv_copies(d)[2].start()
 
-    total = small[...].astype(f32)
-    for copy in small_copies:
-        copy.wait_recv()
     for d in range(1, S):
-        total = total + small_all[d - 1].astype(f32)
-    sm_o[...] = total
+        far = jnp.bitwise_xor(s, d)
+        remote(small, small_all.at[far], sm_send.at[d - 1], sm_recv.at[far], seq=far).wait_recv()
+    sm_o[...] = jnp.zeros(sm_o.shape, f32)
+    for owner in range(S):
+        block = small_all[owner].astype(f32)
+        sm_o[0:IB, owner * width : (owner + 1) * width] = block[0:IB, 0:width]
+        for r in range(share // width):
+            start = owner * share + r * width
+            a, b = start // D, start % D
+            sm_o[IB + a : IB + a + 1, b : b + width] = block[IB + r : IB + r + 1, 0:width]
     mask_bias(segc, segc, bias, G, PP)
     gq.first()
     go.start()
@@ -420,16 +432,30 @@
     for copy in own_kv:
         copy.start()
     put(q, q_o)
-    put(qt, qt_o)
     go.first()
     gi.first()
     gu.start()
 
     row_of = lax.broadcasted_iota(jnp.int32, (128, L), 0)
 
-    def attend(keys, values, fresh, extra):
+    def keep_probs(hp, d):
+        slot = lax.rem(hp, 2)
+        return pltpu.make_async_copy(pst.at[slot], p_o.at[hp, d], p_sem.at[slot])
+
+    def attend(keys, values, d, extra):
+        fresh = isinstance(d, int)
+
         def pair(hp):
             extra(hp)
+            slot = lax.rem(hp, 2)
+            if fresh:
+
+                @pl.when(hp >= 2)
+                def _():
+                    keep_probs(hp, d).wait()
+
+            else:
+                keep_probs(hp, d).wait()
             qv, kv, vt, b = qt[hp], keys[hp], values[hp].T, bias[...]
             for e in range(2):
                 head = slice(e * HEAD_DIM, (e + 1) * HEAD_DIM)
@@ -438,17 +464,21 @@
                 top = jnp.max(scores, axis=0, keepdims=True)
                 if fresh:
                     weights = jnp.exp(scores - top)
-                    m_s[hp, e : e + 1, :] = top
+                    low = weights.astype(bf16)
+                    m_s[d, hp, e : e + 1, :] = top
                     l_s[hp, e : e + 1, :] = colsum(weights)
-                    ctxt[hp, head, :] = dotf(vt[head], weights.astype(bf16))
+                    ctxt[hp, head, :] = dotf(vt[head], low)
                 else:
-                    old = m_s[hp, e : e + 1, :]
+                    old = m_s[d - 1, hp, e : e + 1, :]
                     top = jnp.maximum(old, top)
                     keep = jnp.exp(old - top)
                     weights = jnp.exp(scores - top)
-                    m_s[hp, e : e + 1, :] = top
+                    low = weights.astype(bf16)
+                    m_s[d, hp, e : e + 1, :] = top
                     l_s[hp, e : e + 1, :] = l_s[hp, e : e + 1, :] * keep + colsum(weights)
-                    ctxt[hp, head, :] = ctxt[hp, head, :] * keep + dotf(vt[head], weights.astype(bf16))
+                    ctxt[hp, head, :] = ctxt[hp, head, :] * keep + dotf(vt[head], low)
+                pst[slot, e] = low
+            keep_probs(hp, d).start()
 
         loop(NP, pair)
 
@@ -458,7 +488,7 @@
             go.middle()
             go.last()
 
-    attend(kown, vown, True, in_own)
+    attend(kown, vown, 0, in_own)
 
     def far_chunk(d, carry):
         j = lax.rem(m + d, M)
@@ -474,7 +504,7 @@
         for copy in loads:
             copy.wait()
         mask_bias(segk, segc, bias, G, PP)
-        attend(kc, vc, False, lambda hp: None)
+        attend(kc, vc, d, lambda hp: None)
         return carry
 
     lax.fori_loop(1, M, far_chunk, 0)
@@ -482,15 +512,16 @@
     def close(hp):
         for e in range(2):
             head = slice(e * HEAD_DIM, (e + 1) * HEAD_DIM)
-            ctxt[hp, head, :] = ctxt[hp, head, :] / l_s[hp, e : e + 1, :]
-            l_s[hp, e : e + 1, :] = m_s[hp, e : e + 1, :] + jnp.log(l_s[hp, e : e + 1, :])
+            share = 1.0 / l_s[hp, e : e + 1, :]
+            ctxt[hp, head, :] = ctxt[hp, head, :] * share
+            for d in range(M):
+                fac_o[d, hp, e : e + 1, :] = jnp.exp(m_s[d, hp, e : e + 1, :] - m_s[M - 1, hp, e : e + 1, :]) * share
         ctx[:, tile(hp, 128)] = ctxt[hp].T.astype(bf16)
 
     loop(NP, close)
 
     put(ctxt, ctxt_o)
     put(ctx, ctx_o)
-    put(l_s, lse_o)
     gi.middle()
     gi.last()
     go.ready(True, True)
@@ -580,6 +611,8 @@
     put(gsec, gsec_o)
     put(gb, gb_o)
 
+    for u in range(2):
+        keep_probs(NP - 2 + u, 0).wait()
     for gather in gathers:
         gather.drain()
     for move in (hid_move, cot_move, seg_move):
@@ -593,22 +626,22 @@
         copy.wait()
 
 
-def forward_call(S, C, hid, cot, seg, wq_s, wo_s, wi_s, wu_s, small):
+def forward_call(S, C, hid, cot, seg, wq_s, wo_s, wi_s, wu_s, vectors):
     G, PP, D = hid.shape
     L, M, NP, FF = G * PP, C // G, D // 128, wi_s.shape[1]
     sds = jax.ShapeDtypeStruct
     outs = [
         ((L, D), bf16), ((D, 3 * D), bf16), ((D, D), bf16), ((D, FF), bf16), ((FF, D), bf16),
-        ((M, NP, L, 128), bf16), ((M, NP, L, 128), bf16), ((NP, L, 128), bf16), ((NP, 128, L), bf16),
-        ((M, G, 1, PP), jnp.int32), ((NP, 2, L), f32), ((NP, 128, L), f32), ((L, D), bf16),
+        ((M, NP, L, 128), bf16), ((M, NP, L, 128), bf16), ((NP, L, 128), bf16),
+        ((M, G, 1, PP), jnp.int32), ((NP, M, 2, L, L), bf16), None, ((NP, 128, L), f32), ((L, D), bf16),
         ((L, D), f32), ((L, 1), f32), ((L, D), bf16), ((L, FF), bf16), ((L, FF), bf16),
         ((L, D), f32), ((L, D), bf16), ((L, D), bf16),
     ]
     scratch = [
         ((L, D), bf16), ((L, D), bf16), ((D, 3 * D), bf16), ((D, D), bf16), ((D, FF), bf16), ((FF, D), bf16),
-        ((S - 1, 16, D), bf16), ((G, 1, PP), jnp.int32), ((G, 1, PP), jnp.int32),
+        ((S, 16, D // S + -(D // S) % 128), bf16), ((G, 1, PP), jnp.int32), ((G, 1, PP), jnp.int32),
         ((NP, L, 128), bf16), ((NP, 128, L), bf16), ((NP, L, 128), bf16), ((NP, L, 128), bf16),
-        ((NP, L, 128), bf16), ((NP, L, 128), bf16), ((L, L), f32), ((NP, 2, L), f32), ((NP, 2, L), f32),
+        ((NP, L, 128), bf16), ((NP, L, 128), bf16), ((L, L), f32), ((2, 2, L, L), bf16), ((M, NP, 2, L), f32), ((NP, 2, L), f32),
         ((NP, 128, L), f32), ((L, D), bf16),
         ((L, D), f32), ((L, D), f32), ((L, 1), f32), ((L, D), bf16), ((L, D), f32), ((L, FF), bf16),
         ((L, FF), bf16), ((L, D), f32), ((L, D), f32), ((L, D), bf16), ((L, D), bf16),
@@ -616,32 +649,64 @@
     dma = pltpu.SemaphoreType.DMA
     sems = [
         dma((4, 2, S)), dma((4, 2, S)), dma((4, 2, S)), dma((4, 2, S)), dma((4,)), dma((3, G)), dma((3, G)), dma((3,)),
-        dma((S - 1,)), dma((S - 1,)), dma((3, M)), dma((3, M)), dma((3,)), dma((3,)), dma((24,)),
+        dma((S,)), dma((S,)), dma((3, M)), dma((3, M)), dma((3,)), dma((3,)), dma((2,)), dma((24,)),
     ]
     return pl.pallas_call(
         functools.partial(forward_kernel, (S, C, G, PP)),
-        out_shape=[sds(*o) for o in outs] + [sds((16, D), f32), sds((16, D), f32)],
-        in_specs=[ANY] * 7 + [VMEM],
-        out_specs=[ANY] * len(outs) + [VMEM, VMEM],
+        out_shape=[sds(*(o or ((M, NP, 2, L), f32))) for o in outs] + [sds((16, D), f32), sds((16, D), f32)],
+        in_specs=[ANY] * 7 + [VMEM] * len(vectors),
+        out_specs=[ANY if o else VMEM for o in outs] + [VMEM, VMEM],
         scratch_shapes=[pltpu.VMEM(*x) for x in scratch] + sems,
         compiler_params=pltpu.CompilerParams(
             collective_id=0, has_side_effects=True, vmem_limit_bytes=62 << 20
         ),
         name="forward",
-    )(hid, cot, seg, wq_s, wo_s, wi_s, wu_s, small)
-
-
-def pack_small(S, vectors, inner_bias, D):
-    s = lax.axis_index("seq")
-    width = D // S
-    owner = lax.broadcasted_iota(jnp.int32, (1, D), 1) // width
-    rows = [jnp.where(owner == s, jnp.tile(v, S)[None, :], 0) for v in vectors]
-    share = inner_bias.shape[0]
-    flat = jnp.tile(inner_bias, S)
-    where = lax.broadcasted_iota(jnp.int32, (1, share * S), 1) // share
-    full = jnp.where(where == s, flat[None, :], 0).reshape(share * S // D, D)
-    used = len(vectors) + share * S // D
-    return jnp.concatenate(rows + [full, jnp.zeros((16 - used, D), bf16)], axis=0).astype(bf16)
+    )(hid, cot, seg, wq_s, wo_s, wi_s, wu_s, *vectors)
+
+
+def widen_kernel(count, *refs):
+    srcs, dsts = refs[: count + 1], refs[count + 1 : 2 * count + 2]
+    lows, highs = refs[2 * count + 2 : 3 * count + 2], refs[3 * count + 2 : 4 * count + 2]
+    plain, in_sem, out_sem = refs[4 * count + 2 :]
+    loads, stores = [], []
+    for i in range(count):
+        loads.append(pltpu.make_async_copy(srcs[i], lows[i], in_sem.at[i]))
+        stores.append(pltpu.make_async_copy(highs[i], dsts[i], out_sem.at[i]))
+    loads.append(pltpu.make_async_copy(srcs[count], plain, in_sem.at[count]))
+    stores.append(pltpu.make_async_copy(plain, dsts[count], out_sem.at[count]))
+    for copy in loads:
+        copy.start()
+    for i in range(count):
+        loads[i].wait()
+        rows = lows[i].shape[0]
+        unit = next(u for u in (64, 48, 32, 16) if rows % u == 0)
+
+        def step(r, low=lows[i], high=highs[i], unit=unit):
+            at = tile(r, unit)
+            high[at, :] = low[at, :].astype(f32)
+
+        loop(rows // unit, step)
+        stores[i].start()
+    loads[count].wait()
+    stores[count].start()
+    for copy in stores:
+        copy.wait()
+
+
+def widen(arrays, plain):
+    count = len(arrays)
+    sds = jax.ShapeDtypeStruct
+    return pl.pallas_call(
+        functools.partial(widen_kernel, count),
+        out_shape=[sds(a.shape, f32) for a in arrays] + [sds(plain.shape, plain.dtype)],
+        in_specs=[ANY] * (count + 1),
+        out_specs=[ANY] * (count + 1),
+        scratch_shapes=[pltpu.VMEM(a.shape, bf16) for a in arrays]
+        + [pltpu.VMEM(a.shape, f32) for a in arrays]
+        + [pltpu.VMEM(plain.shape, plain.dtype), pltpu.SemaphoreType.DMA((count + 1,)), pltpu.SemaphoreType.DMA((count + 1,))],
+        compiler_params=pltpu.CompilerParams(vmem_limit_bytes=62 << 20),
+        name="widen",
+    )(*arrays, plain)
 
 
 def add_rows(dst, src):
@@ -650,7 +715,7 @@
 
     def step(r):
         at = tile(r, unit)
-        dst[at, :] = (dst[at, :].astype(f32) + src[at, :].astype(f32)).astype(bf16)
+        dst[at, :] = dst[at, :] + src[at, :]
 
     loop(rows // unit, step)
 
@@ -805,10 +870,19 @@
             far.wait_recv()
 
     def stages(self):
-        out = [functools.partial(self.cross_start, t) for t in range(self.steps)]
-        out += [functools.partial(self.inward, v) for v in range(self.left + 1)]
-        out += [functools.partial(self.outward, d) for d in range(self.left + 1)]
-        return out
+        def each(step, *which):
+            for w in which:
+                step(w)
+
+        run = functools.partial
+        return [
+            run(each, self.cross_start, 0),
+            run(each, self.cross_start, *range(1, self.steps)),
+            run(each, self.inward, 0),
+            run(each, self.inward, *range(1, self.left + 1)),
+            run(each, self.outward, 0),
+            run(each, self.outward, *range(1, self.left + 1)),
+        ]
 
     def drain(self):
         for t in range(self.steps):
@@ -835,37 +909,150 @@
             far.wait_send()
 
 
+class DirectReduce:
+    def __init__(self, S, C, part, far, rx, zx, done, sems, places):
+        self.S, self.K, self.part, self.far, self.rx, self.zx, self.done = S, C // 2, part, far, rx, zx, done
+        self.h_send, self.h_recv, self.x_send, self.x_recv, self.z_send, self.z_recv, self.c_send, self.c_recv, self.l_send = sems
+        self.places = places
+        self.s, self.c = lax.axis_index("seq"), lax.axis_index("ctx")
+        self.core = lax.rem(self.c, 2)
+        self.k = lax.div(self.c, 2)
+
+    def other(self):
+        return jnp.bitwise_xor(self.c, 1)
+
+    def halves(self):
+        return remote(
+            self.part.at[:, 1 - self.core], self.far, self.h_send.at[0], self.h_recv.at[0], ctx=self.other()
+        )
+
+    def start(self):
+        self.halves().start()
+
+    def crossing(self):
+        out = []
+        for d in range(self.S - 1, 0, -1):
+            peer = jnp.bitwise_xor(self.s, d)
+            out.append(
+                remote(
+                    self.part.at[peer, self.core], self.rx.at[d - 1], self.x_send.at[d - 1], self.x_recv.at[d - 1],
+                    seq=peer,
+                )
+            )
+        return out
+
+    def cross_start(self):
+        self.halves().wait_recv()
+        for owner in range(self.S):
+            add_rows(self.part.at[owner, self.core], self.far.at[owner])
+        for copy in self.crossing():
+            copy.start()
+
+    def along(self, d):
+        chip = lax.rem(self.k + d, self.K)
+        return remote(
+            self.part.at[self.s, self.core], self.zx.at[self.k], self.z_send.at[d - 1], self.z_recv.at[self.k],
+            ctx=2 * chip + self.core,
+        )
+
+    def arrival(self, d):
+        chip = lax.rem(self.k + d, self.K)
+        return remote(
+            self.part.at[self.s, self.core], self.zx.at[chip], self.z_send.at[d - 1], self.z_recv.at[chip],
+            ctx=2 * chip + self.core,
+        )
+
+    def along_start(self):
+        mine = self.part.at[self.s, self.core]
+        for copy in self.crossing():
+            copy.wait_recv()
+        total = mine[...].astype(f32)
+        for d in range(1, self.S):
+            total = total + self.rx[d - 1].astype(f32)
+        total = total.astype(bf16)
+        mine[...] = total
+        self.zx[self.k] = total
+        for d in range(self.K - 1, 0, -1):
+            self.along(d).start()
+
+    def outputs(self):
+        out = []
+        for i, (cols, place) in enumerate(self.places):
+            dst = place(self.core)
+            src = self.done.at[:, cols]
+            out.append(
+                (
+                    pltpu.make_async_copy(src, dst, self.l_send.at[i]),
+                    remote(src, dst, self.c_send.at[i], self.c_recv.at[i], ctx=self.other()),
+                )
+            )
+        return out
+
+    def deliver(self):
+        for d in range(1, self.K):
+            self.arrival(d).wait_recv()
+        total = self.zx[0].astype(f32)
+        for j in range(1, self.K):
+            total = total + self.zx[j].astype(f32)
+        self.done[...] = total.astype(bf16)
+        for near, far in self.outputs():
+            near.start()
+            far.start()
+
+    def stages(self):
+        return [self.cross_start, self.along_start, self.deliver]
+
+    def finish(self):
+        for near, far in self.outputs():
+            near.wait()
+            far.wait_recv()
+
+    def drain(self):
+        self.halves().wait_send()
+        for copy in self.crossing():
+            copy.wait_send()
+        for d in range(1, self.K):
+            self.along(d).wait_send()
+        for _, far in self.outputs():
+            far.wait_send()
+
+
 SCHEDULE = {
-    "ffn0": (('u0', 1), ('u1', 1), ('u2', 1)),
-    "ffn2": (('u0', 2), ('i0', 1), ('i1', 1)),
-    "ffn3": (('u1', 2), ('i2', 1)),
-    "first": (('u2', 2), ('i3', 1)),
+    "ffn0": (('u0', 1),),
+    "ffn1": (('u1', 1),),
+    "ffn2": (('u0', 2),),
+    "ffn3": (('u2', 1), ('u1', 2)),
+    "first": (('i0', 1),),
     "norm": (('u0', 3),),
-    "context": (('i0', 2), ('o', 1)),
-    "pair0": (('u0', 4), ('u1', 3), ('i1', 2), ('i2', 2)),
+    "context": (('u2', 2),),
+    "pair0": (('u0', 4), ('u1', 3), ('i0', 2), ('i1', 1), ('i2', 1)),
     "pair1": (('u2', 3),),
-    "project0": (('u0', 5), ('u1', 4), ('i3', 2)),
-    "input0": (('i0', 3), ('q0', 1), ('o', 2)),
-    "pair2": (('u2', 4), ('u0', 6), ('i1', 3), ('u1', 5), ('i2', 3), ('i0', 4)),
-    "pair3": (('i3', 3), ('q0', 2)),
-    "project1": (('u1', 6), ('u2', 5), ('i1', 4), ('o', 3)),
-    "input1": (('i0', 5), ('i2', 4), ('q0', 3), ('q1', 1)),
-    "pair4": (('u2', 6), ('i1', 5), ('i3', 4), ('o', 4), ('q1', 2)),
-    "pair5": (('i0', 6), ('i2', 5), ('q0', 4), ('q1', 3)),
-    "project2": (('i1', 6), ('i3', 5)),
-    "input2": (('o', 5), ('q2', 1), ('s', 1)),
-    "end": (('i2', 6), ('q1', 4), ('q0', 5), ('i3', 6), ('q2', 2), ('s', 2), ('q2', 3), ('s', 3), ('q2', 4), ('s', 4), ('o', 6), ('q1', 5), ('q0', 6), ('q2', 5), ('s', 5), ('q1', 6), ('q2', 6), ('s', 6)),
+    "project0": (('i0', 3), ('i3', 1), ('i1', 2)),
+    "input0": (('u1', 4), ('u0', 5)),
+    "far2": (('i2', 2),),
+    "pair2": (('u2', 4),),
+    "far3": (('i3', 2),),
+    "pair3": (('i0', 4), ('i1', 3), ('u0', 6), ('u1', 5), ('o', 1)),
+    "project1": (('i2', 3), ('q0', 1)),
+    "input1": (('i3', 3), ('u2', 5)),
+    "far4": (('o', 2),),
+    "pair4": (('i1', 4), ('u1', 6), ('q0', 2), ('i0', 5), ('q1', 1)),
+    "far5": (('i2', 4),),
+    "pair5": (('o', 3), ('i3', 4), ('u2', 6), ('q0', 3)),
+    "project2": (('q1', 2), ('i1', 5)),
+    "input2": (('i0', 6), ('q2', 1)),
+    "end": (('i2', 5), ('s', 1), ('g0', 1), ('o', 4), ('q1', 3), ('i3', 5), ('q2', 2), ('i1', 6), ('q0', 4), ('s', 2), ('i2', 6), ('q2', 3), ('o', 5), ('q1', 4), ('i3', 6), ('q0', 5), ('s', 3), ('q2', 4), ('o', 6), ('q1', 5), ('g1', 1), ('q0', 6), ('q2', 5), ('g2', 1), ('q1', 6), ('g3', 1), ('q2', 6)),
 }
 
 
 def backward_kernel(
     dims,
     outv, gsec_i, gb_i, act_i, dgel_i, wu_i, wi_i, wo_i, wq_i, flow_i, n1_i, f1_i, xs_i, ctx_i, ctxt_i,
-    q_i, qt_i, k_i, v_i, seg_i, lse_i, smg_i, sm,
+    q_i, k_i, v_i, p_i, fac, smg_i, sm,
     out_o, gin_o, gq_o, go_o, gi_o, gu_o, land_o, small_o,
-    pu, pi, po, pq, ps, fu, fi, fo, fq, fs, rxu, rxi, rxs, zlu, zli, zls, zru, zri, zrs,
+    pu, pi, po, pq, ps, fu, fi, fo, fq, fs, rxu, rxi, rxs, zlu, zli, zru, zri, zxs, dns,
     gsec, gb, grad_o, grad_ot, delta, smg,
-    cs_send, cs_recv, c_send, c_recv, x_send, x_recv, z_send, z_recv, rg_send, rg_recv, rg_local, in_sem, kv_sem, dkv_send, dkv_recv,
+    cs_send, cs_recv, h_send, h_recv, dx_send, dx_recv, dz_send, dz_recv, c_send, c_recv, x_send, x_recv, z_send, z_recv, rg_send, rg_recv, rg_local, in_sem, wq_sem, kv_sem, p_sem, dkv_send, dkv_recv,
     land_sem, l_send,
 ):
     S, C, G, PP = dims
@@ -914,28 +1101,25 @@
             ],
             pq.at[i], pl.ds(0, H),
         )
-    SR, SW = ps.shape[1] // S, ps.shape[2]
-    piece(
-        "s", [(pl.ds(0, SW), lambda e: small_o.at[e])], ps, SR, 0, SR, pl.ds(0, SW), rxs, zls, zrs
-    )
+    def direct_piece(name, n, places, *refs):
+        m_ = len(items)
+        sems = [a.at[n] for a in (h_send, h_recv, dx_send, dx_recv, dz_send, dz_recv)]
+        items[name] = DirectReduce(S, C, *refs, sems + [a.at[m_] for a in (c_send, c_recv, l_send)], places)
+
+    SW = ps.shape[3]
+    direct_piece("s", 0, [(pl.ds(0, SW), lambda e: small_o.at[e])], ps, fs, rxs, zxs, dns)
     swap_u = CoreSwap(pu, fu, 512, cs_send.at[0], cs_recv.at[0])
     swap_i = [CoreSwap(pi.at[i], fi.at[i], T, cs_send.at[1 + i], cs_recv.at[1 + i]) for i in range(2)]
     swap_o = CoreSwap(po, fo, T, cs_send.at[3], cs_recv.at[3])
     swap_q = [CoreSwap(pq.at[i], fq.at[i], T, cs_send.at[4 + i], cs_recv.at[4 + i]) for i in range(3)]
-    swap_s = CoreSwap(ps, fs, ps.shape[1], cs_send.at[7], cs_recv.at[7])
 
     ticks = {name: item.stages() for name, item in items.items()}
-    at = {name: 0 for name in items}
-    last = len(ticks["s"])
-
-    def tick(name, until):
-        while at[name] < min(until, last):
-            ticks[name][at[name]]()
-            at[name] += 1
+    ran = set()
 
     def point(name):
-        for chunk, until in SCHEDULE.get(name, ()):
-            tick(chunk, until)
+        for step in SCHEDULE.get(name, ()):
+            ran.add(step)
+            ticks[step[0]][step[1] - 1]()
 
     enter(S, C)
     out_move = Ungroup(outv, out_o, rg_send.at[0], rg_recv.at[0], rg_local.at[0], C, G)
@@ -1069,13 +1253,24 @@
     swap_o.add()
     point("context")
 
-    def attention(wq, xs, q, qt, kb, vb, bias, lse, own_k, own_v, stage, land, segs, grads, dqt, turned_q):
+    def attention(wq, xs, q, kb, vb, pb, own_k, own_v, stage, land, grads, dqt, turned_q):
         loads = [
             pltpu.make_async_copy(src, dst, in_sem.at[i])
             for i, (src, dst) in enumerate(
-                ((seg_i, segs), (q_i, q), (qt_i, qt), (lse_i, lse), (xs_i, xs), (wq_i, wq))
+                ((q_i, q), (xs_i, xs))
             )
         ]
+        groups = [(0, 2), (2, 2), (4, 2)]
+
+        def weight_cols(first, count):
+            return [
+                pltpu.make_async_copy(
+                    wq_i.at[:, pl.ds(a * D + first * 128, count * 128)],
+                    wq.at[:, pl.ds(3 * first * 128 + a * count * 128, count * 128)],
+                    wq_sem.at[first, a],
+                )
+                for a in range(3)
+            ]
 
         def kv_load(hp):
             slot = lax.rem(hp, 2)
@@ -1084,12 +1279,16 @@
                 for i, (src, dst) in enumerate(((k_i, kb), (v_i, vb)))
             ]
 
-        for copy in kv_load(0) + loads:
+        def p_load(t):
+            d = lax.rem(lax.rem(t, M) + 1, M)
+            return pltpu.make_async_copy(p_i.at[lax.div(t, M), d], pb.at[lax.rem(t, 2)], p_sem.at[lax.rem(t, 2)])
+
+        for copy in kv_load(0) + [p_load(0)] + loads:
             copy.start()
-        for copy in loads[:4]:
-            copy.wait()
-        for j in range(M):
-            mask_bias(segs.at[j], segs.at[m], bias.at[j], G, PP)
+        for first, count in groups:
+            for copy in weight_cols(first, count):
+                copy.start()
+        loads[0].wait()
         row_of = lax.broadcasted_iota(jnp.int32, (128, L), 0)
         lane_of = lax.broadcasted_iota(jnp.int32, (L, 128), 1)
 
@@ -1100,17 +1299,24 @@
                 ctx=group + lax.rem(m + d, M),
             )
 
-        def chunk(hp, slot, j):
-            key, value, b = kb[slot, j], vb[slot, j], bias[j].astype(f32)
+        def chunk(hp, slot, d):
+            j = lax.rem(m + d, M)
+            t = hp * M + lax.rem(d - 1 + M, M)
+            p_load(t).wait()
+
+            @pl.when(t + 1 < NP * M)
+            def _():
+                p_load(t + 1).start()
+
+            key, value = kb[slot, j], vb[slot, j]
             turned = key.T
-            query, query_t, up, up_t = q[hp], qt[hp], grad_o[hp], grad_ot[hp]
+            query, up, up_t = q[hp], grad_o[hp], grad_ot[hp]
             sums = []
             for e in range(2):
                 rows = (row_of < HEAD_DIM) if e == 0 else (row_of >= HEAD_DIM)
                 lanes = (lane_of < HEAD_DIM) if e == 0 else (lane_of >= HEAD_DIM)
-                zero, zero_t = jnp.zeros_like(query), jnp.zeros_like(query_t)
-                scores = dotf(key, jnp.where(rows, query_t, zero_t)) + b
-                probs = jnp.exp(scores - lse[hp, e : e + 1, :])
+                zero, zero_t = jnp.zeros_like(query), jnp.zeros_like(up_t)
+                probs = pb[lax.rem(t, 2), e].astype(f32) * fac[d, hp, e : e + 1, :]
                 dprobs = dotf(value, jnp.where(rows, up_t, zero_t))
                 dscores = (probs * (dprobs - delta[hp, e : e + 1, :])).astype(bf16)
                 sums.append(
@@ -1123,7 +1329,7 @@
                 dqt[head, :] += dotf(turned[head], dscores)
             return sums[0][0] + sums[1][0], sums[0][1] + sums[1][1]
 
-        def pair(hp):
+        def pair(hp, between):
             slot = lax.rem(hp, 2)
             for copy in kv_load(hp):
                 copy.wait()
@@ -1140,57 +1346,67 @@
                 def _():
                     send_back(hp - 2, d).wait_send()
 
-                dk, dv = chunk(hp, slot, lax.rem(m + d, M))
+                dk, dv = chunk(hp, slot, d)
                 stage[slot, d - 1, 0] = dk.astype(bf16)
                 stage[slot, d - 1, 1] = dv.astype(bf16)
                 send_back(hp, d).start()
                 return carry
 
             lax.fori_loop(1, M, far, 0)
-            dk, dv = chunk(hp, slot, m)
+            between()
+            dk, dv = chunk(hp, slot, 0)
             own_k[slot] = dk
             own_v[slot] = dv
             turned_q[slot] = (dqt[...] * HEAD_DIM**-0.5).T.astype(bf16)
 
-        def fetch(i):
-            for u in range(2):
+        def fetched(first, count):
+            return pltpu.make_async_copy(land_o.at[pl.ds(first, count)], land.at[pl.ds(0, count)], land_sem.at[0])
+
+        def fetch(first, count):
+            for u in range(count):
                 for d in range(1, M):
-                    send_back(2 * i + u, d).wait_recv()
+                    send_back(first + u, d).wait_recv()
             if M > 1:
-                pltpu.make_async_copy(land_o.at[pl.ds(2 * i, 2)], land, land_sem.at[0]).start()
-
-        def project_back(i):
+                fetched(first, count).start()
+
+        def project_back(first, count):
             if M > 1:
-                pltpu.make_async_copy(land_o.at[pl.ds(2 * i, 2)], land, land_sem.at[0]).wait()
-            for u in range(2):
-                dk, dv = own_k[u], own_v[u]
+                fetched(first, count).wait()
+            W = count * 128
+            for u in range(count):
+                slot = (first + u) % 2
+                dk, dv = own_k[slot], own_v[slot]
                 for d in range(1, M):
                     dk = dk + land[u, d - 1, 0].astype(f32)
                     dv = dv + land[u, d - 1, 1].astype(f32)
-                grads[:, u * 128 : (u + 1) * 128] = turned_q[u]
-                grads[:, T + u * 128 : T + (u + 1) * 128] = dk.astype(bf16)
-                grads[:, 2 * T + u * 128 : 2 * T + (u + 1) * 128] = dv.astype(bf16)
-            cols = tile(i, T)
-            smg[QB : QB + 1, cols] = colsum(grads[:, 0:T].astype(f32))
-            smg[VB : VB + 1, cols] = colsum(grads[:, 2 * T : 3 * T].astype(f32))
+                grads[:, u * 128 : (u + 1) * 128] = turned_q[slot]
+                grads[:, W + u * 128 : W + (u + 1) * 128] = dk.astype(bf16)
+                grads[:, 2 * W + u * 128 : 2 * W + (u + 1) * 128] = dv.astype(bf16)
+            cols = slice(first * 128, first * 128 + W)
+            smg[QB : QB + 1, cols] = colsum(grads[:, 0:W].astype(f32))
+            smg[VB : VB + 1, cols] = colsum(grads[:, 2 * W : 3 * W].astype(f32))
 
             def weight(k):
                 rows = tile(k, T)
                 block = dotg(xs[:, rows], grads[...], 0, 0).astype(bf16)
                 for a in range(3):
                     for e in range(2):
-                        pq[i, e, rows, a * 128 : (a + 1) * 128] = block[:, a * T + e * 128 : a * T + (e + 1) * 128]
-                swap_q[i].start(k)
+                        pq[first // 2, e, rows, a * 128 : (a + 1) * 128] = block[
+                            :, a * W + e * 128 : a * W + (e + 1) * 128
+                        ]
+                swap_q[first // 2].start(k)
 
             loop(D // T, weight)
 
-        def input_back(i):
+        def input_back(first, count):
+            for copy in weight_cols(first, count):
+                copy.wait()
+            W = 3 * count * 128
+            base = 3 * first * 128
+
             def back(k):
                 rows = tile(k, T)
-                total = gsec[:, rows]
-                for a in range(3):
-                    total = total + dotg(grads[:, a * T : (a + 1) * T], wq[rows, span(a * D + i * T, T)], 1, 1)
-                gsec[:, rows] = total
+                gsec[:, rows] += dotg(grads[:, 0:W], wq[rows, base : base + W], 1, 1)
 
             loop(D // T, back)
 
@@ -1199,70 +1415,65 @@
                 for d in range(1, M):
                     send_back(hp, d).wait_send()
 
-        def pair_group(i):
+        def pair_group(first, count):
             def body(u):
-                pair(2 * i + u)
-                for k in range(2):
-
-                    @pl.when(u == k)
-                    def _():
-                        point(f"pair{2 * i + k}")
-
-            loop(2, body)
-
-        pair_group(0)
-        fetch(0)
-        loads[4].wait()
-        loads[5].wait()
-        project_back(0)
-        point("project0")
-        input_back(0)
-        swap_q[0].add()
-        point("input0")
-        pair_group(1)
-        fetch(1)
-        project_back(1)
-        point("project1")
-        input_back(1)
-        swap_q[1].add()
-        point("input1")
-        pair_group(2)
-        fetch(2)
-        project_back(2)
+                def here(name):
+                    for k in range(count):
+
+                        @pl.when(u == k)
+                        def _():
+                            point(f"{name}{first + k}")
+
+                pair(first + u, lambda: here("far"))
+                here("pair")
+
+            loop(count, body)
+
+        for g, (first, count) in enumerate(groups[:2]):
+            pair_group(first, count)
+            fetch(first, count)
+            if g == 0:
+                loads[1].wait()
+            project_back(first, count)
+            point(f"project{g}")
+            input_back(first, count)
+            swap_q[g].add()
+            point(f"input{g}")
+        pair_group(*groups[2])
+        fetch(*groups[2])
+        project_back(*groups[2])
 
         width = D // S
         ps[...] = jnp.zeros(ps.shape, bf16)
         share = FF // S
         for owner in range(S):
-            base = owner * ps.shape[1] // S
-            ps[0, base : base + 8, 0:width] = smg[0:8, owner * width : (owner + 1) * width].astype(bf16)
+            ps[owner, 0, 0:8, 0:width] = smg[0:8, owner * width : (owner + 1) * width].astype(bf16)
             for r in range(share // width):
                 start = owner * share + r * width
                 a, b = start // D, start % D
-                ps[0, base + 16 + r : base + 17 + r, 0:width] = smg[IB + a : IB + a + 1, b : b + width].astype(bf16)
-        swap_s.start(0)
+                ps[owner, 1, r : r + 1, 0:width] = smg[IB + a : IB + a + 1, b : b + width].astype(bf16)
+        items["s"].start()
         point("project2")
-        input_back(2)
+        input_back(*groups[2])
         for r in range(L // PP):
             rows = pl.ds(r * PP, PP)
             grads[rows, :] = gsec[rows, :].astype(bf16)
+        swap_q[2].add()
         gin_move = Ungroup(grads, gin_o, rg_send.at[1], rg_recv.at[1], rg_local.at[1], C, G)
-        gin_move.start()
-        swap_q[2].add()
-        swap_s.add()
+        for j in range(G):
+            ticks[f"g{j}"] = [functools.partial(gin_move.start, j)]
         point("input2")
         point("end")
-        for name in items:
-            tick(name, last)
+        assert ran == {(name, i + 1) for name in ticks for i in range(len(ticks[name]))}
         gin_move.finish()
         gin_move.drain()
         drain_stage()
 
     pl.run_scoped(
-        attention, V((D, 3 * D), bf16), V((L, D), bf16), V((NP, L, 128), bf16), V((NP, 128, L), bf16),
-        V((2, M, L, 128), bf16), V((2, M, L, 128), bf16), V((M, L, L), f32 if M <= 2 else bf16), V((NP, 2, L), f32),
+        attention, V((D, 3 * D), bf16), V((L, D), bf16), V((NP, L, 128), bf16),
+        V((2, M, L, 128), bf16), V((2, M, L, 128), bf16), V((2, 2, L, L), bf16),
         V((2, L, 128), f32), V((2, L, 128), f32), V((2, max(M - 1, 1), 2, L, 128), bf16),
-        V((2, max(M - 1, 1), 2, L, 128), bf16), V((M, G, 1, PP), jnp.int32), V((L, 3 * T), bf16), V((128, L), f32),
+        V((2, max(M - 1, 1), 2, L, 128), bf16), V((L, 3 * T), bf16), V((128, L), f32),
         V((2, L, 128), bf16),
     )
     out_move.finish()
@@ -1270,12 +1481,12 @@
     for item in items.values():
         item.finish()
         item.drain()
-    for swap in [swap_u] + swap_i + [swap_o] + swap_q + [swap_s]:
+    for swap in [swap_u] + swap_i + [swap_o] + swap_q:
         swap.drain()
 
 
 def backward_call(S, C, G, PP, saved):
-    (xs, wq, wo, wi, wu, k, v, q, qt, seg, lse, ctxt, ctx, n1, f1, flow, act, dgel, gsec, gb, outv, smg, sm) = saved
+    (xs, wq, wo, wi, wu, k, v, q, _, p, fac, ctxt, ctx, n1, f1, flow, act, dgel, gsec, gb, outv, smg, sm) = saved
     L, D = xs.shape
     M, NP, FF = C // G, D // 128, wi.shape[1]
     R, RU = D // S, FF // S
@@ -1284,37 +1495,38 @@
     H, SR, SW = D // 2, 32, 256
     outs = [
         ((G, PP, D), bf16), ((G, PP, D), bf16), ((R, 3 * D), bf16), ((R, D), bf16), ((R, FF), bf16), ((RU, D), bf16),
-        ((NP, land, 2, L, 128), bf16), ((2, SR, SW), bf16),
+        ((NP, land, 2, L, 128), bf16), ((2, SR // 2, SW), bf16),
     ]
     cut = RU // 3
     scratch = [
-        (2, FF, H), (2, 2, D, D), (2, D, H), (3, 2, D, H), (2, S * SR, SW),
-        (FF, H), (2, D, D), (D, H), (3, D, H), (S * SR, SW),
-        (3, 2, S - 1, cut // 2, H), (8, 2, S - 1, R // 2, H), (2, S - 1, SR // 2, SW),
-        (3, cut, H), (8, R, H), (SR, SW),
-        (3, cut, H), (8, R, H), (SR, SW),
+        (2, FF, H), (2, 2, D, D), (2, D, H), (3, 2, D, H), (S, 2, SR // 2, SW),
+        (FF, H), (2, D, D), (D, H), (3, D, H), (S, SR // 2, SW),
+        (3, 2, S - 1, cut // 2, H), (8, 2, S - 1, R // 2, H), (S - 1, SR // 2, SW),
+        (3, cut, H), (8, R, H), (3, cut, H), (8, R, H),
+        (C // 2, SR // 2, SW), (SR // 2, SW),
     ]
     scratch = [(x, bf16) for x in scratch] + [
         ((L, D), f32), ((L, D), bf16), ((NP, L, 128), bf16), ((NP, 128, L), bf16), ((NP, 2, L), f32), ((16, D), f32),
     ]
     dma = pltpu.SemaphoreType.DMA
     sems = [
-        dma((8, 8)), dma((8, 8)), dma((12, 3)), dma((12, 3)), dma((12, 2, S - 1)), dma((12, 2, S - 1)), dma((12, 2)),
+        dma((8, 8)), dma((8, 8)), dma((1, 1)), dma((1, 1)), dma((1, S - 1)), dma((1, S - 1)), dma((1, C // 2)), dma((1, C // 2)),
+        dma((13, 3)), dma((13, 3)), dma((12, 2, S - 1)), dma((12, 2, S - 1)), dma((12, 2)),
         dma((12, 2)),
-        dma((2, G)), dma((2, G)), dma((2,)), dma((10,)), dma((2, 2)), dma((2, land)), dma((NP, land)), dma((1,)),
-        dma((12, 3)),
+        dma((2, G)), dma((2, G)), dma((2,)), dma((10,)), dma((NP, 3)), dma((2, 2)), dma((2,)), dma((2, land)), dma((NP, land)), dma((1,)),
+        dma((13, 3)),
     ]
     results = pl.pallas_call(
         functools.partial(backward_kernel, (S, C, G, PP)),
         out_shape=[sds(*o) for o in outs],
-        in_specs=[ANY] * 21 + [VMEM, VMEM],
+        in_specs=[ANY] * 19 + [VMEM] * 3,
         out_specs=[ANY] * len(outs),
         scratch_shapes=[pltpu.VMEM(*x) for x in scratch] + sems,
         compiler_params=pltpu.CompilerParams(
             collective_id=1, has_side_effects=True, vmem_limit_bytes=62 << 20
         ),
         name="backward",
-    )(outv, gsec, gb, act, dgel, wu, wi, wo, wq, flow, n1, f1, xs, ctx, ctxt, q, qt, k, v, seg, lse, smg, sm)
+    )(outv, gsec, gb, act, dgel, wu, wi, wo, wq, flow, n1, f1, xs, ctx, ctxt, q, k, v, p, fac, smg, sm)
     return results
 
 
@@ -1325,16 +1537,16 @@
         hid, cot, seg, wq, qb, vb, wo, ob, fg, fs, wi, ib, wu, ub, sg, ss
     ):
         G, PP, D = hid.shape
-        small = pack_small(S, [qb, vb, ob, fg, fs, ub, sg, ss], ib, D)
-        saved = forward_call(S, C, hid, cot, seg.reshape(G, 1, PP), wq, wo, wi, wu, small)
+        saved = forward_call(S, C, hid, cot, seg.reshape(G, 1, PP), wq, wo, wi, wu, [qb, vb, ob, fg, fs, ub, sg, ss, ib])
         out, gin, gq, go, gi, gu, _, gs = backward_call(S, C, G, PP, saved)
-        gs = gs[0].astype(f32)
+        gu, gi, gq, go, gin, out = widen([gu, gi, gq, go, gin.reshape(G * PP, D)], out.reshape(G * PP, D))
+        gs = gs.reshape(-1, gs.shape[-1]).astype(f32)
         width = D // S
         row = lambda r: gs[r, :width]
         grad_ib = gs[16 : 16 + ib.shape[0] // width, :width].reshape(-1)
         return (
-            out, gin.astype(f32), gq.astype(f32), row(QB), row(VB), go.astype(f32), row(OB), row(FG), row(FS),
-            gi.astype(f32), grad_ib, gu.astype(f32), row(UB), row(SG), row(SS),
+            out.reshape(G, PP, D), gin.reshape(G, PP, D), gq, row(QB), row(VB), go, row(OB), row(FG), row(FS), gi,
+            grad_ib, gu, row(UB), row(SG), row(SS),
         )
 
     rows, matrix, vector = P("seq", "ctx", None), P("seq", None), P("seq")

time: 213 us -> 196 us (0.920)
  other arithmetic: 10.4 us -> 0.72 us
  local copies, waits for them, and re-layouts: 9.9 us -> 1.27 us
    convert_element_type x6 -> x1, other arithmetic: 9.58 us -> 0.72 us  [on_device(): gs = gs.reshape(-1, gs.shape[-1]).astype(f32)]
    another operation x16 -> x0, local copies, waits for them, and re-layouts: 5.98 us -> none  [pack_small(): rows = [jnp.where(owner == s, jnp.tile(v, S)[None, :], 0) for v in vectors]]
    pallas_call x0 -> x1, Pallas kernels: none -> 5.19 us  [widen(): pl.pallas_call(functools.partial(widen_kernel, count), out_shape=[sds(a.s...]
    pallas_call x1, Pallas kernels: 111 us -> 107 us  [backward_call(): pl.pallas_call(functools.partial(backward_kernel, (S, C, G, PP)), out_sha...]
where the time goes in v3:
time: 196 us
  Pallas kernels  193 us (98%)
    pallas_call x1, Pallas kernels, backward_call(): pl.pallas_call(functools.partial(backward_kernel, (S, C, G, PP)), out_sha...  107 us
    pallas_call x1, Pallas kernels, forward_call(): pl.pallas_call(functools.partial(forward_kernel, (S, C, G, PP)), out_shap...  80.9 us
    pallas_call x1, Pallas kernels, widen(): pl.pallas_call(functools.partial(widen_kernel, count), out_shape=[sds(a.s...  5.19 us

profile of v3, /device:TPU:0, one launch (start us, length us, event | category | flops | bytes accessed | tf_op | source)
XLA Modules:
  0.0 195.8 jit_solution(12542693930587382472)
XLA Ops:
  0.7 80.9 %forward.1 = (bf16[512,768]{1,0:T(8,128)(2,1)}, bf16[768,2304]{1,0:T(8,128)(2,1)}, bf16[768,768]{1,0:T(8,128)(2,1)}, bf16[768,3072]{1,0:T(8,128)(2,1)}, bf16[307...) custom-call(bf16[4,128,768]{2,1,0:T(8,128)(2,1)} %hid.1, ...), custom_call_target="tpu_custom_call" | custom-call | tf_op jit(solution)/shard_map/forward/pallas_call | solution.py:654
  81.6 106.9 %backward.1 = (bf16[4,128,768]{2,1,0:T(8,128)(2,1)}, bf16[4,128,768]{2,1,0:T(8,128)(2,1)}, bf16[192,2304]{1,0:T(8,128)(2,1)}, bf16[192,768]{1,0:T(8,128)(2,1)}, ...) custom-call(bf16[512,768]{1,0:T(8,128)(2,1)} %get-tuple-element.50.o, ...), custom_call_target="tpu_custom_call" | custom-call | tf_op jit(solution)/shard_map/backward/pallas_call | solution.py:1519
  188.4 0.7 bitcast_convert_fusion
  189.1 0.6 fusion
  189.7 0.7 reshape.56
  190.4 5.2 %widen.1 = (f32[768,768]{1,0:T(8,128)}, f32[192,3072]{1,0:T(8,128)}, f32[192,2304]{1,0:T(8,128)}, f32[192,768]{1,0:T(8,128)}, f32[512,768]{1,0:T(8,128)}, /*index=5*/bf16[512,768]{1,0:T(8,128)(2,1)}) custom-call(bf16[768,768]{1,0:T(8,128)(2,1)} %get-tuple-element.72.refs_0_, bf16[192,3072]{1,0:T(8,128)(2,1)} %get-tuple-element.73.refs_1_, ...), custom_call_target="tpu_custom_call" | custom-call | tf_op jit(solution)/shard_map/widen/pallas_call | solution.py:699
  (1 shorter events, 0.0 us)

commit v4 on v3

--- a/solution.py
+++ b/solution.py
@@ -64,7 +64,11 @@
         return carry
 
     lax.fori_loop(1, C, greet, 0)
-    pl.semaphore_wait(barrier, S - 1 + C - 1)
+
+    def wait():
+        pl.semaphore_wait(barrier, S - 1 + C - 1)
+
+    return wait
 
 
 def bit_orders(S):
@@ -176,6 +180,70 @@
                     copy.wait_send()
 
 
+class PairGather(Gather):
+    def __init__(self, S, shard, full, send, recv, swap_send, swap_recv, local, pair_sems):
+        super().__init__(S, shard, full, send, recv, swap_send, swap_recv, local)
+        self.pair_send, self.pair_recv, self.late_send, self.late_recv = pair_sems
+        core, odd, width = lax.rem(self.c, 2), lax.rem(lax.div(self.c, 2), 2), self.N // 4
+        self.cols = span((2 * core + odd) * width, width)
+        self.late_cols = span((2 * core + 1 - odd) * width, width)
+        self.quarters = [2 * core + odd, 2 * (1 - core) + odd, 2 * core + 1 - odd, 2 * (1 - core) + 1 - odd]
+
+    def late_block(self, owner, p):
+        return self.full.at[span(owner * self.R + p * self.half, self.half, 16), self.late_cols]
+
+    def arrived(self, t, direct):
+        for p in range(2):
+            order = self.orders[p]
+            for i, mask in enumerate(subsets(order[:t])):
+                if (mask == 0) == direct:
+                    yield p, (1 << t) - 1 + i, jnp.bitwise_xor(self.s, order[t] ^ mask)
+
+    def pair_copies(self, t, direct):
+        return [
+            remote(
+                self.block(owner, p), self.block(owner, p), self.pair_send.at[p, k], self.pair_recv.at[p, k],
+                ctx=jnp.bitwise_xor(self.c, 2),
+            )
+            for p, k, owner in self.arrived(t, direct)
+        ]
+
+    def late_swaps(self, t, direct):
+        return [
+            remote(
+                self.late_block(owner, p), self.late_block(owner, p), self.late_send.at[p, k], self.late_recv.at[p, k],
+                ctx=jnp.bitwise_xor(self.c, 1),
+            )
+            for p, k, owner in self.arrived(t, direct)
+        ]
+
+    def arrive(self, t, direct):
+        super().arrive(t, direct)
+        for copy in self.pair_copies(t, direct):
+            copy.start()
+
+    def every(self):
+        return [(t, direct) for t in range(self.steps) for direct in (True, False)]
+
+    def late(self):
+        for which in self.every():
+            for copy in self.pair_copies(*which):
+                copy.wait_recv()
+            for copy in self.late_swaps(*which):
+                copy.start()
+
+    def late_ready(self):
+        for which in self.every():
+            for copy in self.late_swaps(*which):
+                copy.wait_recv()
+
+    def drain(self):
+        super().drain()
+        for which in self.every():
+            for copy in self.pair_copies(*which) + self.late_swaps(*which):
+                copy.wait_send()
+
+
 class Regroup:
     def __init__(self, src, dst, send, recv, local, C, G):
         self.src, self.dst, self.send, self.recv, self.local = src, dst, send, recv, local
@@ -314,8 +382,8 @@
     xs_o, wq_o, wo_o, wi_o, wu_o, k_o, v_o, q_o, seg_o, p_o, fac_o, ctxt_o, ctx_o,
     n1_o, f1_o, flow_o, act_o, dgel_o, gsec_o, gb_o, out_o, smg_o, sm_o,
     xs, ct, wq, wo, wi, wu, small_all, segc, segk, q, qt, kown, vown, kc, vc, bias, pst, m_s, l_s, ctxt, ctx,
-    first, n1, f1, flow, h, act, dgel, n2, gsec, gb, outv,
-    ag_send, ag_recv, sw_send, sw_recv, ag_local, rg_send, rg_recv, rg_local, sm_send, sm_recv,
+    first, n1, f1, flow, h, h2, act, dgel, n2, gsec, gb, outv,
+    ag_send, ag_recv, sw_send, sw_recv, pair_sem, ag_local, rg_send, rg_recv, rg_local, sm_send, sm_recv,
     kv_send, kv_recv, kv_local, kc_sem, p_sem, out_sem,
 ):
     S, C, G, PP = dims
@@ -326,9 +394,15 @@
     s, c = lax.axis_index("seq"), lax.axis_index("ctx")
     m = lax.rem(c, M)
 
+    def gather(kind, w, shard, full, *more):
+        sems = [a.at[w] for a in (ag_send, ag_recv, sw_send, sw_recv, ag_local)]
+        return kind(S, shard, full, *sems, *more)
+
     gathers = [
-        Gather(S, shard, full, *[a.at[w] for a in (ag_send, ag_recv, sw_send, sw_recv, ag_local)])
-        for w, (shard, full) in enumerate(((wq_s, wq), (wo_s, wo), (wi_s, wi), (wu_s, wu)))
+        gather(Gather, 0, wq_s, wq),
+        gather(Gather, 1, wo_s, wo),
+        gather(PairGather, 2, wi_s, wi, [pair_sem.at[i] for i in range(4)]),
+        gather(Gather, 3, wu_s, wu),
     ]
     gq, go, gi, gu = gathers
     pending = []
@@ -338,7 +412,7 @@
         copy.start()
         pending.append(copy)
 
-    enter(S, C)
+    enter(S, C)()
     hid_move = Regroup(hid, xs, rg_send.at[0], rg_recv.at[0], rg_local.at[0], C, G)
     cot_move = Regroup(cot, ct, rg_send.at[1], rg_recv.at[1], rg_local.at[1], C, G)
     seg_move = Regroup(seg, segc, rg_send.at[2], rg_recv.at[2], rg_local.at[2], C, G)
@@ -401,7 +475,6 @@
     gq.middle()
     gq.last()
     hid_move.finish()
-    cot_move.start()
     put(xs, xs_o)
     gq.ready(True, True)
     put(wq, wq_o)
@@ -487,6 +560,12 @@
         def _():
             go.middle()
             go.last()
+            gi.middle()
+
+        @pl.when(hp == NP - 1)
+        def _():
+            gi.last()
+            cot_move.start()
 
     attend(kown, vown, 0, in_own)
 
@@ -504,7 +583,13 @@
         for copy in loads:
             copy.wait()
         mask_bias(segk, segc, bias, G, PP)
-        attend(kc, vc, d, lambda hp: None)
+
+        def in_far(hp):
+            @pl.when(jnp.logical_and(d == M - 1, hp == NP - 2))
+            def _():
+                gu.first()
+
+        attend(kc, vc, d, in_far)
         return carry
 
     lax.fori_loop(1, M, far_chunk, 0)
@@ -522,8 +607,6 @@
 
     put(ctxt, ctxt_o)
     put(ctx, ctx_o)
-    gi.middle()
-    gi.last()
     go.ready(True, True)
     put(wo, wo_o)
 
@@ -546,26 +629,40 @@
     put(n1, n1_o)
     put(f1, f1_o)
     put(flow, flow_o)
-    gu.first()
+    if M == 1:
+        gu.first()
     gi.ready(True, True)
+
+    def feed_quarter(now, before):
+        def step(k):
+            cols = tile(k, T)
+            if now is not None:
+                number, place = now
+                where = gi.quarters[number] * (FF // 4)
+                row = lax.div(where, D)
+                place[:, cols] = dotf(flow[...], wi[:, span(where + k * T, T)]) + sm_o[pl.ds(IB + row, 1), cols]
+            if before is not None:
+                number, place = before
+                where = gi.quarters[number] * (FF // 4) + k * T
+                for r in range(L // RB):
+                    rows = pl.ds(r * RB, RB)
+                    x = place[rows, cols]
+                    share = 0.5 * (1.0 + lax.erf(x * ROOT_HALF))
+                    act[rows, span(where, T)] = (x * share).astype(bf16)
+                    dgel[rows, span(where, T)] = (
+                        share + x * (PDF_SCALE * jnp.exp(-0.5 * x * x))
+                    ).astype(bf16)
+
+        loop(FF // 4 // T, step)
+
+    feed_quarter((0, h), None)
+    feed_quarter((1, h2), (0, h))
+    gi.late()
+    feed_quarter((2, h), (1, h2))
+    gi.late_ready()
     put(wi, wi_o)
-
-    def feed_in(i):
-        cols = tile(i, D)
-        h[...] = dotf(flow[...], wi[:, cols]) + sm_o[pl.ds(IB + i, 1), :]
-
-        def gelu(k):
-            rows, lanes = tile(lax.div(k, D // T), RB), lax.rem(k, D // T) * T
-            x = h[rows, span(lanes, T)]
-            share = 0.5 * (1.0 + lax.erf(x * ROOT_HALF))
-            act[rows, span(i * D + lanes, T)] = (x * share).astype(bf16)
-            dgel[rows, span(i * D + lanes, T)] = (
-                share + x * (PDF_SCALE * jnp.exp(-0.5 * x * x))
-            ).astype(bf16)
-
-        loop(L // RB * (D // T), gelu)
-
-    loop(FF // D, feed_in)
+    feed_quarter((3, h2), (2, h))
+    feed_quarter(None, (3, h2))
     put(act, act_o)
     put(dgel, dgel_o)
     RU = FF // S
@@ -643,12 +740,12 @@
         ((NP, L, 128), bf16), ((NP, 128, L), bf16), ((NP, L, 128), bf16), ((NP, L, 128), bf16),
         ((NP, L, 128), bf16), ((NP, L, 128), bf16), ((L, L), f32), ((2, 2, L, L), bf16), ((M, NP, 2, L), f32), ((NP, 2, L), f32),
         ((NP, 128, L), f32), ((L, D), bf16),
-        ((L, D), f32), ((L, D), f32), ((L, 1), f32), ((L, D), bf16), ((L, D), f32), ((L, FF), bf16),
+        ((L, D), f32), ((L, D), f32), ((L, 1), f32), ((L, D), bf16), ((L, D), f32), ((L, D), f32), ((L, FF), bf16),
         ((L, FF), bf16), ((L, D), f32), ((L, D), f32), ((L, D), bf16), ((L, D), bf16),
     ]
     dma = pltpu.SemaphoreType.DMA
     sems = [
-        dma((4, 2, S)), dma((4, 2, S)), dma((4, 2, S)), dma((4, 2, S)), dma((4,)), dma((3, G)), dma((3, G)), dma((3,)),
+        dma((4, 2, S)), dma((4, 2, S)), dma((4, 2, S)), dma((4, 2, S)), dma((4, 2, S)), dma((4,)), dma((3, G)), dma((3, G)), dma((3,)),
         dma((S,)), dma((S,)), dma((3, M)), dma((3, M)), dma((3,)), dma((3,)), dma((2,)), dma((24,)),
     ]
     return pl.pallas_call(
@@ -1018,30 +1115,31 @@
 
 
 SCHEDULE = {
-    "ffn0": (('u0', 1),),
-    "ffn1": (('u1', 1),),
-    "ffn2": (('u0', 2),),
-    "ffn3": (('u2', 1), ('u1', 2)),
-    "first": (('i0', 1),),
-    "norm": (('u0', 3),),
-    "context": (('u2', 2),),
-    "pair0": (('u0', 4), ('u1', 3), ('i0', 2), ('i1', 1), ('i2', 1)),
-    "pair1": (('u2', 3),),
-    "project0": (('i0', 3), ('i3', 1), ('i1', 2)),
-    "input0": (('u1', 4), ('u0', 5)),
-    "far2": (('i2', 2),),
-    "pair2": (('u2', 4),),
-    "far3": (('i3', 2),),
-    "pair3": (('i0', 4), ('i1', 3), ('u0', 6), ('u1', 5), ('o', 1)),
-    "project1": (('i2', 3), ('q0', 1)),
-    "input1": (('i3', 3), ('u2', 5)),
-    "far4": (('o', 2),),
-    "pair4": (('i1', 4), ('u1', 6), ('q0', 2), ('i0', 5), ('q1', 1)),
-    "far5": (('i2', 4),),
-    "pair5": (('o', 3), ('i3', 4), ('u2', 6), ('q0', 3)),
-    "project2": (('q1', 2), ('i1', 5)),
-    "input2": (('i0', 6), ('q2', 1)),
-    "end": (('i2', 5), ('s', 1), ('g0', 1), ('o', 4), ('q1', 3), ('i3', 5), ('q2', 2), ('i1', 6), ('q0', 4), ('s', 2), ('i2', 6), ('q2', 3), ('o', 5), ('q1', 4), ('i3', 6), ('q0', 5), ('s', 3), ('q2', 4), ('o', 6), ('q1', 5), ('g1', 1), ('q0', 6), ('q2', 5), ('g2', 1), ('q1', 6), ('g3', 1), ('q2', 6)),
+    "outer": (('u0', 1),),
+    "ffn0": (('u1', 1),),
+    "ffn1": (('u0', 2), ('u2', 1)),
+    "ffn2": (('u1', 2),),
+    "ffn3": (('i0', 1),),
+    "first": (('u0', 3), ('u2', 2)),
+    "context": (('u1', 3), ('i1', 1)),
+    "far0": (('u0', 4), ('i0', 2)),
+    "pair0": (('i2', 1),),
+    "far1": (('u2', 3), ('i1', 2), ('i3', 1)),
+    "pair1": (('u1', 4),),
+    "project0": (('u0', 5), ('i0', 3)),
+    "input0": (('i2', 2),),
+    "far2": (('o', 1),),
+    "pair2": (('u2', 4), ('i1', 3)),
+    "far3": (('u0', 6), ('u1', 5), ('i0', 4), ('i3', 2)),
+    "pair3": (('i2', 3),),
+    "project1": (('o', 2),),
+    "input1": (('u2', 5), ('i1', 4), ('q0', 1)),
+    "far4": (('i3', 3), ('u1', 6), ('q1', 1)),
+    "pair4": (('i0', 5), ('i2', 4), ('o', 3)),
+    "far5": (('q0', 2),),
+    "pair5": (('u2', 6), ('i1', 5), ('i3', 4), ('q1', 2)),
+    "input2": (('i0', 6), ('i2', 5), ('o', 4), ('q0', 3), ('q2', 1), ('q3', 1), ('q4', 1)),
+    "end": (('q1', 3), ('s', 1), ('i1', 6), ('i3', 5), ('g0', 1), ('q2', 2), ('q3', 2), ('q4', 2), ('i2', 6), ('o', 5), ('q0', 4), ('s', 2), ('q2', 3), ('q3', 3), ('q4', 3), ('i3', 6), ('q1', 4), ('q0', 5), ('q2', 4), ('q3', 4), ('o', 6), ('s', 3), ('q4', 4), ('q1', 5), ('g1', 1), ('q2', 5), ('q3', 5), ('q0', 6), ('q4', 5), ('g2', 1), ('q1', 6), ('g3', 1), ('q2', 6), ('q3', 6), ('q4', 6)),
 }
 
 
@@ -1050,7 +1148,7 @@
     outv, gsec_i, gb_i, act_i, dgel_i, wu_i, wi_i, wo_i, wq_i, flow_i, n1_i, f1_i, xs_i, ctx_i, ctxt_i,
     q_i, k_i, v_i, p_i, fac, smg_i, sm,
     out_o, gin_o, gq_o, go_o, gi_o, gu_o, land_o, small_o,
-    pu, pi, po, pq, ps, fu, fi, fo, fq, fs, rxu, rxi, rxs, zlu, zli, zru, zri, zxs, dns,
+    pu, pi, po, pq, ps, fu, fi, fo, fq, fs, rxu, rxi, rxq, rxs, zlu, zli, zlq, zru, zri, zrq, zxs, dns,
     gsec, gb, grad_o, grad_ot, delta, smg,
     cs_send, cs_recv, h_send, h_recv, dx_send, dx_recv, dz_send, dz_recv, c_send, c_recv, x_send, x_recv, z_send, z_recv, rg_send, rg_recv, rg_local, in_sem, wq_sem, kv_sem, p_sem, dkv_send, dkv_recv,
     land_sem, l_send,
@@ -1077,7 +1175,7 @@
     for i in range(3):
         piece(
             f"u{i}", [(pl.ds(0, H), lambda e, i=i: gu_o.at[pl.ds(i * cut, cut), span(e * H, H)])],
-            pu, RU, i * cut, cut, pl.ds(0, H), rxu.at[i], zlu.at[i], zru.at[i],
+            pu.at[i], cut, 0, cut, pl.ds(0, H), rxu.at[i], zlu.at[i], zru.at[i],
         )
 
     def narrow_piece(name, places, part, cols):
@@ -1092,14 +1190,18 @@
                 pi.at[i], pl.ds(j * H, H),
             )
     narrow_piece("o", [(pl.ds(0, H), lambda e: go_o.at[:, span(e * H, H)])], po, pl.ds(0, H))
-    for i in range(3):
+
+    def qkv_place(i, a):
+        return lambda e: gq_o.at[:, span(a * D + (2 * i + e) * 128, 128)]
+
+    for i in range(2):
         narrow_piece(
-            f"q{i}",
-            [
-                (pl.ds(a * 128, 128), lambda e, i=i, a=a: gq_o.at[:, span(a * D + (2 * i + e) * 128, 128)])
-                for a in range(3)
-            ],
-            pq.at[i], pl.ds(0, H),
+            f"q{i}", [(pl.ds(a * 128, 128), qkv_place(i, a)) for a in range(3)], pq.at[i], pl.ds(0, H)
+        )
+    for a in range(3):
+        piece(
+            f"q{2 + a}", [(pl.ds(0, 128), qkv_place(2, a))],
+            pq.at[2], R, 0, R, pl.ds(a * 128, 128), rxq.at[a], zlq.at[a], zrq.at[a],
         )
     def direct_piece(name, n, places, *refs):
         m_ = len(items)
@@ -1108,7 +1210,7 @@
 
     SW = ps.shape[3]
     direct_piece("s", 0, [(pl.ds(0, SW), lambda e: small_o.at[e])], ps, fs, rxs, zxs, dns)
-    swap_u = CoreSwap(pu, fu, 512, cs_send.at[0], cs_recv.at[0])
+    swap_u = [CoreSwap(pu.at[i], fu.at[i], cut, cs_send.at[7 + i], cs_recv.at[7 + i]) for i in range(3)]
     swap_i = [CoreSwap(pi.at[i], fi.at[i], T, cs_send.at[1 + i], cs_recv.at[1 + i]) for i in range(2)]
     swap_o = CoreSwap(po, fo, T, cs_send.at[3], cs_recv.at[3])
     swap_q = [CoreSwap(pq.at[i], fq.at[i], T, cs_send.at[4 + i], cs_recv.at[4 + i]) for i in range(3)]
@@ -1121,9 +1223,8 @@
             ran.add(step)
             ticks[step[0]][step[1] - 1]()
 
-    enter(S, C)
+    met = enter(S, C)
     out_move = Ungroup(outv, out_o, rg_send.at[0], rg_recv.at[0], rg_local.at[0], C, G)
-    out_move.start()
     smg[...] = smg_i[...]
 
     def feed_forward(act, dgel, wu, wi, h, n1, f1, flow):
@@ -1139,14 +1240,19 @@
         loads[0].wait()
         loads[1].wait()
 
-        def outer_grad(i):
-            rows = tile(i, 512)
-            block = dotg(act[:, rows], gb[...], 0, 0).astype(bf16)
-            for e in range(2):
-                pu[e, rows, :] = block[:, e * (D // 2) : (e + 1) * (D // 2)]
-            swap_u.start(i)
-
-        loop(FF // 512, outer_grad)
+        met()
+        out_move.start()
+        for i in range(3):
+
+            def outer_grad(owner, i=i):
+                block = dotg(act[:, span(owner * RU + i * cut, cut)], gb[...], 0, 0).astype(bf16)
+                for e in range(2):
+                    pu[i, e, tile(owner, cut), :] = block[:, e * H : (e + 1) * H]
+                swap_u[i].start(owner)
+
+            loop(S, outer_grad)
+        swap_u[0].add()
+        point("outer")
         for copy in loads[2:5]:
             copy.wait()
 
@@ -1173,7 +1279,8 @@
             loop(D // T, grad)
 
         inner_grad(0, 1 - core, True)
-        swap_u.add()
+        swap_u[1].add()
+        swap_u[2].add()
         point("ffn0")
         inner_grad(0, core, False)
         point("ffn1")
@@ -1299,7 +1406,7 @@
                 ctx=group + lax.rem(m + d, M),
             )
 
-        def chunk(hp, slot, d):
+        def chunk(hp, slot, d, put):
             j = lax.rem(m + d, M)
             t = hp * M + lax.rem(d - 1 + M, M)
             p_load(t).wait()
@@ -1308,26 +1415,36 @@
             def _():
                 p_load(t + 1).start()
 
-            key, value = kb[slot, j], vb[slot, j]
-            turned = key.T
-            query, up, up_t = q[hp], grad_o[hp], grad_ot[hp]
-            sums = []
-            for e in range(2):
-                rows = (row_of < HEAD_DIM) if e == 0 else (row_of >= HEAD_DIM)
-                lanes = (lane_of < HEAD_DIM) if e == 0 else (lane_of >= HEAD_DIM)
-                zero, zero_t = jnp.zeros_like(query), jnp.zeros_like(up_t)
-                probs = pb[lax.rem(t, 2), e].astype(f32) * fac[d, hp, e : e + 1, :]
-                dprobs = dotf(value, jnp.where(rows, up_t, zero_t))
-                dscores = (probs * (dprobs - delta[hp, e : e + 1, :])).astype(bf16)
-                sums.append(
-                    (
-                        dotf(dscores, jnp.where(lanes, query, zero)),
-                        dotf(probs.astype(bf16), jnp.where(lanes, up, zero)),
+            def block(ks, qs, kn, qn):
+                key, value = kb[slot, j, ks, :], vb[slot, j, ks, :]
+                turned = key.T
+                query, up, up_t = q[hp, qs, :], grad_o[hp, qs, :], grad_ot[hp, :, qs]
+                row_of = lax.broadcasted_iota(jnp.int32, (128, qn), 0)
+                lane_of = lax.broadcasted_iota(jnp.int32, (qn, 128), 1)
+                sums = []
+                for e in range(2):
+                    rows = (row_of < HEAD_DIM) if e == 0 else (row_of >= HEAD_DIM)
+                    lanes = (lane_of < HEAD_DIM) if e == 0 else (lane_of >= HEAD_DIM)
+                    zero, zero_t = jnp.zeros_like(query), jnp.zeros_like(up_t)
+                    probs = pb[lax.rem(t, 2), e, ks, qs].astype(f32) * fac[d, hp, e : e + 1, qs]
+                    dprobs = dotf(value, jnp.where(rows, up_t, zero_t))
+                    dscores = (probs * (dprobs - delta[hp, e : e + 1, qs])).astype(bf16)
+                    sums.append(
+                        (
+                            dotf(dscores, jnp.where(lanes, query, zero)),
+                            dotf(probs.astype(bf16), jnp.where(lanes, up, zero)),
+                        )
                     )
-                )
-                head = slice(e * HEAD_DIM, (e + 1) * HEAD_DIM)
-                dqt[head, :] += dotf(turned[head], dscores)
-            return sums[0][0] + sums[1][0], sums[0][1] + sums[1][1]
+                    head = slice(e * HEAD_DIM, (e + 1) * HEAD_DIM)
+                    dqt[head, qs] += dotf(turned[head], dscores)
+                put(ks, sums[0][0] + sums[1][0], sums[0][1] + sums[1][1])
+
+            if M == 2 and not isinstance(d, int):
+                near, far = span(m * (L // 2), L // 2), span((1 - m) * (L // 2), L // 2)
+                block(near, pl.ds(0, L), L // 2, L)
+                block(far, far, L // 2, L // 2)
+            else:
+                block(pl.ds(0, L), pl.ds(0, L), L, L)
 
         def pair(hp, between):
             slot = lax.rem(hp, 2)
@@ -1346,17 +1463,22 @@
                 def _():
                     send_back(hp - 2, d).wait_send()
 
-                dk, dv = chunk(hp, slot, d)
-                stage[slot, d - 1, 0] = dk.astype(bf16)
-                stage[slot, d - 1, 1] = dv.astype(bf16)
+                def put(ks, dk, dv):
+                    stage[slot, d - 1, 0, ks, :] = dk.astype(bf16)
+                    stage[slot, d - 1, 1, ks, :] = dv.astype(bf16)
+
+                chunk(hp, slot, d, put)
                 send_back(hp, d).start()
                 return carry
 
             lax.fori_loop(1, M, far, 0)
             between()
-            dk, dv = chunk(hp, slot, 0)
-            own_k[slot] = dk
-            own_v[slot] = dv
+
+            def put_own(ks, dk, dv):
+                own_k[slot, ks, :] = dk
+                own_v[slot, ks, :] = dv
+
+            chunk(hp, slot, 0, put_own)
             turned_q[slot] = (dqt[...] * HEAD_DIM**-0.5).T.astype(bf16)
 
         def fetched(first, count):
@@ -1481,7 +1603,7 @@
     for item in items.values():
         item.finish()
         item.drain()
-    for swap in [swap_u] + swap_i + [swap_o] + swap_q:
+    for swap in swap_u + swap_i + [swap_o] + swap_q:
         swap.drain()
 
 
@@ -1499,10 +1621,10 @@
     ]
     cut = RU // 3
     scratch = [
-        (2, FF, H), (2, 2, D, D), (2, D, H), (3, 2, D, H), (S, 2, SR // 2, SW),
-        (FF, H), (2, D, D), (D, H), (3, D, H), (S, SR // 2, SW),
-        (3, 2, S - 1, cut // 2, H), (8, 2, S - 1, R // 2, H), (S - 1, SR // 2, SW),
-        (3, cut, H), (8, R, H), (3, cut, H), (8, R, H),
+        (3, 2, S * cut, H), (2, 2, D, D), (2, D, H), (3, 2, D, H), (S, 2, SR // 2, SW),
+        (3, S * cut, H), (2, D, D), (D, H), (3, D, H), (S, SR // 2, SW),
+        (3, 2, S - 1, cut // 2, H), (7, 2, S - 1, R // 2, H), (3, 2, S - 1, R // 2, 128), (S - 1, SR // 2, SW),
+        (3, cut, H), (7, R, H), (3, R, 128), (3, cut, H), (7, R, H), (3, R, 128),
         (C // 2, SR // 2, SW), (SR // 2, SW),
     ]
     scratch = [(x, bf16) for x in scratch] + [
@@ -1510,11 +1632,11 @@
     ]
     dma = pltpu.SemaphoreType.DMA
     sems = [
-        dma((8, 8)), dma((8, 8)), dma((1, 1)), dma((1, 1)), dma((1, S - 1)), dma((1, S - 1)), dma((1, C // 2)), dma((1, C // 2)),
-        dma((13, 3)), dma((13, 3)), dma((12, 2, S - 1)), dma((12, 2, S - 1)), dma((12, 2)),
-        dma((12, 2)),
+        dma((10, 8)), dma((10, 8)), dma((1, 1)), dma((1, 1)), dma((1, S - 1)), dma((1, S - 1)), dma((1, C // 2)), dma((1, C // 2)),
+        dma((16, 3)), dma((16, 3)), dma((16, 2, S - 1)), dma((16, 2, S - 1)), dma((16, 2)),
+        dma((16, 2)),
         dma((2, G)), dma((2, G)), dma((2,)), dma((10,)), dma((NP, 3)), dma((2, 2)), dma((2,)), dma((2, land)), dma((NP, land)), dma((1,)),
-        dma((13, 3)),
+        dma((16, 3)),
     ]
     results = pl.pallas_call(
         functools.partial(backward_kernel, (S, C, G, PP)),

time: 196 us -> 192 us (0.980)
  Pallas kernels: 193 us -> 189 us
    pallas_call x1, Pallas kernels: 107 us -> 104 us  [backward_call(): pl.pallas_call(functools.partial(backward_kernel, (S, C, G, PP)), out_sha...]
where the time goes in v4:
time: 192 us; the launch traced here: 191 us
  Pallas kernels  189 us (98%)
    pallas_call x1, Pallas kernels, backward_call(): pl.pallas_call(functools.partial(backward_kernel, (S, C, G, PP)), out_sha...  104 us
    pallas_call x1, Pallas kernels, forward_call(): pl.pallas_call(functools.partial(forward_kernel, (S, C, G, PP)), out_shap...  79.1 us
    pallas_call x1, Pallas kernels, widen(): pl.pallas_call(functools.partial(widen_kernel, count), out_shape=[sds(a.s...  5.19 us

profile of v4, /device:TPU:0, one launch (start us, length us, event | category | flops | bytes accessed | tf_op | source)
XLA Modules:
  0.0 191.4 jit_solution(14713768931682414167)
XLA Ops:
  0.7 79.1 %forward.1 = (bf16[512,768]{1,0:T(8,128)(2,1)}, bf16[768,2304]{1,0:T(8,128)(2,1)}, bf16[768,768]{1,0:T(8,128)(2,1)}, bf16[768,3072]{1,0:T(8,128)(2,1)}, bf16[307...) custom-call(bf16[4,128,768]{2,1,0:T(8,128)(2,1)} %hid.1, ...), custom_call_target="tpu_custom_call" | custom-call | tf_op jit(solution)/shard_map/forward/pallas_call | solution.py:751
  79.7 104.3 %backward.1 = (bf16[4,128,768]{2,1,0:T(8,128)(2,1)}, bf16[4,128,768]{2,1,0:T(8,128)(2,1)}, bf16[192,2304]{1,0:T(8,128)(2,1)}, bf16[192,768]{1,0:T(8,128)(2,1)}, ...) custom-call(bf16[512,768]{1,0:T(8,128)(2,1)} %get-tuple-element.50.o, ...), custom_call_target="tpu_custom_call" | custom-call | tf_op jit(solution)/shard_map/backward/pallas_call | solution.py:1641
  184.0 0.7 bitcast_convert_fusion
  184.8 0.6 fusion
  185.4 0.7 reshape.56
  186.0 5.2 %widen.1 = (f32[768,768]{1,0:T(8,128)}, f32[192,3072]{1,0:T(8,128)}, f32[192,2304]{1,0:T(8,128)}, f32[192,768]{1,0:T(8,128)}, f32[512,768]{1,0:T(8,128)}, /*index=5*/bf16[512,768]{1,0:T(8,128)(2,1)}) custom-call(bf16[768,768]{1,0:T(8,128)(2,1)} %get-tuple-element.72.refs_0_, bf16[192,3072]{1,0:T(8,128)(2,1)} %get-tuple-element.73.refs_1_, ...), custom_call_target="tpu_custom_call" | custom-call | tf_op jit(solution)/shard_map/widen/pallas_call | solution.py:796
  (1 shorter events, 0.0 us)

commit v5 on v4

--- a/solution.py
+++ b/solution.py
@@ -515,6 +515,31 @@
         slot = lax.rem(hp, 2)
         return pltpu.make_async_copy(pst.at[slot], p_o.at[hp, d], p_sem.at[slot])
 
+    def reachable(keys, values, hp, d, slot):
+        near, far = span(m * (L // 2), L // 2), span((1 - m) * (L // 2), L // 2)
+        qv, qf = qt[hp], qt[hp, :, far]
+        vn, vf = values[hp, near, :].T, values[hp, far, :].T
+        low_rows = lax.broadcasted_iota(jnp.int32, (128, L // 2), 0) < HEAD_DIM
+        for e in range(2):
+            head, one = slice(e * HEAD_DIM, (e + 1) * HEAD_DIM), slice(e, e + 1)
+            mine = (row_of < HEAD_DIM) if e == 0 else (row_of >= HEAD_DIM)
+            mine_far = low_rows if e == 0 else jnp.logical_not(low_rows)
+            s_near = dotf(keys[hp, near, :], jnp.where(mine, qv, jnp.zeros_like(qv))) + bias[near, :]
+            s_far = dotf(keys[hp, far, :], jnp.where(mine_far, qf, jnp.zeros_like(qf))) + bias[far, far]
+            old = m_s[d - 1, hp, one, :]
+            m_s[d, hp, one, :] = jnp.maximum(old, jnp.max(s_near, axis=0, keepdims=True))
+            m_s[d, hp, one, far] = jnp.maximum(m_s[d, hp, one, far], jnp.max(s_far, axis=0, keepdims=True))
+            top = m_s[d, hp, one, :]
+            keep = jnp.exp(old - top)
+            w_near, w_far = jnp.exp(s_near - top), jnp.exp(s_far - m_s[d, hp, one, far])
+            low_near, low_far = w_near.astype(bf16), w_far.astype(bf16)
+            l_s[hp, one, :] = l_s[hp, one, :] * keep + colsum(w_near)
+            l_s[hp, one, far] += colsum(w_far)
+            ctxt[hp, head, :] = ctxt[hp, head, :] * keep + dotf(vn[head], low_near)
+            ctxt[hp, head, far] += dotf(vf[head], low_far)
+            pst[slot, e, near, :] = low_near
+            pst[slot, e, far, far] = low_far
+
     def attend(keys, values, d, extra):
         fresh = isinstance(d, int)
 
@@ -529,6 +554,10 @@
 
             else:
                 keep_probs(hp, d).wait()
+            if M == 2 and not fresh:
+                reachable(keys, values, hp, d, slot)
+                keep_probs(hp, d).start()
+                return
             qv, kv, vt, b = qt[hp], keys[hp], values[hp].T, bias[...]
             for e in range(2):
                 head = slice(e * HEAD_DIM, (e + 1) * HEAD_DIM)

time: 192 us -> 192 us (level)
  no operation moved by 1% of the time
where the time goes in v5:
time: 192 us; the launch traced here: 191 us
  Pallas kernels  189 us (98%)
    pallas_call x1, Pallas kernels, backward_call(): pl.pallas_call(functools.partial(backward_kernel, (S, C, G, PP)), out_sha...  104 us
    pallas_call x1, Pallas kernels, forward_call(): pl.pallas_call(functools.partial(forward_kernel, (S, C, G, PP)), out_shap...  79 us
    pallas_call x1, Pallas kernels, widen(): pl.pallas_call(functools.partial(widen_kernel, count), out_shape=[sds(a.s...  5.19 us

profile of v5, /device:TPU:0, one launch (start us, length us, event | category | flops | bytes accessed | tf_op | source)
XLA Modules:
  0.0 191.4 jit_solution(17870476485934934045)
XLA Ops:
  0.7 79.0 %forward.1 = (bf16[512,768]{1,0:T(8,128)(2,1)}, bf16[768,2304]{1,0:T(8,128)(2,1)}, bf16[768,768]{1,0:T(8,128)(2,1)}, bf16[768,3072]{1,0:T(8,128)(2,1)}, bf16[307...) custom-call(bf16[4,128,768]{2,1,0:T(8,128)(2,1)} %hid.1, ...), custom_call_target="tpu_custom_call" | custom-call | tf_op jit(solution)/shard_map/forward/pallas_call | solution.py:780
  79.7 104.3 %backward.1 = (bf16[4,128,768]{2,1,0:T(8,128)(2,1)}, bf16[4,128,768]{2,1,0:T(8,128)(2,1)}, bf16[192,2304]{1,0:T(8,128)(2,1)}, bf16[192,768]{1,0:T(8,128)(2,1)}, ...) custom-call(bf16[512,768]{1,0:T(8,128)(2,1)} %get-tuple-element.50.o, ...), custom_call_target="tpu_custom_call" | custom-call | tf_op jit(solution)/shard_map/backward/pallas_call | solution.py:1670
  184.0 0.7 bitcast_convert_fusion
  184.7 0.6 fusion
  185.3 0.7 reshape.56
  186.0 5.2 %widen.1 = (f32[768,768]{1,0:T(8,128)}, f32[192,3072]{1,0:T(8,128)}, f32[192,2304]{1,0:T(8,128)}, f32[192,768]{1,0:T(8,128)}, f32[512,768]{1,0:T(8,128)}, /*index=5*/bf16[512,768]{1,0:T(8,128)(2,1)}) custom-call(bf16[768,768]{1,0:T(8,128)(2,1)} %get-tuple-element.72.refs_0_, bf16[192,3072]{1,0:T(8,128)(2,1)} %get-tuple-element.73.refs_1_, ...), custom_call_target="tpu_custom_call" | custom-call | tf_op jit(solution)/shard_map/widen/pallas_call | solution.py:825
  (1 shorter events, 0.0 us)
